TPU v7x, 32 devices: a whole 2x2x4 slice. The times are simulated.
32 devices in a mesh: section: 2 (over y), replica: 4 (over x, core), shard: 4 (over z).
Axes of the slice: x: 2, y: 2, z: 4, core: 2. Of those that a mesh axis runs over, the one named last changes fastest.
Arguments:
- tokens: bfloat16 [2, 4, 1024, 1536], P(None, 'replica', 'shard'), may hold values from -6 to 6
- segments: int32 [2, 4, 1024], P(None, 'replica'), may hold values from 0 to 7, never falling along the last dimension, each value on 1 to 512 neighbouring positions
- norm_attn: bfloat16 [2, 1536], P('section', 'shard'), may hold values from 0.25 to 1.75
- w_query: bfloat16 [2, 1536, 1536], P('section', 'shard'), may hold values from -0.15625 to 0.15625
- w_key: bfloat16 [2, 1536, 768], P('section', 'shard'), may hold values from -0.15625 to 0.15625
- w_value: bfloat16 [2, 1536, 768], P('section', 'shard'), may hold values from -0.15625 to 0.15625
- w_out: bfloat16 [2, 1536, 1536], P('section', 'shard'), may hold values from -0.3125 to 0.3125
- norm_ffn: bfloat16 [2, 1536], P('section', 'shard'), may hold values from 0.25 to 1.75
- w_gate: bfloat16 [2, 1536, 4096], P('section', 'shard'), may hold values from -0.15625 to 0.15625
- w_up: bfloat16 [2, 1536, 4096], P('section', 'shard'), may hold values from -0.15625 to 0.15625
- w_down: bfloat16 [2, 4096, 1536], P('section', 'shard'), may hold values from -0.09375 to 0.09375
- cotangent: bfloat16 [2, 4, 1024, 1536], P(None, 'replica', 'shard'), may hold values from -6 to 6
Outputs:
- section_outputs: bfloat16 [2, 2, 4, 1024, 1536], P('section', None, 'replica', 'shard')
- input_grads: float32 [2, 2, 4, 1024, 1536], P('section', None, 'replica', 'shard')
- grad_norm_attn: float32 [2, 1536], P('section', 'shard')
- grad_query: float32 [2, 1536, 1536], P('section', 'shard')
- grad_key: float32 [2, 1536, 768], P('section', 'shard')
- grad_value: float32 [2, 1536, 768], P('section', 'shard')
- grad_out: float32 [2, 1536, 1536], P('section', 'shard')
- grad_norm_ffn: float32 [2, 1536], P('section', 'shard')
- grad_gate: float32 [2, 1536, 4096], P('section', 'shard')
- grad_up: float32 [2, 1536, 4096], P('section', 'shard')
- grad_down: float32 [2, 4096, 1536], P('section', 'shard')
Inputs may be any that keep to these rules, and one draw needn't show every extreme that they name: `segments`: along each sequence the numbers never fall; a document holds at most half of 1024 tokens, and one document of each sequence holds exactly that many.
All inputs are finite; a program needn't handle non-finite values.
Results may differ from a plain program's by a relative error of at most 0.023.
Values may be sent and summed in bfloat16 or wider, within the bound.
A program may use at most 448 MiB of HBM per device.

v0:
```python
import jax
import jax.numpy as jnp
from jax import lax
from jax.sharding import PartitionSpec as P

QH = 16
KVH = 8
HD = 96


EPSILON = 1e-05
ROPE_BASE = 100000.0


def from_behind(x, axis, by):
    devices = lax.axis_size(axis)
    pairs = [(i, i + by) for i in range(devices) if 0 <= i + by < devices]
    return lax.ppermute(x, axis, pairs)


def rotate(values, cosine_table, sine_table, turn_sign):
    half_dim = values.shape[-1] // 2
    leading = values[..., :half_dim]
    trailing = values[..., half_dim:]
    return jnp.concatenate(
        [
            leading * cosine_table - turn_sign * trailing * sine_table,
            trailing * cosine_table + turn_sign * leading * sine_table,
        ],
        axis=-1,
    )


def gather_layer(pieces):
    attention = (
        lax.all_gather(pieces[0], "shard", axis=0, tiled=True),
        lax.all_gather(pieces[1], "shard", axis=0, tiled=True),
        lax.all_gather(pieces[2], "shard", axis=0, tiled=True),
        lax.all_gather(pieces[3], "shard", axis=0, tiled=True),
        lax.all_gather(pieces[4], "shard", axis=0, tiled=True),
    )
    feedforward = (
        lax.all_gather(pieces[5], "shard", axis=0, tiled=True),
        lax.all_gather(pieces[6], "shard", axis=0, tiled=True),
        lax.all_gather(pieces[7], "shard", axis=0, tiled=True),
        lax.all_gather(pieces[8], "shard", axis=0, tiled=True),
    )
    return tuple(attention) + tuple(feedforward)


def forward_layer(inputs, weights, segment, row_start):
    norm_attn, w_query, w_key, w_value, w_out, norm_ffn, w_gate, w_up, w_down = weights
    row_count = inputs.shape[0]
    seq_length = segment.shape[0]
    groups = QH // KVH
    half_dim = HD // 2
    local_segment = lax.dynamic_slice_in_dim(segment, row_start, row_count)
    query_index = row_start + jnp.arange(row_count, dtype=jnp.int32)
    starts = jnp.searchsorted(segment, local_segment, side="left")
    positions = query_index - starts
    frequency = ROPE_BASE ** (-(jnp.arange(half_dim, dtype=jnp.float32) * 2.0) / HD)
    angles = positions.astype(jnp.float32)[:, None, None] * frequency[None, None, :]
    cosine_table = jnp.cos(angles)
    sine_table = jnp.sin(angles)
    recip_one = lax.rsqrt(jnp.mean(inputs * inputs, axis=-1, keepdims=True) + EPSILON)
    scaled = inputs * recip_one
    normed = (scaled * norm_attn.astype(jnp.float32)).astype(jnp.bfloat16)
    raw_query = jnp.dot(normed, w_query, preferred_element_type=jnp.float32).reshape(
        row_count, KVH, groups, HD
    )
    queries = rotate(raw_query, cosine_table[:, :, None, :], sine_table[:, :, None, :], 1.0).astype(
        jnp.bfloat16
    )
    raw_key = jnp.dot(normed, w_key, preferred_element_type=jnp.float32).reshape(row_count, KVH, HD)
    key_rows = (
        rotate(raw_key, cosine_table, sine_table, 1.0)
        .astype(jnp.bfloat16)
        .reshape(row_count, KVH * HD)
    )
    value_rows = jnp.dot(normed, w_value, preferred_element_type=jnp.float32).astype(jnp.bfloat16)
    all_keys, all_values = (
        lax.all_gather(key_rows, "shard", axis=0, tiled=True),
        lax.all_gather(value_rows, "shard", axis=0, tiled=True),
    )
    all_keys = all_keys.reshape(seq_length, KVH, HD)
    all_values = all_values.reshape(seq_length, KVH, HD)
    key_index = jnp.arange(seq_length, dtype=jnp.int32)
    allowed = (key_index[None, :] <= query_index[:, None]) & (
        segment[None, :] == local_segment[:, None]
    )
    scores = jnp.einsum(
        "ihgd,jhd->hgij", queries, all_keys, preferred_element_type=jnp.float32
    ) * HD ** (-0.5)
    scores = jnp.where(allowed, scores, -1e30)
    row_top = jnp.max(scores, axis=-1, keepdims=True)
    exponent = jnp.exp(scores - row_top)
    row_total = jnp.sum(exponent, axis=-1, keepdims=True)
    probabilities = exponent / row_total
    log_total = row_top + jnp.log(row_total)
    attended = jnp.einsum(
        "hgij,jhd->ihgd",
        probabilities.astype(jnp.bfloat16),
        all_values,
        preferred_element_type=jnp.float32,
    )
    attended = attended.reshape(row_count, QH * HD).astype(jnp.bfloat16)
    middle = inputs + jnp.dot(attended, w_out, preferred_element_type=jnp.float32)
    recip_two = lax.rsqrt(jnp.mean(middle * middle, axis=-1, keepdims=True) + EPSILON)
    scaled_mid = middle * recip_two
    normed_mid = (scaled_mid * norm_ffn.astype(jnp.float32)).astype(jnp.bfloat16)
    gate_proj = jnp.dot(normed_mid, w_gate, preferred_element_type=jnp.float32)
    up_proj = jnp.dot(normed_mid, w_up, preferred_element_type=jnp.float32)
    hidden = (jax.nn.silu(gate_proj) * up_proj).astype(jnp.bfloat16)
    result = middle + jnp.dot(hidden, w_down, preferred_element_type=jnp.float32)
    saved = (
        scaled,
        recip_one,
        normed,
        queries,
        all_keys,
        all_values,
        allowed,
        log_total,
        attended,
        scaled_mid,
        recip_two,
        normed_mid,
        gate_proj,
        up_proj,
        hidden,
        cosine_table,
        sine_table,
    )
    return (result, saved)


def backward_layer(grad_result, weights, saved):
    norm_attn, w_query, w_key, w_value, w_out, norm_ffn, w_gate, w_up, w_down = weights
    (
        scaled,
        recip_one,
        normed,
        queries,
        all_keys,
        all_values,
        allowed,
        log_total,
        attended,
        scaled_mid,
        recip_two,
        normed_mid,
        gate_proj,
        up_proj,
        hidden,
        cosine_table,
        sine_table,
    ) = saved
    row_count = grad_result.shape[0]
    seq_length = all_keys.shape[0]
    groups = QH // KVH
    score_scale = HD ** (-0.5)
    branch_grad = grad_result.astype(jnp.bfloat16)
    grad_hidden = jnp.einsum("td,fd->tf", branch_grad, w_down, preferred_element_type=jnp.float32)
    sigmoid_gate = jax.nn.sigmoid(gate_proj)
    gate_low = (
        grad_hidden * up_proj * (sigmoid_gate * (1.0 + gate_proj * (1.0 - sigmoid_gate)))
    ).astype(jnp.bfloat16)
    up_low = (grad_hidden * jax.nn.silu(gate_proj)).astype(jnp.bfloat16)
    grad_normed_mid = jnp.einsum("tf,df->td", gate_low, w_gate, preferred_element_type=jnp.float32)
    grad_normed_mid = grad_normed_mid + jnp.einsum(
        "tf,df->td", up_low, w_up, preferred_element_type=jnp.float32
    )
    grad_norm_ffn = jnp.sum(grad_normed_mid * scaled_mid, axis=0)
    grad_scaled_mid = grad_normed_mid * norm_ffn.astype(jnp.float32)
    grad_middle = grad_result + recip_two * (
        grad_scaled_mid
        - scaled_mid * jnp.mean(grad_scaled_mid * scaled_mid, axis=-1, keepdims=True)
    )
    attn_grad = grad_middle.astype(jnp.bfloat16)
    grad_attended = jnp.einsum("td,qd->tq", attn_grad, w_out, preferred_element_type=jnp.float32)
    grad_attended = grad_attended.astype(jnp.bfloat16).reshape(row_count, KVH, groups, HD)
    scores = (
        jnp.einsum("ihgd,jhd->hgij", queries, all_keys, preferred_element_type=jnp.float32)
        * score_scale
    )
    scores = jnp.where(allowed, scores, -1e30)
    probabilities = jnp.exp(scores - log_total)
    grad_probs = jnp.einsum(
        "ihgd,jhd->hgij", grad_attended, all_values, preferred_element_type=jnp.float32
    )
    row_dot = jnp.sum(probabilities * grad_probs, axis=-1, keepdims=True)
    grad_scores = (probabilities * (grad_probs - row_dot)).astype(jnp.bfloat16)
    grad_queries = (
        jnp.einsum("hgij,jhd->ihgd", grad_scores, all_keys, preferred_element_type=jnp.float32)
        * score_scale
    )
    key_terms = (
        jnp.einsum("hgij,ihgd->jhd", grad_scores, queries, preferred_element_type=jnp.float32)
        * score_scale
    )
    value_terms = jnp.einsum(
        "hgij,ihgd->jhd",
        probabilities.astype(jnp.bfloat16),
        grad_attended,
        preferred_element_type=jnp.float32,
    )
    key_terms = key_terms.reshape(seq_length, KVH * HD)
    value_terms = value_terms.reshape(seq_length, KVH * HD)
    grad_keys, grad_values = (
        lax.psum_scatter(key_terms, "shard", scatter_dimension=0, tiled=True),
        lax.psum_scatter(value_terms, "shard", scatter_dimension=0, tiled=True),
    )
    query_low = rotate(grad_queries, cosine_table[:, :, None, :], sine_table[:, :, None, :], -1.0)
    query_low = query_low.reshape(row_count, QH * HD).astype(jnp.bfloat16)
    key_low = rotate(grad_keys.reshape(row_count, KVH, HD), cosine_table, sine_table, -1.0)
    key_low = key_low.reshape(row_count, KVH * HD).astype(jnp.bfloat16)
    value_low = grad_values.astype(jnp.bfloat16)
    grad_normed = jnp.einsum("tq,dq->td", query_low, w_query, preferred_element_type=jnp.float32)
    grad_normed = grad_normed + jnp.einsum(
        "tq,dq->td", key_low, w_key, preferred_element_type=jnp.float32
    )
    grad_normed = grad_normed + jnp.einsum(
        "tq,dq->td", value_low, w_value, preferred_element_type=jnp.float32
    )
    grad_norm_attn = jnp.sum(grad_normed * scaled, axis=0)
    grad_scaled = grad_normed * norm_attn.astype(jnp.float32)
    grad_inputs = grad_middle + recip_one * (
        grad_scaled - scaled * jnp.mean(grad_scaled * scaled, axis=-1, keepdims=True)
    )
    operands = (
        normed,
        query_low,
        key_low,
        value_low,
        attended,
        attn_grad,
        normed_mid,
        gate_low,
        up_low,
        hidden,
        branch_grad,
    )
    return (grad_inputs, (grad_norm_attn, grad_norm_ffn), operands)


def row_product(left, right):
    return jnp.einsum("td,tq->dq", left, right, preferred_element_type=jnp.float32)


def weight_terms(gains, operands):
    (
        normed,
        query_low,
        key_low,
        value_low,
        attended,
        attn_grad,
        normed_mid,
        gate_low,
        up_low,
        hidden,
        branch_grad,
    ) = operands
    return (
        gains[0],
        row_product(normed, query_low),
        row_product(normed, key_low),
        row_product(normed, value_low),
        row_product(attended, attn_grad),
        gains[1],
        row_product(normed_mid, gate_low),
        row_product(normed_mid, up_low),
        row_product(hidden, branch_grad),
    )


def add_terms(earlier, later):
    if earlier is None:
        return later
    return tuple((left_term + right_term for left_term, right_term in zip(earlier, later)))


def body(
    tokens,
    segments,
    norm_attn,
    w_query,
    w_key,
    w_value,
    w_out,
    norm_ffn,
    w_gate,
    w_up,
    w_down,
    cotangent,
):
    micro_count = tokens.shape[0]
    row_count = tokens.shape[2]
    width = tokens.shape[3]
    first_section = lax.axis_index("section") == 0
    row_start = lax.axis_index("shard") * row_count
    pieces = (
        norm_attn[0],
        w_query[0],
        w_key[0],
        w_value[0],
        w_out[0],
        norm_ffn[0],
        w_gate[0],
        w_up[0],
        w_down[0],
    )
    held_weights = gather_layer(pieces)
    saved_ticks = []
    result_ticks = []
    arriving = jnp.zeros((row_count, width), jnp.bfloat16)
    for tick_index in range(micro_count + 1):
        weights = held_weights
        own_input = tokens[min(tick_index, micro_count - 1), 0].astype(jnp.float32)
        layer_input = jnp.where(first_section, own_input, arriving.astype(jnp.float32))
        segment = jnp.where(
            first_section,
            segments[min(tick_index, micro_count - 1), 0],
            segments[max(tick_index - 1, 0), 0],
        )
        result, saved = forward_layer(layer_input, weights, segment, row_start)
        result_low = result.astype(jnp.bfloat16)
        result_ticks.append(result_low)
        saved_ticks.append(saved)
        if tick_index < micro_count:
            arriving = from_behind(result_low, "section", 1)
    flow_ticks = []
    shares = None
    gain_sums = None
    operand_ticks = []
    returning = jnp.zeros((row_count, width), jnp.bfloat16)
    for tick_index in range(micro_count + 1):
        weights = held_weights
        later_grad = cotangent[min(tick_index, micro_count - 1), 0].astype(jnp.float32)
        incoming = jnp.where(first_section, returning.astype(jnp.float32), later_grad)
        active = jnp.where(first_section, tick_index >= 1, tick_index < micro_count)
        incoming = jnp.where(active, incoming, 0.0)
        saved = jax.tree.map(
            lambda early_value, late_value: jnp.where(first_section, early_value, late_value),
            saved_ticks[max(tick_index - 1, 0)],
            saved_ticks[min(tick_index + 1, micro_count)],
        )
        grad_inputs, gains, operands = backward_layer(incoming, weights, saved)
        flow_ticks.append(grad_inputs)
        if tick_index < micro_count:
            returning = from_behind(grad_inputs.astype(jnp.bfloat16), "section", -1)
        gain_sums = add_terms(gain_sums, gains)
        operand_ticks.append(operands)
    joined = tuple(
        (
            jnp.concatenate([tick_ops[index_op] for tick_ops in operand_ticks], axis=0)
            for index_op in range(len(operand_ticks[0]))
        )
    )
    full_terms = weight_terms(gain_sums, joined)
    shares = tuple(
        (
            lax.psum_scatter(full_terms[0], "shard", scatter_dimension=0, tiled=True),
            lax.psum_scatter(full_terms[1], "shard", scatter_dimension=0, tiled=True),
            lax.psum_scatter(full_terms[2], "shard", scatter_dimension=0, tiled=True),
            lax.psum_scatter(full_terms[3], "shard", scatter_dimension=0, tiled=True),
            lax.psum_scatter(full_terms[4], "shard", scatter_dimension=0, tiled=True),
            lax.psum_scatter(full_terms[5], "shard", scatter_dimension=0, tiled=True),
            lax.psum_scatter(full_terms[6], "shard", scatter_dimension=0, tiled=True),
            lax.psum_scatter(full_terms[7], "shard", scatter_dimension=0, tiled=True),
            lax.psum_scatter(full_terms[8], "shard", scatter_dimension=0, tiled=True),
        )
    )
    totals = lax.psum(
        (
            shares[0],
            shares[1],
            shares[2],
            shares[3],
            shares[4],
            shares[5],
            shares[6],
            shares[7],
            shares[8],
        ),
        "replica",
    )
    section_outputs = jnp.stack(
        [
            jnp.where(first_section, result_ticks[index_micro], result_ticks[index_micro + 1])
            for index_micro in range(micro_count)
        ]
    )
    input_grads = jnp.stack(
        [
            jnp.where(first_section, flow_ticks[index_micro + 1], flow_ticks[index_micro])
            for index_micro in range(micro_count)
        ]
    )
    return (
        section_outputs[None, :, None],
        input_grads[None, :, None],
        totals[0][None],
        totals[1][None],
        totals[2][None],
        totals[3][None],
        totals[4][None],
        totals[5][None],
        totals[6][None],
        totals[7][None],
        totals[8][None],
    )


def solution(mesh):
    in_specs = (
        P(None, "replica", "shard", None),
        P(None, "replica", None),
        P("section", "shard"),
        P("section", "shard", None),
        P("section", "shard", None),
        P("section", "shard", None),
        P("section", "shard", None),
        P("section", "shard"),
        P("section", "shard", None),
        P("section", "shard", None),
        P("section", "shard", None),
        P(None, "replica", "shard", None),
    )
    out_specs = (
        P("section", None, "replica", "shard", None),
        P("section", None, "replica", "shard", None),
        P("section", "shard"),
        P("section", "shard", None),
        P("section", "shard", None),
        P("section", "shard", None),
        P("section", "shard", None),
        P("section", "shard"),
        P("section", "shard", None),
        P("section", "shard", None),
        P("section", "shard", None),
    )
    return jax.shard_map(body, mesh=mesh, in_specs=in_specs, out_specs=out_specs, check_vma=False)
```

profile of v0, /device:TPU:13, one launch (start us, length us, event | category | flops | bytes accessed | tf_op | source)
XLA Modules:
  0.0 4143.3 jit_solution(9085358403374294909)
XLA Ops:
  19.9 39.5 all-gather.35.cloned.1.call-done
  63.7 16.1 while.50
  79.8 16.1 while.52
  96.0 16.0 while.51
  136.5 12.6 all-gather.23.cloned.1.call-done
  151.6 85.9 %all-gather.39.cloned.1.call-done = bf16[1,1536,1536]{2,1,0:T(8,128)(2,1)} async-done(((bf16[1,384,1536]{2,1,0:T(8,128)(2,1)}), bf16[1,1536,1536]{2,1,0:T(8,128)(2,1)}) %all-gather.39.cloned.1.call-update) | async-done | bytes 4718608 | tf_op jit(solution)/shard_map/all_gather | solution.py:37
  248.3 27.7 all-gather.25.cloned.1.call-done
  303.5 61.3 %all-gather.41.cloned.1.call-done = bf16[1,1536,1536]{2,1,0:T(8,128)(2,1)} async-done(((bf16[1,384,1536]{2,1,0:T(8,128)(2,1)}), bf16[1,1536,1536]{2,1,0:T(8,128)(2,1)}) %all-gather.41.cloned.1.call-update) | async-done | bytes 4718608 | tf_op jit(solution)/shard_map/all_gather | solution.py:40
  369.7 213.1 %all-gather.43.cloned.1.call-done = bf16[1,1536,4096]{2,1,0:T(8,128)(2,1)} async-done(((bf16[1,384,4096]{2,1,0:T(8,128)(2,1)}), bf16[1,1536,4096]{2,1,0:T(8,128)(2,1)}) %all-gather.43.cloned.1.call-update) | async-done | bytes 12582928 | tf_op jit(solution)/shard_map/all_gather | solution.py:44
  582.8 10.6 fusion.61
  593.4 207.4 %all-gather.45.cloned.1.call-done = bf16[1,1536,4096]{2,1,0:T(8,128)(2,1)} async-done(((bf16[1,384,4096]{2,1,0:T(8,128)(2,1)}), bf16[1,1536,4096]{2,1,0:T(8,128)(2,1)}) %all-gather.45.cloned.1.call-update) | async-done | bytes 12582928 | tf_op jit(solution)/shard_map/all_gather | solution.py:45
  800.8 13.2 multiply_convert_fusion.8
  814.0 204.8 %all-gather.47.cloned.1.call-done = bf16[1,4096,1536]{2,1,0:T(8,128)(2,1)} async-done(((bf16[1,1024,1536]{2,1,0:T(8,128)(2,1)}), bf16[1,4096,1536]{2,1,0:T(8,128)(2,1)}) %all-gather.47.cloned.1.call-update) | async-done | bytes 12582928 | tf_op jit(solution)/shard_map/all_gather | solution.py:46
  1029.1 19.0 collective-permute-done
  1062.8 27.0 all-gather.29.cloned.1.call-done
  1108.3 20.2 all-gather.27.cloned.1.call-done
  1157.2 10.9 multiply_convert_fusion.5
  1178.0 12.7 multiply_reduce_fusion.2
  1208.6 13.0 fusion.16
  1231.8 12.1 fusion.18
  1268.1 24.8 reduce-scatter.16.cloned.1.call-done
  1294.1 62.0 %reduce-scatter.14.cloned.1.call-done = f32[256,768]{0,1:T(8,128)} async-done(((f32[1024,768]{0,1:T(8,128)}), f32[256,768]{0,1:T(8,128)}) %reduce-scatter.14.cloned.1.call-update) | async-done | bytes 786448 | tf_op jit(solution)/shard_map/reduce_scatter | solution.py:210
  1394.9 11.4 all-gather.33.cloned.1.call-done
  1424.8 19.9 all-gather.31.cloned.1.call-done
  1474.1 11.1 multiply_convert_fusion.3
  1495.0 12.6 multiply_reduce_fusion.1
  1526.4 13.2 fusion.11
  1539.6 11.5 fusion.13
  1577.4 39.3 reduce-scatter.18.cloned.1.call-done
  1618.0 61.8 %reduce-scatter.20.cloned.1.call-done = f32[256,768]{0,1:T(8,128)} async-done(((f32[1024,768]{0,1:T(8,128)}), f32[256,768]{0,1:T(8,128)}) %reduce-scatter.20.cloned.1.call-update) | async-done | bytes 786448 | tf_op jit(solution)/shard_map/reduce_scatter | solution.py:211
  1694.3 16.2 collective-permute-done.3
  1711.7 11.1 multiply_convert_fusion.1
  1732.9 12.1 multiply_reduce_fusion
  1762.3 13.2 fusion.6
  1785.7 12.4 fusion.8
  1804.8 43.2 %reduce-scatter.24.cloned.1.call-done = f32[256,768]{0,1:T(8,128)} async-done(((f32[1024,768]{0,1:T(8,128)}), f32[256,768]{0,1:T(8,128)}) %reduce-scatter.24.cloned.1.call-update) | async-done | bytes 786448 | tf_op jit(solution)/shard_map/reduce_scatter | solution.py:211
  1855.9 55.2 %reduce-scatter.22.cloned.1.call-done = f32[256,768]{0,1:T(8,128)} async-done(((f32[1024,768]{0,1:T(8,128)}), f32[256,768]{0,1:T(8,128)}) %reduce-scatter.22.cloned.1.call-update) | async-done | bytes 786448 | tf_op jit(solution)/shard_map/reduce_scatter | solution.py:210
  1952.5 17.5 fusion.84
  1972.4 17.7 fusion.72
  1991.2 17.8 fusion.78
  2009.1 79.3 %reduce-scatter.28.cloned.1.call-done = f32[384,768]{1,0:T(8,128)} async-done(((f32[1536,768]{1,0:T(8,128)}), f32[384,768]{1,0:T(8,128)}) %reduce-scatter.28.cloned.1.call-update) | async-done | bytes 1179664 | tf_op jit(solution)/shard_map/reduce_scatter | solution.py:365
  2088.3 164.0 %reduce-scatter.32.cloned.1.call-done = f32[384,1536]{1,0:T(8,128)} async-done(((f32[1536,1536]{1,0:T(8,128)}), f32[384,1536]{1,0:T(8,128)}) %reduce-scatter.32.cloned.1.call-update) | async-done | bytes 2359312 | tf_op jit(solution)/shard_map/reduce_scatter | solution.py:367
  2252.3 164.5 %reduce-scatter.26.cloned.1.call-done = f32[384,1536]{1,0:T(8,128)} async-done(((f32[1536,1536]{1,0:T(8,128)}), f32[384,1536]{1,0:T(8,128)}) %reduce-scatter.26.cloned.1.call-update) | async-done | bytes 2359312 | tf_op jit(solution)/shard_map/reduce_scatter | solution.py:364
  2416.8 417.4 %reduce-scatter.38.cloned.1.call-done = f32[1024,1536]{1,0:T(8,128)} async-done(((f32[4096,1536]{1,0:T(8,128)}), f32[1024,1536]{1,0:T(8,128)}) %reduce-scatter.38.cloned.1.call-update) | async-done | bytes 6291472 | tf_op jit(solution)/shard_map/reduce_scatter | solution.py:371
  2834.2 418.7 %reduce-scatter.34.cloned.1.call-done = f32[384,4096]{1,0:T(8,128)} async-done(((f32[1536,4096]{1,0:T(8,128)}), f32[384,4096]{1,0:T(8,128)}) %reduce-scatter.34.cloned.1.call-update) | async-done | bytes 6291472 | tf_op jit(solution)/shard_map/reduce_scatter | solution.py:369
  3252.9 418.5 %reduce-scatter.36.cloned.1.call-done = f32[384,4096]{1,0:T(8,128)} async-done(((f32[1536,4096]{1,0:T(8,128)}), f32[384,4096]{1,0:T(8,128)}) %reduce-scatter.36.cloned.1.call-update) | async-done | bytes 6291472 | tf_op jit(solution)/shard_map/reduce_scatter | solution.py:370
  3695.3 13.2 all-reduce.2
  3723.3 393.4 %all-reduce.7.cloned.1.call-done = (f32[1,384,1536]{2,1,0:T(8,128)}, f32[1,384,768]{2,1,0:T(8,128)}, f32[1,384,768]{2,1,0:T(8,128)}, f32[1,384,1536]{2,1,0:T(8,1...) async-done(((f32[1,384,1536]{2,1,0:T(8,128)}, f32[1,384,768]{2,1,0:T(8,128)}, f32[1,384,768]{2,1,0:T(8,128)}, ...) | async-done | bytes 25952272 | tf_op jit(solution)/shard_map/psum | solution.py:374
  (843 shorter events, 579.9 us)
Async XLA Ops:
  7.2 52.2 %all-gather.35.cloned.1.call-start = ((), (), s32[]{:S(2)}) async-start(), calls=%async_computation.32 | async-start | bytes 2949120 | tf_op jit(solution)/shard_map/all_gather | solution.py:39
  7.9 105.4 %all-gather.37.cloned.1.call-start = ((), (), s32[]{:S(2)}) async-start(), calls=%async_computation.33 | async-start | bytes 2949120 | tf_op jit(solution)/shard_map/all_gather | solution.py:38
  8.7 140.4 %all-gather.23.cloned.1.call-start = ((), (), s32[]{:S(2)}) async-start(), calls=%async_computation.13 | async-start | bytes 1966080 | tf_op jit(solution)/shard_map/all_gather | solution.py:83
  18.4 1030.1 %copy-start.123 = (f32[1536]{0:T(1024)}, f32[1536]{0:T(1024)S(1)}, u32[]{:S(2)}) copy-start(f32[1536]{0:T(1024)S(1)} %convert_reduce_fusion.1) | copy-start | bytes 18436
  19.9 43.0 %copy-start.159 = (f32[256]{0:T(256)}, f32[256]{0:T(256)S(1)}, u32[]{:S(2)}) copy-start(f32[256]{0:T(256)S(1)} %fusion.217) | copy-start | bytes 3076
  19.9 1028.6 %copy-start.138 = (f32[256]{0:T(256)}, f32[256]{0:T(256)S(1)}, u32[]{:S(2)}) copy-start(f32[256]{0:T(256)S(1)} %add_rsqrt_fusion.5) | copy-start | bytes 3076
  19.9 43.7 %copy-start.165 = (s32[2,1,1024]{2,1,0:T(1,128)S(1)}, s32[2,1,1024]{2,1,0:T(1,128)}, u32[]{:S(2)}) copy-start(s32[2,1,1024]{2,1,0:T(1,128)} %param.19) | copy-start | bytes 24580
  62.9 174.6 %all-gather.39.cloned.1.call-start = ((), (), s32[]{:S(2)}) async-start(), calls=%async_computation.34 | async-start | bytes 5898240 | tf_op jit(solution)/shard_map/all_gather | solution.py:37
  63.5 212.4 %all-gather.25.cloned.1.call-start = ((), (), s32[]{:S(2)}) async-start(), calls=%async_computation.14 | async-start | bytes 1966080 | tf_op jit(solution)/shard_map/all_gather | solution.py:82
  121.2 243.6 %all-gather.41.cloned.1.call-start = ((), (), s32[]{:S(2)}) async-start(), calls=%async_computation.35 | async-start | bytes 5898240 | tf_op jit(solution)/shard_map/all_gather | solution.py:40
  121.8 461.0 %all-gather.43.cloned.1.call-start = ((), (), s32[]{:S(2)}) async-start(), calls=%async_computation.36 | async-start | bytes 15728640 | tf_op jit(solution)/shard_map/all_gather | solution.py:44
  122.5 678.3 %all-gather.45.cloned.1.call-start = ((), (), s32[]{:S(2)}) async-start(), calls=%async_computation.37 | async-start | bytes 15728640 | tf_op jit(solution)/shard_map/all_gather | solution.py:45
  123.3 895.5 %all-gather.47.cloned.1.call-start = ((), (), s32[]{:S(2)}) async-start(), calls=%async_computation.38 | async-start | bytes 15728640 | tf_op jit(solution)/shard_map/all_gather | solution.py:46
  124.0 965.8 %all-gather.29.cloned.1.call-start = ((), (), s32[]{:S(2)}) async-start(), calls=%async_computation.16 | async-start | bytes 1966080 | tf_op jit(solution)/shard_map/all_gather | solution.py:82
  136.5 953.4 %copy-start.62 = (pred[256,1024]{0,1:T(8,128)(4,1)}, pred[256,1024]{0,1:T(8,128)(4,1)S(1)}, u32[]{:S(2)}) copy-start(pred[256,1024]{0,1:T(8,128)(4,1)S(1)} %get-tuple-element.398) | copy-start | bytes 786436
  303.5 66.2 %copy-start.50 = (bf16[8,96,2,256]{3,1,2,0:T(8,128)(2,1)}, bf16[8,96,2,256]{3,1,2,0:T(8,128)(2,1)S(1)}, u32[]{:S(2)}) copy-start(bf16[8,96,2,256]{3,1,2,0:T(8,128)(2,1)S(1)} %fusion.235) | copy-start | bytes 2359300
  369.7 223.7 %copy-start.141 = (f32[256]{0:T(256)}, f32[256]{0:T(256)S(1)}, u32[]{:S(2)}) copy-start(f32[256]{0:T(256)S(1)} %get-tuple-element.429) | copy-start | bytes 3076
  369.7 431.1 %copy-start.150 = (f32[256]{0:T(256)}, f32[256]{0:T(256)S(1)}, u32[]{:S(2)}) copy-start(f32[256]{0:T(256)S(1)} %add_rsqrt_fusion.4) | copy-start | bytes 3076
  1027.8 20.3 collective-permute-start
  1052.3 76.2 %all-gather.27.cloned.1.call-start = ((), (), s32[]{:S(2)}) async-start(), calls=%async_computation.15 | async-start | bytes 1966080 | tf_op jit(solution)/shard_map/all_gather | solution.py:83
  1058.2 234.7 %reduce-scatter.16.cloned.1.call-start = ((), (), s32[]{:S(2)}) async-start(), calls=%async_computation.20 | async-start | bytes 3932160 | tf_op jit(solution)/shard_map/reduce_scatter | solution.py:211
  1062.8 181.1 %copy-start.26 = (bf16[256,8,2,48]{0,3,2,1:T(8,128)(2,1)}, bf16[256,8,2,48]{0,3,2,1:T(8,128)(2,1)S(1)}, u32[]{:S(2)}) copy-start(bf16[256,8,2,48]{0,3,2,1:T(8,128)(2,1)S(1)} %get-tuple-element.373) | copy-start | bytes 1179652
  1098.6 109.9 %copy-start.130 = (f32[8,2,256]{2,1,0:T(2,128)}, f32[8,2,256]{2,1,0:T(2,128)S(1)}, u32[]{:S(2)}) copy-start(f32[8,2,256]{2,1,0:T(2,128)S(1)} %get-tuple-element.433) | copy-start | bytes 49156
  1098.7 41.0 slice-start
  1108.2 100.3 %copy-start.135 = (f32[8,2,256]{2,1,0:T(2,128)}, f32[8,2,256]{2,1,0:T(2,128)S(1)}, u32[]{:S(2)}) copy-start(f32[8,2,256]{2,1,0:T(2,128)S(1)} %fusion.22) | copy-start | bytes 49156
  1231.8 124.4 %reduce-scatter.14.cloned.1.call-start = ((), (), s32[]{:S(2)}) async-start(), calls=%async_computation.19 | async-start | bytes 3932160 | tf_op jit(solution)/shard_map/reduce_scatter | solution.py:210
  1248.4 157.9 %all-gather.33.cloned.1.call-start = ((), (), s32[]{:S(2)}) async-start(), calls=%async_computation.18 | async-start | bytes 1966080 | tf_op jit(solution)/shard_map/all_gather | solution.py:82
  1258.6 101.9 %collective-permute-start.1 = (bf16[256,1536]{1,0:T(8,128)(2,1)}, bf16[256,1536]{1,0:T(8,128)(2,1)}, u32[]{:S(2)}, u32[]{:S(2)}) collective-permute-start(bf16[256,1536]{1,0:T(8,128)(2,1)} %fusion.142), channel_id=1, source_target_pairs={{0,16},{1,17},{2,18},{3,19},{4,20},{5,21},{6,22},{7,23},{8,24},{9,... | collective-permute-start | bytes 2359304 | tf_op jit(solution)/shard_map/ppermute | solution.py:18
  1294.1 66.4 %copy-start.118 = (bf16[256,768]{0,1:T(8,128)(2,1)}, bf16[256,768]{0,1:T(8,128)(2,1)S(1)}, u32[]{:S(2)}) copy-start(bf16[256,768]{0,1:T(8,128)(2,1)S(1)} %convert_element_type.346) | copy-start | bytes 1179652
  1370.3 74.4 %all-gather.31.cloned.1.call-start = ((), (), s32[]{:S(2)}) async-start(), calls=%async_computation.17 | async-start | bytes 1966080 | tf_op jit(solution)/shard_map/all_gather | solution.py:83
  1375.0 18.7 collective-permute-start.2
  1378.8 238.0 %reduce-scatter.18.cloned.1.call-start = ((), (), s32[]{:S(2)}) async-start(), calls=%async_computation.21 | async-start | bytes 3932160 | tf_op jit(solution)/shard_map/reduce_scatter | solution.py:210
  1383.7 167.4 %copy-start.38 = (bf16[256,8,2,48]{0,3,2,1:T(8,128)(2,1)}, bf16[256,8,2,48]{0,3,2,1:T(8,128)(2,1)S(1)}, u32[]{:S(2)}) copy-start(bf16[256,8,2,48]{0,3,2,1:T(8,128)(2,1)S(1)} %get-tuple-element.369) | copy-start | bytes 1179652
  1555.6 124.2 %reduce-scatter.20.cloned.1.call-start = ((), (), s32[]{:S(2)}) async-start(), calls=%async_computation.22 | async-start | bytes 3932160 | tf_op jit(solution)/shard_map/reduce_scatter | solution.py:211
  1565.8 282.1 %reduce-scatter.24.cloned.1.call-start = ((), (), s32[]{:S(2)}) async-start(), calls=%async_computation.24 | async-start | bytes 3932160 | tf_op jit(solution)/shard_map/reduce_scatter | solution.py:211
  1618.0 66.1 %copy-start.78 = (bf16[256,8,96]{0,2,1:T(8,128)(2,1)}, bf16[256,8,96]{0,2,1:T(8,128)(2,1)S(1)}, u32[]{:S(2)}) copy-start(bf16[256,8,96]{0,2,1:T(8,128)(2,1)S(1)} %pad_maximum_fusion.14) | copy-start | bytes 1179652
  1692.1 18.5 collective-permute-start.3
  1785.6 125.5 %reduce-scatter.22.cloned.1.call-start = ((), (), s32[]{:S(2)}) async-start(), calls=%async_computation.23 | async-start | bytes 3932160 | tf_op jit(solution)/shard_map/reduce_scatter | solution.py:210
  1802.6 47.3 %copy-start.119 = (bf16[256,768]{0,1:T(8,128)(2,1)S(1)}, bf16[256,768]{0,1:T(8,128)(2,1)}, u32[]{:S(2)}) copy-start(bf16[256,768]{0,1:T(8,128)(2,1)} %copy-done.118) | copy-start | bytes 1179652
  1802.6 206.5 %reduce-scatter.30.cloned.1.call-start = ((), (), s32[]{:S(2)}) async-start(), calls=%async_computation.27 | async-start | bytes 5898240 | tf_op jit(solution)/shard_map/reduce_scatter | solution.py:366
  1855.8 57.3 %copy-start.75 = (bf16[256,8,96]{0,2,1:T(8,128)(2,1)S(1)}, bf16[256,8,96]{0,2,1:T(8,128)(2,1)}, u32[]{:S(2)}) copy-start(bf16[256,8,96]{0,2,1:T(8,128)(2,1)} %copy-done.74) | copy-start | bytes 1179652
  1855.8 232.5 %reduce-scatter.28.cloned.1.call-start = ((), (), s32[]{:S(2)}) async-start(), calls=%async_computation.26 | async-start | bytes 5898240 | tf_op jit(solution)/shard_map/reduce_scatter | solution.py:365
  1919.1 333.2 %reduce-scatter.32.cloned.1.call-start = ((), (), s32[]{:S(2)}) async-start(), calls=%async_computation.28 | async-start | bytes 11796480 | tf_op jit(solution)/shard_map/reduce_scatter | solution.py:367
  1935.0 481.8 %reduce-scatter.26.cloned.1.call-start = ((), (), s32[]{:S(2)}) async-start(), calls=%async_computation.25 | async-start | bytes 11796480 | tf_op jit(solution)/shard_map/reduce_scatter | solution.py:364
  1948.7 885.5 %reduce-scatter.38.cloned.1.call-start = ((), (), s32[]{:S(2)}) async-start(), calls=%async_computation.31 | async-start | bytes 31457280 | tf_op jit(solution)/shard_map/reduce_scatter | solution.py:371
  1970.1 1282.8 %reduce-scatter.34.cloned.1.call-start = ((), (), s32[]{:S(2)}) async-start(), calls=%async_computation.29 | async-start | bytes 31457280 | tf_op jit(solution)/shard_map/reduce_scatter | solution.py:369
  1990.1 1681.3 %reduce-scatter.36.cloned.1.call-start = ((), (), s32[]{:S(2)}) async-start(), calls=%async_computation.30 | async-start | bytes 31457280 | tf_op jit(solution)/shard_map/reduce_scatter | solution.py:370
  2009.0 2107.7 %all-reduce.7.cloned.1.call-start = ((), (), s32[]{:S(2)}) async-start(), calls=%async_computation.39 | async-start | bytes 51904512 | tf_op jit(solution)/shard_map/psum | solution.py:374
  (188 other events, 1280.3 us)
Sparse Core Ops, SparseCore 0:
  9.6 49.7 all-gather.34
  61.0 49.2 all-gather.36
  112.4 36.5 all-gather.22
  150.5 86.9 all-gather.38
  239.5 36.3 all-gather.24
  277.3 87.3 all-gather.40
  366.3 216.4 all-gather.42
  584.4 216.3 all-gather.44
  802.4 216.3 all-gather.46
  1052.4 37.3 all-gather.28
  1092.0 36.4 all-gather.26
  1231.9 60.9 reduce-scatter.15
  1295.8 60.2 reduce-scatter.13
  1370.4 35.8 all-gather.32
  1408.3 36.3 all-gather.30
  1555.7 60.9 reduce-scatter.17
  1619.5 60.2 reduce-scatter.19
  1785.8 62.1 reduce-scatter.23
  1850.8 60.2 reduce-scatter.21
  1913.8 85.7 reduce-scatter.29
  2002.5 85.7 reduce-scatter.27
  2090.7 161.5 reduce-scatter.31
  2254.7 162.1 reduce-scatter.25
  2419.1 415.1 reduce-scatter.37
  2836.7 416.1 reduce-scatter.33
  3255.2 416.1 reduce-scatter.35
  3674.9 441.7 all-reduce.6
where the time goes:
time: 4150 us; the launch traced here: 4140 us
  waiting for transfers between devices  3320 us (80%)
  matrix products  504 us (12%)
  other arithmetic  129 us (3%)
  local copies, waits for them, and re-layouts  116 us (3%)
  blocking collectives  42.1 us (1%)
    reduce_scatter x1, waiting for transfers between devices, body(): lax.psum_scatter(full_terms[6], 'shard', scatter_dimension=0, tiled=True)  419 us
    reduce_scatter x1, waiting for transfers between devices, body(): lax.psum_scatter(full_terms[7], 'shard', scatter_dimension=0, tiled=True)  418 us
    reduce_scatter x1, waiting for transfers between devices, body(): lax.psum_scatter(full_terms[8], 'shard', scatter_dimension=0, tiled=True)  417 us
    psum x1, waiting for transfers between devices, body(): lax.psum((shares[0], shares[1], shares[2], shares[3], shares[4], shares[5...  393 us
    all_gather x1, waiting for transfers between devices, gather_layer(): lax.all_gather(pieces[6], 'shard', axis=0, tiled=True)  213 us
    all_gather x1, waiting for transfers between devices, gather_layer(): lax.all_gather(pieces[7], 'shard', axis=0, tiled=True)  207 us
    all_gather x1, waiting for transfers between devices, gather_layer(): lax.all_gather(pieces[8], 'shard', axis=0, tiled=True)  205 us
    reduce_scatter x1, waiting for transfers between devices, body(): lax.psum_scatter(full_terms[1], 'shard', scatter_dimension=0, tiled=True)  165 us
  transfers between devices with their start and end apart: 31, of which 28 were waited for; matrix products, arithmetic and copies ran while one was open for 9% of the time, Pallas kernels for 0%

commit v1 on v0

--- a/solution.py
+++ b/solution.py
@@ -31,21 +31,24 @@
     )
 
 
+def gather_rows(piece):
+    if piece.ndim == 1:
+        return lax.all_gather(piece, "shard", axis=0, tiled=True)
+    rows = piece.shape[0] // lax.axis_size("replica")
+    own = lax.dynamic_slice_in_dim(piece, lax.axis_index("replica") * rows, rows)
+    return lax.all_gather(own, ("shard", "replica"), axis=0, tiled=True)
+
+
+def scatter_rows(term):
+    if term.ndim == 1:
+        return lax.psum(lax.psum_scatter(term, "shard", scatter_dimension=0, tiled=True), "replica")
+    low = term.astype(jnp.bfloat16)
+    part = lax.psum_scatter(low, ("shard", "replica"), scatter_dimension=0, tiled=True)
+    return lax.all_gather(part, "replica", axis=0, tiled=True).astype(jnp.float32)
+
+
 def gather_layer(pieces):
-    attention = (
-        lax.all_gather(pieces[0], "shard", axis=0, tiled=True),
-        lax.all_gather(pieces[1], "shard", axis=0, tiled=True),
-        lax.all_gather(pieces[2], "shard", axis=0, tiled=True),
-        lax.all_gather(pieces[3], "shard", axis=0, tiled=True),
-        lax.all_gather(pieces[4], "shard", axis=0, tiled=True),
-    )
-    feedforward = (
-        lax.all_gather(pieces[5], "shard", axis=0, tiled=True),
-        lax.all_gather(pieces[6], "shard", axis=0, tiled=True),
-        lax.all_gather(pieces[7], "shard", axis=0, tiled=True),
-        lax.all_gather(pieces[8], "shard", axis=0, tiled=True),
-    )
-    return tuple(attention) + tuple(feedforward)
+    return tuple(gather_rows(piece) for piece in pieces)
 
 
 def forward_layer(inputs, weights, segment, row_start):
@@ -56,7 +59,7 @@
     half_dim = HD // 2
     local_segment = lax.dynamic_slice_in_dim(segment, row_start, row_count)
     query_index = row_start + jnp.arange(row_count, dtype=jnp.int32)
-    starts = jnp.searchsorted(segment, local_segment, side="left")
+    starts = jnp.sum((segment[None, :] < local_segment[:, None]).astype(jnp.int32), axis=1)
     positions = query_index - starts
     frequency = ROPE_BASE ** (-(jnp.arange(half_dim, dtype=jnp.float32) * 2.0) / HD)
     angles = positions.astype(jnp.float32)[:, None, None] * frequency[None, None, :]
@@ -207,8 +210,12 @@
     key_terms = key_terms.reshape(seq_length, KVH * HD)
     value_terms = value_terms.reshape(seq_length, KVH * HD)
     grad_keys, grad_values = (
-        lax.psum_scatter(key_terms, "shard", scatter_dimension=0, tiled=True),
-        lax.psum_scatter(value_terms, "shard", scatter_dimension=0, tiled=True),
+        lax.psum_scatter(
+            key_terms.astype(jnp.bfloat16), "shard", scatter_dimension=0, tiled=True
+        ).astype(jnp.float32),
+        lax.psum_scatter(
+            value_terms.astype(jnp.bfloat16), "shard", scatter_dimension=0, tiled=True
+        ).astype(jnp.float32),
     )
     query_low = rotate(grad_queries, cosine_table[:, :, None, :], sine_table[:, :, None, :], -1.0)
     query_low = query_low.reshape(row_count, QH * HD).astype(jnp.bfloat16)
@@ -330,7 +337,6 @@
         if tick_index < micro_count:
             arriving = from_behind(result_low, "section", 1)
     flow_ticks = []
-    shares = None
     gain_sums = None
     operand_ticks = []
     returning = jnp.zeros((row_count, width), jnp.bfloat16)
@@ -358,33 +364,7 @@
         )
     )
     full_terms = weight_terms(gain_sums, joined)
-    shares = tuple(
-        (
-            lax.psum_scatter(full_terms[0], "shard", scatter_dimension=0, tiled=True),
-            lax.psum_scatter(full_terms[1], "shard", scatter_dimension=0, tiled=True),
-            lax.psum_scatter(full_terms[2], "shard", scatter_dimension=0, tiled=True),
-            lax.psum_scatter(full_terms[3], "shard", scatter_dimension=0, tiled=True),
-            lax.psum_scatter(full_terms[4], "shard", scatter_dimension=0, tiled=True),
-            lax.psum_scatter(full_terms[5], "shard", scatter_dimension=0, tiled=True),
-            lax.psum_scatter(full_terms[6], "shard", scatter_dimension=0, tiled=True),
-            lax.psum_scatter(full_terms[7], "shard", scatter_dimension=0, tiled=True),
-            lax.psum_scatter(full_terms[8], "shard", scatter_dimension=0, tiled=True),
-        )
-    )
-    totals = lax.psum(
-        (
-            shares[0],
-            shares[1],
-            shares[2],
-            shares[3],
-            shares[4],
-            shares[5],
-            shares[6],
-            shares[7],
-            shares[8],
-        ),
-        "replica",
-    )
+    totals = tuple(scatter_rows(term) for term in full_terms)
     section_outputs = jnp.stack(
         [
             jnp.where(first_section, result_ticks[index_micro], result_ticks[index_micro + 1])

time: 4150 us -> 2170 us (0.52)
  waiting for transfers between devices: 3320 us -> 1360 us
  local copies, waits for them, and re-layouts: 116 us -> 60 us
    reduce_scatter x13, waiting for transfers between devices: 1950 us -> 676 us  [the longest x7 601 us: scatter_rows(): lax.psum_scatter(low, ('shard', 'replica'), scatter_dimension=0, tiled=True)]
    psum x1 -> x0, waiting for transfers between devices: 393 us -> none  [body(): lax.psum((shares[0], shares[1], shares[2], shares[3], shares[4], shares[5...]
    all_gather x7 -> x12, waiting for transfers between devices: 812 us -> 530 us  [the longest x7 430 us: gather_rows(): return lax.all_gather(own, ('shard', 'replica'), axis=0, tiled=True)]
    gather x33 -> x0, local copies, waits for them, and re-layouts: 45.1 us -> none  [forward_layer(): starts = jnp.searchsorted(segment, local_segment, side='left')]
  transfers between devices with their start and end apart: 31 -> 35, of which waited for: 28 -> 33; matrix products, arithmetic and copies ran while one was open for 9% -> 17% of each run, Pallas kernels for 0% -> 0%
where the time goes in v1:
time: 2170 us; the launch traced here: 2160 us
  waiting for transfers between devices  1360 us (63%)
  matrix products  505 us (23%)
  other arithmetic  150 us (7%)
  blocking collectives  60.8 us (3%)
  local copies, waits for them, and re-layouts  60 us (3%)
    reduce_scatter x7, waiting for transfers between devices, scatter_rows(): lax.psum_scatter(low, ('shard', 'replica'), scatter_dimension=0, tiled=True)  601 us
    all_gather x7, waiting for transfers between devices, gather_rows(): return lax.all_gather(own, ('shard', 'replica'), axis=0, tiled=True)  430 us
    all_gather x5, waiting for transfers between devices, scatter_rows(): lax.all_gather(part, 'replica', axis=0, tiled=True).astype(jnp.float32)  101 us
    dot_general x7, matrix products, row_product(): jnp.einsum('td,tq->dq', left, right, preferred_element_type=jnp.float32)  68.7 us
    all_gather x3, waiting for transfers between devices, forward_layer(): lax.all_gather(key_rows, 'shard', axis=0, tiled=True)  60.9 us
    reduce_scatter x3, waiting for transfers between devices, backward_layer(): lax.psum_scatter(value_terms.astype(jnp.bfloat16), 'shard', scatter_dimen...  60.9 us
    all_gather x3, waiting for transfers between devices, forward_layer(): lax.all_gather(value_rows, 'shard', axis=0, tiled=True)  47.2 us
    ppermute x4, waiting for transfers between devices, from_behind(): return lax.ppermute(x, axis, pairs)  43.9 us
  transfers between devices with their start and end apart: 35, of which 33 were waited for; matrix products, arithmetic and copies ran while one was open for 17% of the time, Pallas kernels for 0%

profile of v1, /device:TPU:13, one launch (start us, length us, event | category | flops | bytes accessed | tf_op | source)
XLA Modules:
  0.0 2162.9 jit_solution(18011308757566453221)
XLA Ops:
  21.9 32.4 %all-gather.50.cloned.1.call-done = bf16[1,1536,768]{2,1,0:T(8,128)(2,1)} async-done(((bf16[1,96,768]{2,1,0:T(8,128)(2,1)}), bf16[1,1536,768]{2,1,0:T(8,128)(2,1)}) %all-gather.50.cloned.1.call-update) | async-done | bytes 2359312 | tf_op jit(solution)/shard_map/all_gather | solution.py:39
  61.7 36.5 %all-gather.52.cloned.1.call-done = bf16[1,1536,768]{2,1,0:T(8,128)(2,1)} async-done(((bf16[1,96,768]{2,1,0:T(8,128)(2,1)}), bf16[1,1536,768]{2,1,0:T(8,128)(2,1)}) %all-gather.52.cloned.1.call-update) | async-done | bytes 2359312 | tf_op jit(solution)/shard_map/all_gather | solution.py:39
  137.0 54.8 %all-gather.54.cloned.1.call-done = bf16[1,1536,1536]{2,1,0:T(8,128)(2,1)} async-done(((bf16[1,96,1536]{2,1,0:T(8,128)(2,1)}), bf16[1,1536,1536]{2,1,0:T(8,128)(2,1)}) %all-gather.54.cloned.1.call-update) | async-done | bytes 4718608 | tf_op jit(solution)/shard_map/all_gather | solution.py:39
  203.7 23.7 %all-gather.30.cloned.1.call-done = bf16[1024,768]{0,1:T(8,128)(2,1)} async-done(((bf16[256,768]{0,1:T(8,128)(2,1)}), bf16[1024,768]{0,1:T(8,128)(2,1)}) %all-gather.30.cloned.1.call-update) | async-done | bytes 1572880 | tf_op jit(solution)/shard_map/all_gather | solution.py:85
  256.9 27.4 %all-gather.56.cloned.1.call-done = bf16[1,1536,1536]{2,1,0:T(8,128)(2,1)} async-done(((bf16[1,96,1536]{2,1,0:T(8,128)(2,1)}), bf16[1,1536,1536]{2,1,0:T(8,128)(2,1)}) %all-gather.56.cloned.1.call-update) | async-done | bytes 4718608 | tf_op jit(solution)/shard_map/all_gather | solution.py:39
  288.9 96.2 %all-gather.58.cloned.1.call-done = bf16[1,1536,4096]{2,1,0:T(8,128)(2,1)} async-done(((bf16[1,96,4096]{2,1,0:T(8,128)(2,1)}), bf16[1,1536,4096]{2,1,0:T(8,128)(2,1)}) %all-gather.58.cloned.1.call-update) | async-done | bytes 12582928 | tf_op jit(solution)/shard_map/all_gather | solution.py:39
  394.8 92.2 %all-gather.60.cloned.1.call-done = bf16[1,1536,4096]{2,1,0:T(8,128)(2,1)} async-done(((bf16[1,96,4096]{2,1,0:T(8,128)(2,1)}), bf16[1,1536,4096]{2,1,0:T(8,128)(2,1)}) %all-gather.60.cloned.1.call-update) | async-done | bytes 12582928 | tf_op jit(solution)/shard_map/all_gather | solution.py:39
  487.0 11.3 multiply_convert_fusion.8
  498.2 90.5 %all-gather.62.cloned.1.call-done = bf16[1,4096,1536]{2,1,0:T(8,128)(2,1)} async-done(((bf16[1,256,1536]{2,1,0:T(8,128)(2,1)}), bf16[1,4096,1536]{2,1,0:T(8,128)(2,1)}) %all-gather.62.cloned.1.call-update) | async-done | bytes 12582928 | tf_op jit(solution)/shard_map/all_gather | solution.py:39
  598.7 19.5 collective-permute-done
  633.5 25.5 %all-gather.34.cloned.1.call-done = bf16[1024,768]{0,1:T(8,128)(2,1)} async-done(((bf16[256,768]{0,1:T(8,128)(2,1)}), bf16[1024,768]{0,1:T(8,128)(2,1)}) %all-gather.34.cloned.1.call-update) | async-done | bytes 1572880 | tf_op jit(solution)/shard_map/all_gather | solution.py:85
  668.0 10.1 fusion.16
  678.1 19.4 all-gather.32.cloned.1.call-done
  728.8 10.6 multiply_convert_fusion.5
  749.4 12.6 multiply_reduce_fusion.2
  778.0 13.1 fusion.10
  791.1 11.5 fusion.12
  847.1 29.6 %reduce-scatter.16.cloned.1.call-done = bf16[256,768]{0,1:T(8,128)(2,1)} async-done(((bf16[1024,768]{0,1:T(8,128)(2,1)}), bf16[256,768]{0,1:T(8,128)(2,1)}) %reduce-scatter.16.cloned.1.call-update) | async-done | bytes 393232 | tf_op jit(solution)/shard_map/reduce_scatter | solution.py:216
  912.4 11.8 all-gather.38.cloned.1.call-done
  944.2 17.8 all-gather.36.cloned.1.call-done
  992.3 10.8 multiply_convert_fusion.3
  1013.0 12.6 multiply_reduce_fusion.1
  1043.6 13.0 fusion.5
  1056.6 11.5 fusion.7
  1093.3 12.4 reduce-scatter.18.cloned.1.call-done
  1110.9 31.2 %reduce-scatter.20.cloned.1.call-done = bf16[256,768]{0,1:T(8,128)(2,1)} async-done(((bf16[1024,768]{0,1:T(8,128)(2,1)}), bf16[256,768]{0,1:T(8,128)(2,1)}) %reduce-scatter.20.cloned.1.call-update) | async-done | bytes 393232 | tf_op jit(solution)/shard_map/reduce_scatter | solution.py:216
  1152.6 15.3 collective-permute-done.3
  1169.0 11.1 multiply_convert_fusion.1
  1190.1 12.1 multiply_reduce_fusion
  1218.7 13.0 fusion
  1241.4 12.1 fusion.2
  1290.8 15.8 convolution_convert_fusion
  1308.9 15.9 convolution_convert_fusion.2
  1326.0 16.0 convolution_convert_fusion.1
  1354.9 39.5 %reduce-scatter.32.cloned.1.call-done = bf16[96,1536]{1,0:T(8,128)(2,1)} async-done(((bf16[1536,1536]{1,0:T(8,128)(2,1)}), bf16[96,1536]{1,0:T(8,128)(2,1)}) %reduce-scatter.32.cloned.1.call-update) | async-done | bytes 294928 | tf_op jit(solution)/shard_map/reduce_scatter | solution.py:46
  1394.5 79.5 %reduce-scatter.26.cloned.1.call-done = bf16[96,1536]{1,0:T(8,128)(2,1)} async-done(((bf16[1536,1536]{1,0:T(8,128)(2,1)}), bf16[96,1536]{1,0:T(8,128)(2,1)}) %reduce-scatter.26.cloned.1.call-update) | async-done | bytes 294928 | tf_op jit(solution)/shard_map/reduce_scatter | solution.py:46
  1474.1 138.8 %reduce-scatter.38.cloned.1.call-done = bf16[256,1536]{1,0:T(8,128)(2,1)} async-done(((bf16[4096,1536]{1,0:T(8,128)(2,1)}), bf16[256,1536]{1,0:T(8,128)(2,1)}) %reduce-scatter.38.cloned.1.call-update) | async-done | bytes 786448 | tf_op jit(solution)/shard_map/reduce_scatter | solution.py:46
  1613.0 137.9 %reduce-scatter.34.cloned.1.call-done = bf16[96,4096]{1,0:T(8,128)(2,1)} async-done(((bf16[1536,4096]{1,0:T(8,128)(2,1)}), bf16[96,4096]{1,0:T(8,128)(2,1)}) %reduce-scatter.34.cloned.1.call-update) | async-done | bytes 786448 | tf_op jit(solution)/shard_map/reduce_scatter | solution.py:46
  1775.2 113.5 %reduce-scatter.36.cloned.1.call-done = bf16[96,4096]{1,0:T(8,128)(2,1)} async-done(((bf16[1536,4096]{1,0:T(8,128)(2,1)}), bf16[96,4096]{1,0:T(8,128)(2,1)}) %reduce-scatter.36.cloned.1.call-update) | async-done | bytes 786448 | tf_op jit(solution)/shard_map/reduce_scatter | solution.py:46
  1893.3 11.4 all-reduce.2
  1918.5 35.5 %reduce-scatter.30.cloned.1.call-done = bf16[96,768]{1,0:T(8,128)(2,1)} async-done(((bf16[1536,768]{1,0:T(8,128)(2,1)}), bf16[96,768]{1,0:T(8,128)(2,1)}) %reduce-scatter.30.cloned.1.call-update) | async-done | bytes 147472 | tf_op jit(solution)/shard_map/reduce_scatter | solution.py:46
  1953.9 10.2 all_gather.83
  1964.1 56.5 %reduce-scatter.28.cloned.1.call-done = bf16[96,768]{1,0:T(8,128)(2,1)} async-done(((bf16[1536,768]{1,0:T(8,128)(2,1)}), bf16[96,768]{1,0:T(8,128)(2,1)}) %reduce-scatter.28.cloned.1.call-update) | async-done | bytes 147472 | tf_op jit(solution)/shard_map/reduce_scatter | solution.py:46
  2020.6 10.2 all_gather.82
  2044.0 16.1 all-gather.40.cloned.1.call-done
  2063.1 27.2 %all-gather.48.cloned.1.call-done = bf16[1024,1536]{1,0:T(8,128)(2,1)} async-done(((bf16[256,1536]{1,0:T(8,128)(2,1)}), bf16[1024,1536]{1,0:T(8,128)(2,1)}) %all-gather.48.cloned.1.call-update) | async-done | bytes 3145744 | tf_op jit(solution)/shard_map/all_gather | solution.py:47
  2095.7 24.5 %all-gather.44.cloned.1.call-done = bf16[384,4096]{1,0:T(8,128)(2,1)} async-done(((bf16[96,4096]{1,0:T(8,128)(2,1)}), bf16[384,4096]{1,0:T(8,128)(2,1)}) %all-gather.44.cloned.1.call-update) | async-done | bytes 3145744 | tf_op jit(solution)/shard_map/all_gather | solution.py:47
  2125.6 24.8 %all-gather.46.cloned.1.call-done = bf16[384,4096]{1,0:T(8,128)(2,1)} async-done(((bf16[96,4096]{1,0:T(8,128)(2,1)}), bf16[384,4096]{1,0:T(8,128)(2,1)}) %all-gather.46.cloned.1.call-update) | async-done | bytes 3145744 | tf_op jit(solution)/shard_map/all_gather | solution.py:47
  (658 shorter events, 570.4 us)
Async XLA Ops:
  7.2 100.9 %copy-start = (bf16[1,384,4096]{2,1,0:T(8,128)(2,1)S(1)}, bf16[1,384,4096]{2,1,0:T(8,128)(2,1)}, u32[]{:S(2)}) copy-start(bf16[1,384,4096]{2,1,0:T(8,128)(2,1)} %param.20) | copy-start | bytes 9437188
  7.2 47.0 %all-gather.50.cloned.1.call-start = ((), (), s32[]{:S(2)}) async-start(), calls=%async_computation.37 | async-start | bytes 2506752 | tf_op jit(solution)/shard_map/all_gather | solution.py:39
  9.0 89.2 %all-gather.52.cloned.1.call-start = ((), (), s32[]{:S(2)}) async-start(), calls=%async_computation.38 | async-start | bytes 2506752 | tf_op jit(solution)/shard_map/all_gather | solution.py:39
  10.7 124.6 %all-gather.28.cloned.1.call-start = ((), (), s32[]{:S(2)}) async-start(), calls=%async_computation.13 | async-start | bytes 1966080 | tf_op jit(solution)/shard_map/all_gather | solution.py:86
  20.4 598.7 %copy-start.128 = (f32[1536]{0:T(1024)}, f32[1536]{0:T(1024)S(1)}, u32[]{:S(2)}) copy-start(f32[1536]{0:T(1024)S(1)} %convert_reduce_fusion.4) | copy-start | bytes 18436
  21.8 176.7 %copy-start.147 = (f32[256]{0:T(256)}, f32[256]{0:T(256)S(1)}, u32[]{:S(2)}) copy-start(f32[256]{0:T(256)S(1)} %add_rsqrt_fusion.5) | copy-start | bytes 3076
  57.8 134.0 %all-gather.54.cloned.1.call-start = ((), (), s32[]{:S(2)}) async-start(), calls=%async_computation.39 | async-start | bytes 5013504 | tf_op jit(solution)/shard_map/all_gather | solution.py:39
  59.5 167.8 %all-gather.30.cloned.1.call-start = ((), (), s32[]{:S(2)}) async-start(), calls=%async_computation.14 | async-start | bytes 1966080 | tf_op jit(solution)/shard_map/all_gather | solution.py:85
  61.7 43.6 %copy-start.126 = (f32[256,48]{0,1:T(8,128)}, f32[256,48]{0,1:T(8,128)S(1)}, u32[]{:S(2)}) copy-start(f32[256,48]{0,1:T(8,128)S(1)} %get-tuple-element.139) | copy-start | bytes 147460
  106.2 178.1 %all-gather.56.cloned.1.call-start = ((), (), s32[]{:S(2)}) async-start(), calls=%async_computation.40 | async-start | bytes 5013504 | tf_op jit(solution)/shard_map/all_gather | solution.py:39
  108.0 277.1 %all-gather.58.cloned.1.call-start = ((), (), s32[]{:S(2)}) async-start(), calls=%async_computation.41 | async-start | bytes 13369344 | tf_op jit(solution)/shard_map/all_gather | solution.py:39
  109.1 377.9 %all-gather.60.cloned.1.call-start = ((), (), s32[]{:S(2)}) async-start(), calls=%async_computation.42 | async-start | bytes 13369344 | tf_op jit(solution)/shard_map/all_gather | solution.py:39
  111.2 477.6 %all-gather.62.cloned.1.call-start = ((), (), s32[]{:S(2)}) async-start(), calls=%async_computation.43 | async-start | bytes 13369344 | tf_op jit(solution)/shard_map/all_gather | solution.py:39
  113.3 545.6 %all-gather.34.cloned.1.call-start = ((), (), s32[]{:S(2)}) async-start(), calls=%async_computation.16 | async-start | bytes 1966080 | tf_op jit(solution)/shard_map/all_gather | solution.py:85
  137.0 109.9 %copy-start.20 = (bf16[1024,768]{0,1:T(8,128)(2,1)}, bf16[1024,768]{0,1:T(8,128)(2,1)S(1)}, u32[]{:S(2)}) copy-start(bf16[1024,768]{0,1:T(8,128)(2,1)S(1)} %copy.94) | copy-start | bytes 4718596
  288.4 300.4 %copy-start.48 = (f32[256,1536]{1,0:T(8,128)}, f32[256,1536]{1,0:T(8,128)S(1)}, u32[]{:S(2)}) copy-start(f32[256,1536]{1,0:T(8,128)S(1)} %get-tuple-element.155) | copy-start | bytes 4718596
  288.9 198.0 %copy-start.160 = (f32[256]{0:T(256)}, f32[256]{0:T(256)S(1)}, u32[]{:S(2)}) copy-start(f32[256]{0:T(256)S(1)} %add_rsqrt_fusion.4) | copy-start | bytes 3076
  597.4 20.8 collective-permute-start
  623.5 74.0 %all-gather.32.cloned.1.call-start = ((), (), s32[]{:S(2)}) async-start(), calls=%async_computation.15 | async-start | bytes 1966080 | tf_op jit(solution)/shard_map/all_gather | solution.py:86
  628.8 211.4 %reduce-scatter.14.cloned.1.call-start = ((), (), s32[]{:S(2)}) async-start(), calls=%async_computation.19 | async-start | bytes 1966080 | tf_op jit(solution)/shard_map/reduce_scatter | solution.py:213
  633.5 169.2 %copy-start.31 = (bf16[256,8,2,48]{0,3,2,1:T(8,128)(2,1)}, bf16[256,8,2,48]{0,3,2,1:T(8,128)(2,1)S(1)}, u32[]{:S(2)}) copy-start(bf16[256,8,2,48]{0,3,2,1:T(8,128)(2,1)S(1)} %get-tuple-element.98) | copy-start | bytes 1179652
  712.5 49.5 %copy-start.162 = (f32[256]{0:T(256)}, f32[256]{0:T(256)S(1)}, u32[]{:S(2)}) copy-start(f32[256]{0:T(256)S(1)} %get-tuple-element.150) | copy-start | bytes 3076
  806.5 70.2 %reduce-scatter.16.cloned.1.call-start = ((), (), s32[]{:S(2)}) async-start(), calls=%async_computation.20 | async-start | bytes 1966080 | tf_op jit(solution)/shard_map/reduce_scatter | solution.py:216
  816.5 107.7 %all-gather.38.cloned.1.call-start = ((), (), s32[]{:S(2)}) async-start(), calls=%async_computation.18 | async-start | bytes 1966080 | tf_op jit(solution)/shard_map/all_gather | solution.py:85
  826.6 20.5 collective-permute-start.1
  887.8 74.2 %all-gather.36.cloned.1.call-start = ((), (), s32[]{:S(2)}) async-start(), calls=%async_computation.17 | async-start | bytes 1966080 | tf_op jit(solution)/shard_map/all_gather | solution.py:86
  892.4 17.8 collective-permute-start.2
  897.0 208.6 %reduce-scatter.18.cloned.1.call-start = ((), (), s32[]{:S(2)}) async-start(), calls=%async_computation.21 | async-start | bytes 1966080 | tf_op jit(solution)/shard_map/reduce_scatter | solution.py:213
  902.7 165.4 %copy-start.42 = (bf16[256,8,2,48]{0,3,2,1:T(8,128)(2,1)}, bf16[256,8,2,48]{0,3,2,1:T(8,128)(2,1)S(1)}, u32[]{:S(2)}) copy-start(bf16[256,8,2,48]{0,3,2,1:T(8,128)(2,1)S(1)} %get-tuple-element.94) | copy-start | bytes 1179652
  1072.0 70.1 %reduce-scatter.20.cloned.1.call-start = ((), (), s32[]{:S(2)}) async-start(), calls=%async_computation.22 | async-start | bytes 1966080 | tf_op jit(solution)/shard_map/reduce_scatter | solution.py:216
  1081.9 260.2 %reduce-scatter.24.cloned.1.call-start = ((), (), s32[]{:S(2)}) async-start(), calls=%async_computation.24 | async-start | bytes 1966080 | tf_op jit(solution)/shard_map/reduce_scatter | solution.py:216
  1150.1 17.8 collective-permute-start.3
  1241.3 107.4 %reduce-scatter.22.cloned.1.call-start = ((), (), s32[]{:S(2)}) async-start(), calls=%async_computation.23 | async-start | bytes 1966080 | tf_op jit(solution)/shard_map/reduce_scatter | solution.py:213
  1257.4 137.0 %reduce-scatter.32.cloned.1.call-start = ((), (), s32[]{:S(2)}) async-start(), calls=%async_computation.29 | async-start | bytes 5013504 | tf_op jit(solution)/shard_map/reduce_scatter | solution.py:46
  1272.3 201.7 %reduce-scatter.26.cloned.1.call-start = ((), (), s32[]{:S(2)}) async-start(), calls=%async_computation.25 | async-start | bytes 5013504 | tf_op jit(solution)/shard_map/reduce_scatter | solution.py:46
  1286.8 326.1 %reduce-scatter.38.cloned.1.call-start = ((), (), s32[]{:S(2)}) async-start(), calls=%async_computation.35 | async-start | bytes 13369344 | tf_op jit(solution)/shard_map/reduce_scatter | solution.py:46
  1306.6 444.2 %reduce-scatter.34.cloned.1.call-start = ((), (), s32[]{:S(2)}) async-start(), calls=%async_computation.31 | async-start | bytes 13369344 | tf_op jit(solution)/shard_map/reduce_scatter | solution.py:46
  1324.9 563.8 %reduce-scatter.36.cloned.1.call-start = ((), (), s32[]{:S(2)}) async-start(), calls=%async_computation.33 | async-start | bytes 13369344 | tf_op jit(solution)/shard_map/reduce_scatter | solution.py:46
  1342.1 611.9 %reduce-scatter.30.cloned.1.call-start = ((), (), s32[]{:S(2)}) async-start(), calls=%async_computation.28 | async-start | bytes 2506752 | tf_op jit(solution)/shard_map/reduce_scatter | solution.py:46
  1348.4 672.2 %reduce-scatter.28.cloned.1.call-start = ((), (), s32[]{:S(2)}) async-start(), calls=%async_computation.27 | async-start | bytes 2506752 | tf_op jit(solution)/shard_map/reduce_scatter | solution.py:46
  1354.9 396.1 %copy-start.188 = (u32[32]{0:T(128)S(1)}, u32[32]{0:T(128)}, u32[]{:S(2)}) copy-start(u32[32]{0:T(128)} %constant.95) | copy-start | bytes 388
  1354.9 686.2 %all-gather.42.cloned.1.call-start = ((), (), s32[]{:S(2)}) async-start(), calls=%async_computation.30 | async-start | bytes 1474560 | tf_op jit(solution)/shard_map/all_gather | solution.py:47
  1394.5 665.6 %all-gather.40.cloned.1.call-start = ((), (), s32[]{:S(2)}) async-start(), calls=%async_computation.26 | async-start | bytes 1474560 | tf_op jit(solution)/shard_map/all_gather | solution.py:47
  1474.0 279.5 %copy-start.55 = (f32[256,1536]{1,0:T(8,128)S(1)}, f32[256,1536]{1,0:T(8,128)}, u32[]{:S(2)}) copy-start(f32[256,1536]{1,0:T(8,128)} %copy-done.53) | copy-start | bytes 4718596
  1474.0 616.2 %all-gather.48.cloned.1.call-start = ((), (), s32[]{:S(2)}) async-start(), calls=%async_computation.36 | async-start | bytes 3932160 | tf_op jit(solution)/shard_map/all_gather | solution.py:47
  1612.9 507.3 %all-gather.44.cloned.1.call-start = ((), (), s32[]{:S(2)}) async-start(), calls=%async_computation.32 | async-start | bytes 3932160 | tf_op jit(solution)/shard_map/all_gather | solution.py:47
  1750.9 399.5 %all-gather.46.cloned.1.call-start = ((), (), s32[]{:S(2)}) async-start(), calls=%async_computation.34 | async-start | bytes 3932160 | tf_op jit(solution)/shard_map/all_gather | solution.py:47
  1771.4 117.3 %copy-start.176 = (f32[256]{0:T(256)S(1)}, f32[256]{0:T(256)}, u32[]{:S(2)}) copy-start(f32[256]{0:T(256)} %get-tuple-element.143) | copy-start | bytes 3076
  (192 other events, 1783.3 us)
Sparse Core Ops, SparseCore 0:
  10.9 43.2 all-gather.49
  57.1 41.0 all-gather.51
  100.4 34.8 all-gather.27
  138.0 53.7 all-gather.53
  193.8 33.5 all-gather.29
  230.0 54.1 all-gather.55
  287.1 97.9 all-gather.57
  388.0 98.9 all-gather.59
  489.8 98.9 all-gather.61
  623.6 35.2 all-gather.33
  661.1 36.3 all-gather.31
  806.7 33.4 reduce-scatter.13
  842.5 34.2 reduce-scatter.15
  887.9 36.2 all-gather.37
  925.6 36.3 all-gather.35
  1072.1 33.4 reduce-scatter.17
  1107.8 34.2 reduce-scatter.19
  1241.4 37.0 reduce-scatter.23
  1281.4 34.2 reduce-scatter.21
  1319.9 74.4 reduce-scatter.31
  1399.4 74.5 reduce-scatter.25
  1478.1 134.7 reduce-scatter.37
  1616.9 133.8 reduce-scatter.33
  1754.8 133.8 reduce-scatter.35
  1893.0 60.8 reduce-scatter.29
  1958.6 62.0 reduce-scatter.27
  2022.0 18.9 all-gather.41
  2042.6 17.4 all-gather.39
  2061.7 28.5 all-gather.47
  2091.6 28.5 all-gather.43
  2121.8 28.5 all-gather.45

commit v2 on v1

--- a/solution.py
+++ b/solution.py
@@ -1,6 +1,10 @@
+import functools
+
 import jax
 import jax.numpy as jnp
 from jax import lax
+from jax.experimental import pallas as pl
+from jax.experimental.pallas import tpu as pltpu
 from jax.sharding import PartitionSpec as P
 
 QH = 16
@@ -31,28 +35,520 @@
     )
 
 
-def gather_rows(piece):
-    if piece.ndim == 1:
-        return lax.all_gather(piece, "shard", axis=0, tiled=True)
-    rows = piece.shape[0] // lax.axis_size("replica")
-    own = lax.dynamic_slice_in_dim(piece, lax.axis_index("replica") * rows, rows)
-    return lax.all_gather(own, ("shard", "replica"), axis=0, tiled=True)
-
-
-def scatter_rows(term):
-    if term.ndim == 1:
-        return lax.psum(lax.psum_scatter(term, "shard", scatter_dimension=0, tiled=True), "replica")
-    low = term.astype(jnp.bfloat16)
-    part = lax.psum_scatter(low, ("shard", "replica"), scatter_dimension=0, tiled=True)
-    return lax.all_gather(part, "replica", axis=0, tiled=True).astype(jnp.float32)
+PARTS = 4
+
+
+def start_remote(source, target, send_sem, recv_sem, device):
+    pltpu.make_async_remote_copy(
+        src_ref=source,
+        dst_ref=target,
+        send_sem=send_sem,
+        recv_sem=recv_sem,
+        device_id=device,
+        device_id_type=pl.DeviceIdType.MESH,
+    ).start()
+
+
+def wait_bytes(ref, sem):
+    pltpu.make_async_copy(ref, ref, sem).wait()
+
+
+def greet(shards):
+    place = lax.axis_index("shard")
+    member = lax.axis_index("replica")
+    barrier = pltpu.get_barrier_semaphore()
+    pl.semaphore_signal(barrier, inc=1, device_id={"replica": member ^ 1}, device_id_type=pl.DeviceIdType.MESH)
+    pl.semaphore_signal(barrier, inc=1, device_id={"replica": member ^ 2}, device_id_type=pl.DeviceIdType.MESH)
+
+    @pl.when(place > 0)
+    def _():
+        pl.semaphore_signal(barrier, inc=1, device_id={"shard": place - 1}, device_id_type=pl.DeviceIdType.MESH)
+
+    @pl.when(place < shards - 1)
+    def _():
+        pl.semaphore_signal(barrier, inc=1, device_id={"shard": place + 1}, device_id_type=pl.DeviceIdType.MESH)
+
+    pl.semaphore_wait(barrier, 2 + (place > 0).astype(jnp.int32) + (place < shards - 1).astype(jnp.int32))
+
+
+def gather_kernel(shards, chunks, count, *refs):
+    pieces, wholes = refs[:count], refs[count : 2 * count]
+    held = refs[2 * count : 3 * count]
+    (local_sem, own_send, pass_send, line_recv, x_send, x_recv, core_send, core_recv) = refs[
+        3 * count :
+    ]
+    place = lax.axis_index("shard")
+    member = lax.axis_index("replica")
+    part = member % PARTS
+    greet(shards)
+
+    def loads(index):
+        return pltpu.make_async_copy(pieces[index], held[index], local_sem.at[index])
+
+    def stores(index):
+        rows = pieces[index].shape[0]
+        target = wholes[index].at[pl.ds(pl.multiple_of(place * rows, rows), rows), :]
+        return pltpu.make_async_copy(held[index], target, local_sem.at[index])
+
+    for index in range(count):
+        loads(index).start()
+
+    def window(chunk, block, whose):
+        index, first, length = chunk
+        rows = pieces[index].shape[0]
+        width = pieces[index].shape[1] // PARTS
+        return wholes[index].at[
+            pl.ds(pl.multiple_of(block * rows + first, length), length),
+            pl.ds(pl.multiple_of(whose * width, width), width),
+        ]
+
+    def own(j):
+        index, first, length = chunks[j]
+        width = pieces[index].shape[1] // PARTS
+        source = pieces[index].at[
+            pl.ds(first, length), pl.ds(pl.multiple_of(part * width, width), width)
+        ]
+        for slot, way in enumerate((1, -1)):
+            @pl.when((place + way >= 0) & (place + way < shards))
+            def _():
+                start_remote(
+                    source,
+                    window(chunks[j], place, part),
+                    own_send.at[j, slot],
+                    line_recv.at[j, place],
+                    {"shard": place + way},
+                )
+
+    def hop(j, k):
+        for way in (1, -1):
+            block = place - way * k
+
+            @pl.when((block >= 0) & (block < shards))
+            def _():
+                mine = window(chunks[j], block, part)
+                wait_bytes(mine, line_recv.at[j, block])
+
+                @pl.when((place + way >= 0) & (place + way < shards))
+                def _():
+                    start_remote(
+                        mine, mine, pass_send.at[j, block], line_recv.at[j, block], {"shard": place + way}
+                    )
+
+                start_remote(mine, mine, x_send.at[j, block], x_recv.at[j, block], {"replica": member ^ 2})
+                start_remote(
+                    mine, mine, core_send.at[j, block, 0], core_recv.at[j, block, 0], {"replica": member ^ 1}
+                )
+
+    def across(j, k):
+        for way in (1, -1):
+            block = place - way * k
+
+            @pl.when((block >= 0) & (block < shards))
+            def _():
+                theirs = window(chunks[j], block, part ^ 2)
+                wait_bytes(theirs, x_recv.at[j, block])
+                start_remote(
+                    theirs, theirs, core_send.at[j, block, 1], core_recv.at[j, block, 1], {"replica": member ^ 1}
+                )
+
+    total = len(chunks)
+    for step in range(total + shards + 1):
+        if step < total:
+            own(step)
+        if 1 <= step <= count:
+            loads(step - 1).wait()
+            stores(step - 1).start()
+        for k in range(1, shards):
+            if 0 <= step - k < total:
+                hop(step - k, k)
+        for k in range(1, shards):
+            if 0 <= step - k - 1 < total:
+                across(step - k - 1, k)
+
+    for j in range(total):
+        for slot, way in enumerate((1, -1)):
+            @pl.when((place + way >= 0) & (place + way < shards))
+            def _():
+                wait_bytes(window(chunks[j], place, part), own_send.at[j, slot])
+
+        for k in range(1, shards):
+            for way in (1, -1):
+                block = place - way * k
+
+                @pl.when((block >= 0) & (block < shards))
+                def _():
+                    mine = window(chunks[j], block, part)
+
+                    @pl.when((place + way >= 0) & (place + way < shards))
+                    def _():
+                        wait_bytes(mine, pass_send.at[j, block])
+
+                    wait_bytes(mine, x_send.at[j, block])
+                    for which in range(2):
+                        wait_bytes(mine, core_send.at[j, block, which])
+                        wait_bytes(mine, core_recv.at[j, block, which])
+    for index in range(count):
+        stores(index).wait()
+
+
+def gather_weights(pieces, shards, pace=192 * 1024):
+    chunks = []
+    for index, piece in enumerate(pieces):
+        rows, width = piece.shape
+        cuts = 1
+        while rows % (2 * cuts * 16) == 0 and rows // cuts * (width // PARTS) > pace:
+            cuts *= 2
+        for cut in range(cuts):
+            chunks.append((index, cut * (rows // cuts), rows // cuts))
+    count, total = len(pieces), len(chunks)
+    dma = pltpu.SemaphoreType.DMA
+    return pl.pallas_call(
+        functools.partial(gather_kernel, shards, tuple(chunks), count),
+        out_shape=[jax.ShapeDtypeStruct((shards * p.shape[0], p.shape[1]), p.dtype) for p in pieces],
+        in_specs=[pl.BlockSpec(memory_space=pl.ANY)] * count,
+        out_specs=[pl.BlockSpec(memory_space=pl.ANY)] * count,
+        scratch_shapes=[pltpu.VMEM(p.shape, p.dtype) for p in pieces]
+        + [
+            dma((count,)),
+            dma((total, 2)),
+            dma((total, shards)),
+            dma((total, shards)),
+            dma((total, shards)),
+            dma((total, shards)),
+            dma((total, shards, 2)),
+            dma((total, shards, 2)),
+        ],
+        compiler_params=pltpu.CompilerParams(collective_id=0, has_side_effects=True, vmem_limit_bytes=24 * 1024 * 1024),
+        name="gather_weights",
+    )(*pieces)
+
+
+LANES = 128
+
+
+def add_rows(target, left, right, rows):
+    step = next(size for size in (128, 64, 16) if rows % size == 0)
+
+    def body(i, carry):
+        window = pl.ds(pl.multiple_of(i * step, step), step)
+        target[window, :] = (
+            left[window, :].astype(jnp.float32) + right[window, :].astype(jnp.float32)
+        ).astype(target.dtype)
+        return carry
+
+    lax.fori_loop(0, rows // step, body, 0)
+
+
+def reduce_kernel(shards, plan, count, *refs):
+    leads, trails, heights, kinds = plan
+    chunks = leads + trails
+    total = len(chunks)
+    terms, refs = refs[:count], refs[count:]
+    sums, refs = refs[:count], refs[count:]
+    near, refs = refs[:count], refs[count:]
+    landed, refs = refs[:total], refs[total:]
+    passing, refs = refs[:total], refs[total:]
+    swapped, refs = refs[: len(trails)], refs[len(trails) :]
+    stages = []
+    for kind in range(len(kinds)):
+        stages.append(refs[:6])
+        refs = refs[6:]
+    trail_stage, refs = refs[:4], refs[4:]
+    (load_sem, core_send, core_recv, x_send, x_recv, line_send, line_recv) = refs[:7]
+    (end_local, end_x_send, end_x_recv, end_core_send, end_core_recv) = refs[7:]
+    place = lax.axis_index("shard")
+    member = lax.axis_index("replica")
+    core = member % 2
+    side = (member // 2) % 2
+    x_mate = {"replica": member ^ 2}
+    core_mate = {"replica": member ^ 1}
+    greet(shards)
+
+    def leading(j):
+        return j < len(leads)
+
+    def height(j):
+        return heights[chunks[j][0]]
+
+    def columns(j, whose):
+        index, first, width = chunks[j]
+        part = terms[index].shape[1] // PARTS
+        return pl.ds(pl.multiple_of(whose * part + first, LANES), width)
+
+    def send_near(j):
+        index = chunks[j][0]
+        for which in range(2):
+            start_remote(
+                terms[index].at[:, columns(j, (1 - core) * 2 + which)],
+                near[index].at[:, columns(j, which)],
+                core_send.at[j, which],
+                core_recv.at[j, which],
+                core_mate,
+            )
+
+    def staged(j):
+        if leading(j):
+            a0, a1, b0, b1, c, d = stages[kinds.index((height(j), chunks[j][2]))]
+            return (b0, b1, c, d) if j % 2 else (a0, a1, c, d)
+        return trail_stage
+
+    def load_copies(j):
+        index = chunks[j][0]
+        whose = (1 - side, side) if leading(j) else (0, 1)
+        at = staged(j)
+        sem = 0 if leading(j) else 4
+        sources = [terms[index].at[:, columns(j, core * 2 + w)] for w in whose]
+        sources += [near[index].at[:, columns(j, w)] for w in whose]
+        return [pltpu.make_async_copy(s, at[i], load_sem.at[sem + i]) for i, s in enumerate(sources)]
+
+    def load(j):
+        for which in range(2):
+            wait_bytes(near[chunks[j][0]].at[:, columns(j, which)], core_recv.at[j, which])
+        for copy in load_copies(j):
+            copy.start()
+
+    def near_sum(j):
+        size = shards * height(j)
+        at = staged(j)
+        for copy in load_copies(j):
+            copy.wait()
+        if leading(j):
+            add_rows(at[0], at[0], at[2], size)
+            start_remote(at[0], landed[j], x_send.at[j], x_recv.at[j], x_mate)
+            add_rows(at[1], at[1], at[3], size)
+        else:
+            width = chunks[j][2]
+            for which in range(2):
+                window = landed[j].at[:, pl.ds(which * width, width)]
+                add_rows(window, at[which], at[2 + which], size)
+
+    def x_sum(j):
+        at = staged(j)
+        wait_bytes(at[0], x_send.at[j])
+        wait_bytes(landed[j], x_recv.at[j])
+        add_rows(landed[j], landed[j], at[1], shards * height(j))
+
+    def block(j, t):
+        rows = height(j)
+        return landed[j].at[pl.ds(pl.multiple_of(t * rows, rows), rows), :]
+
+    def inside(t):
+        return (t >= 0) & (t < shards)
+
+    def line(j, hop):
+        for slot, way in enumerate((1, -1)):
+            t = place + way * (shards - hop)
+            target = passing[j].at[slot, hop - 1]
+            sems = (line_send.at[j, slot, hop - 1], line_recv.at[j, slot, hop - 1])
+            ahead = {"shard": place + way}
+            own = block(j, jnp.clip(t, 0, shards - 1))
+            if hop == 1:
+
+                @pl.when(inside(t))
+                def _():
+                    start_remote(own, target, *sems, ahead)
+            else:
+                arrived = passing[j].at[slot, hop - 2]
+
+                @pl.when(inside(t) & inside(place - way))
+                def _():
+                    wait_bytes(arrived, line_recv.at[j, slot, hop - 2])
+                    add_rows(arrived, arrived, own, height(j))
+                    start_remote(arrived, target, *sems, ahead)
+
+                @pl.when(inside(t) & jnp.logical_not(inside(place - way)))
+                def _():
+                    start_remote(own, target, *sems, ahead)
+
+    def sum_window(j, whose):
+        return sums[chunks[j][0]].at[:, columns(j, whose)]
+
+    def share(j):
+        width = chunks[j][2]
+        for which in range(1 if leading(j) else 2):
+            rows = block(j, place).at[:, pl.ds(which * width, width)]
+            target = sum_window(j, core * 2 + (side if leading(j) else which))
+            pltpu.make_async_copy(rows, target, end_local.at[j, which]).start()
+            start_remote(rows, target, end_core_send.at[j, which], end_core_recv.at[j, which], core_mate)
+
+    def line_end(j):
+        mine = block(j, place)
+        for slot, way in enumerate((1, -1)):
+
+            @pl.when(inside(place - way))
+            def _():
+                arrived = passing[j].at[slot, shards - 2]
+                wait_bytes(arrived, line_recv.at[j, slot, shards - 2])
+                add_rows(mine, mine, arrived, height(j))
+
+        target = sum_window(j, core * 2 + side) if leading(j) else swapped[j - len(leads)]
+        start_remote(mine, target, end_x_send.at[j], end_x_recv.at[j], x_mate)
+        if leading(j):
+            share(j)
+
+    def finish(j):
+        if leading(j):
+            theirs = sum_window(j, core * 2 + (1 - side))
+            wait_bytes(theirs, end_x_recv.at[j])
+            start_remote(theirs, theirs, end_core_send.at[j, 1], end_core_recv.at[j, 1], core_mate)
+        else:
+            mine, other = block(j, place), swapped[j - len(leads)]
+            wait_bytes(mine, end_x_send.at[j])
+            wait_bytes(other, end_x_recv.at[j])
+            add_rows(mine, mine, other, height(j))
+            share(j)
+
+    first, second = len(leads), len(trails)
+    for j in range(max(first, second)):
+        if j < first:
+            send_near(j)
+        if j < second:
+            send_near(first + j)
+    load(0)
+    load(first)
+    for step in range(max(first + shards + 2, second + shards + 1)):
+        if step < first:
+            near_sum(step)
+        if step < second:
+            near_sum(first + step)
+            if step + 1 < second:
+                load(first + step + 1)
+            line(first + step, 1)
+        for hop in range(2, shards):
+            if 0 <= step - hop < first:
+                line(step - hop, hop)
+            if 0 <= step - hop + 1 < second:
+                line(first + step - hop + 1, hop)
+        if 0 <= step - shards < first:
+            line_end(step - shards)
+        if 0 <= step - shards + 1 < second:
+            line_end(first + step - shards + 1)
+        if 0 <= step - shards - 1 < first:
+            finish(step - shards - 1)
+        if 0 <= step - shards < second:
+            finish(first + step - shards)
+        if 1 <= step <= first:
+            x_sum(step - 1)
+            line(step - 1, 1)
+        if step + 1 < first:
+            load(step + 1)
+
+    for j in range(total):
+        for which in range(2):
+            wait_bytes(near[chunks[j][0]].at[:, columns(j, which)], core_send.at[j, which])
+        for slot, way in enumerate((1, -1)):
+            for hop in range(1, shards):
+
+                @pl.when(inside(place + way * (shards - hop)))
+                def _():
+                    wait_bytes(passing[j].at[slot, hop - 1], line_send.at[j, slot, hop - 1])
+
+        if leading(j):
+            wait_bytes(sum_window(j, 0), end_x_send.at[j])
+        for which in range(2):
+            if which == 0 or not leading(j):
+                wait_bytes(sum_window(j, 0), end_local.at[j, which])
+            wait_bytes(sum_window(j, 0), end_core_send.at[j, which])
+            wait_bytes(sum_window(j, 0), end_core_recv.at[j, which])
+
+
+def reduce_terms(leading, trailing, shards, lead_cells=1536 * 256):
+    terms = list(leading) + list(trailing)
+    count = len(terms)
+    heights = tuple(t.shape[0] // shards for t in terms)
+    leads, trails = [], []
+    for index, term in enumerate(terms):
+        part = term.shape[1] // PARTS
+        if index < len(leading):
+            width = part
+            while width % (2 * LANES) == 0 and width * term.shape[0] > lead_cells:
+                width //= 2
+            if width * term.shape[0] > lead_cells and width % LANES == 0:
+                width = LANES
+            leads += [(index, first, width) for first in range(0, part, width)]
+        else:
+            trails += [(index, first, LANES) for first in range(0, part, LANES)]
+    kinds = []
+    for index, first, width in leads:
+        if (heights[index], width) not in kinds:
+            kinds.append((heights[index], width))
+    chunks = leads + trails
+    total = len(chunks)
+    bf16, dma = jnp.bfloat16, pltpu.SemaphoreType.DMA
+
+    def rows_and_width(j):
+        index, first, width = chunks[j]
+        return heights[index], width if j < len(leads) else 2 * width
+
+    scratch = []
+    for j in range(total):
+        rows, width = rows_and_width(j)
+        scratch.append(pltpu.VMEM((shards * rows, width), bf16))
+    for j in range(total):
+        rows, width = rows_and_width(j)
+        scratch.append(pltpu.VMEM((2, shards - 1, rows, width), bf16))
+    for j in range(len(leads), total):
+        rows, width = rows_and_width(j)
+        scratch.append(pltpu.VMEM((rows, width), bf16))
+    for rows, width in kinds:
+        scratch += [pltpu.VMEM((shards * rows, width), bf16)] * 6
+    scratch += [pltpu.VMEM((shards * heights[-1], LANES), bf16)] * 4
+    scratch += [
+        dma((8,)),
+        dma((total, 2)),
+        dma((total, 2)),
+        dma((total,)),
+        dma((total,)),
+        dma((total, 2, shards - 1)),
+        dma((total, 2, shards - 1)),
+        dma((total, 2)),
+        dma((total,)),
+        dma((total,)),
+        dma((total, 2)),
+        dma((total, 2)),
+    ]
+    outs = pl.pallas_call(
+        functools.partial(reduce_kernel, shards, (tuple(leads), tuple(trails), heights, tuple(kinds)), count),
+        out_shape=[jax.ShapeDtypeStruct((t.shape[0] // shards, t.shape[1]), bf16) for t in terms]
+        + [jax.ShapeDtypeStruct((t.shape[0], t.shape[1] // 2), bf16) for t in terms],
+        in_specs=[pl.BlockSpec(memory_space=pl.ANY)] * count,
+        out_specs=[pl.BlockSpec(memory_space=pl.ANY)] * (2 * count),
+        scratch_shapes=scratch,
+        compiler_params=pltpu.CompilerParams(
+            collective_id=1, has_side_effects=True, vmem_limit_bytes=62 * 1024 * 1024
+        ),
+        name="reduce_terms",
+    )(*terms)
+    return outs[:count]
+
+
+def swap(x, bit):
+    members = lax.axis_size("replica")
+    return lax.ppermute(x, "replica", [(r, r ^ (1 << bit)) for r in range(members)])
+
+
+def gain_width(rows):
+    return -(-2 * rows // (PARTS * LANES)) * PARTS * LANES
 
 
 def gather_layer(pieces):
-    return tuple(gather_rows(piece) for piece in pieces)
+    norm_attn, w_query, w_key, w_value, w_out, norm_ffn, w_gate, w_up, w_down = pieces
+    rows = norm_attn.shape[0]
+    gains = jnp.concatenate([norm_attn, norm_ffn])
+    gains = jnp.pad(gains[None], ((0, 15), (0, gain_width(rows) - 2 * rows)))
+    w_qkv = jnp.concatenate([w_query, w_key, w_value], axis=1)
+    shards = lax.axis_size("shard")
+    w_qkv, w_out, w_gate, w_up, w_down, gains = gather_weights(
+        [w_qkv, w_out, w_gate, w_up, w_down, gains], shards
+    )
+    gains = gains.reshape(shards, 16, -1)[:, 0]
+    norm_attn = gains[:, :rows].reshape(-1)
+    norm_ffn = gains[:, rows : 2 * rows].reshape(-1)
+    return norm_attn, w_qkv, w_out, norm_ffn, w_gate, w_up, w_down
 
 
 def forward_layer(inputs, weights, segment, row_start):
-    norm_attn, w_query, w_key, w_value, w_out, norm_ffn, w_gate, w_up, w_down = weights
+    norm_attn, w_qkv, w_out, norm_ffn, w_gate, w_up, w_down = weights
     row_count = inputs.shape[0]
     seq_length = segment.shape[0]
     groups = QH // KVH
@@ -68,19 +564,19 @@
     recip_one = lax.rsqrt(jnp.mean(inputs * inputs, axis=-1, keepdims=True) + EPSILON)
     scaled = inputs * recip_one
     normed = (scaled * norm_attn.astype(jnp.float32)).astype(jnp.bfloat16)
-    raw_query = jnp.dot(normed, w_query, preferred_element_type=jnp.float32).reshape(
-        row_count, KVH, groups, HD
-    )
+    raw = jnp.dot(normed, w_qkv, preferred_element_type=jnp.float32)
+    raw_query, raw_key, raw_value = jnp.split(raw, [QH * HD, (QH + KVH) * HD], axis=1)
+    raw_query = raw_query.reshape(row_count, KVH, groups, HD)
     queries = rotate(raw_query, cosine_table[:, :, None, :], sine_table[:, :, None, :], 1.0).astype(
         jnp.bfloat16
     )
-    raw_key = jnp.dot(normed, w_key, preferred_element_type=jnp.float32).reshape(row_count, KVH, HD)
+    raw_key = raw_key.reshape(row_count, KVH, HD)
     key_rows = (
         rotate(raw_key, cosine_table, sine_table, 1.0)
         .astype(jnp.bfloat16)
         .reshape(row_count, KVH * HD)
     )
-    value_rows = jnp.dot(normed, w_value, preferred_element_type=jnp.float32).astype(jnp.bfloat16)
+    value_rows = raw_value.astype(jnp.bfloat16)
     all_keys, all_values = (
         lax.all_gather(key_rows, "shard", axis=0, tiled=True),
         lax.all_gather(value_rows, "shard", axis=0, tiled=True),
@@ -138,7 +634,7 @@
 
 
 def backward_layer(grad_result, weights, saved):
-    norm_attn, w_query, w_key, w_value, w_out, norm_ffn, w_gate, w_up, w_down = weights
+    norm_attn, w_qkv, w_out, norm_ffn, w_gate, w_up, w_down = weights
     (
         scaled,
         recip_one,
@@ -222,13 +718,8 @@
     key_low = rotate(grad_keys.reshape(row_count, KVH, HD), cosine_table, sine_table, -1.0)
     key_low = key_low.reshape(row_count, KVH * HD).astype(jnp.bfloat16)
     value_low = grad_values.astype(jnp.bfloat16)
-    grad_normed = jnp.einsum("tq,dq->td", query_low, w_query, preferred_element_type=jnp.float32)
-    grad_normed = grad_normed + jnp.einsum(
-        "tq,dq->td", key_low, w_key, preferred_element_type=jnp.float32
-    )
-    grad_normed = grad_normed + jnp.einsum(
-        "tq,dq->td", value_low, w_value, preferred_element_type=jnp.float32
-    )
+    qkv_low = jnp.concatenate([query_low, key_low, value_low], axis=1)
+    grad_normed = jnp.einsum("tq,dq->td", qkv_low, w_qkv, preferred_element_type=jnp.float32)
     grad_norm_attn = jnp.sum(grad_normed * scaled, axis=0)
     grad_scaled = grad_normed * norm_attn.astype(jnp.float32)
     grad_inputs = grad_middle + recip_one * (
@@ -236,9 +727,7 @@
     )
     operands = (
         normed,
-        query_low,
-        key_low,
-        value_low,
+        qkv_low,
         attended,
         attn_grad,
         normed_mid,
@@ -254,12 +743,10 @@
     return jnp.einsum("td,tq->dq", left, right, preferred_element_type=jnp.float32)
 
 
-def weight_terms(gains, operands):
+def reduce_gradients(operand_pairs, gains):
     (
         normed,
-        query_low,
-        key_low,
-        value_low,
+        qkv_low,
         attended,
         attn_grad,
         normed_mid,
@@ -267,17 +754,40 @@
         up_low,
         hidden,
         branch_grad,
-    ) = operands
+    ) = zip(*operand_pairs)
+    shards = lax.axis_size("shard")
+    rows = gains[0].shape[0] // shards
+
+    def product(lefts, rights):
+        return sum(row_product(left, right) for left, right in zip(lefts, rights)).astype(
+            jnp.bfloat16
+        )
+
+    gain_term = jnp.stack([gain.reshape(shards, rows) for gain in gains], axis=1)
+    gain_term = gain_term.reshape(shards, 1, 2 * rows).astype(jnp.bfloat16)
+    gain_term = jnp.pad(gain_term, ((0, 0), (0, 15), (0, gain_width(rows) - 2 * rows)))
+    leading = [
+        product(hidden, branch_grad),
+        product(normed_mid, gate_low),
+        product(normed_mid, up_low),
+        gain_term.reshape(shards * 16, -1),
+    ]
+    trailing = [product(normed, qkv_low), product(attended, attn_grad)]
+    totals = [total.astype(jnp.float32) for total in reduce_terms(leading, trailing, shards)]
+    members = lax.axis_size("replica")
+    for bit in range(PARTS.bit_length() - 1, members.bit_length() - 1):
+        totals = [total + swap(total, bit) for total in totals]
+    down, gate, up, own_gains, qkv, out = totals
     return (
-        gains[0],
-        row_product(normed, query_low),
-        row_product(normed, key_low),
-        row_product(normed, value_low),
-        row_product(attended, attn_grad),
-        gains[1],
-        row_product(normed_mid, gate_low),
-        row_product(normed_mid, up_low),
-        row_product(hidden, branch_grad),
+        own_gains[0, :rows],
+        qkv[:, : QH * HD],
+        qkv[:, QH * HD : (QH + KVH) * HD],
+        qkv[:, (QH + KVH) * HD :],
+        out,
+        own_gains[0, rows : 2 * rows],
+        gate,
+        up,
+        down,
     )
 
 
@@ -346,25 +856,27 @@
         incoming = jnp.where(first_section, returning.astype(jnp.float32), later_grad)
         active = jnp.where(first_section, tick_index >= 1, tick_index < micro_count)
         incoming = jnp.where(active, incoming, 0.0)
-        saved = jax.tree.map(
-            lambda early_value, late_value: jnp.where(first_section, early_value, late_value),
-            saved_ticks[max(tick_index - 1, 0)],
-            saved_ticks[min(tick_index + 1, micro_count)],
-        )
+        if 0 < tick_index < micro_count:
+            saved = jax.tree.map(
+                lambda early_value, late_value: jnp.where(first_section, early_value, late_value),
+                saved_ticks[tick_index - 1],
+                saved_ticks[tick_index + 1],
+            )
+        else:
+            saved = saved_ticks[1 if tick_index == 0 else micro_count - 1]
         grad_inputs, gains, operands = backward_layer(incoming, weights, saved)
         flow_ticks.append(grad_inputs)
         if tick_index < micro_count:
             returning = from_behind(grad_inputs.astype(jnp.bfloat16), "section", -1)
         gain_sums = add_terms(gain_sums, gains)
         operand_ticks.append(operands)
-    joined = tuple(
-        (
-            jnp.concatenate([tick_ops[index_op] for tick_ops in operand_ticks], axis=0)
-            for index_op in range(len(operand_ticks[0]))
-        )
-    )
-    full_terms = weight_terms(gain_sums, joined)
-    totals = tuple(scatter_rows(term) for term in full_terms)
+    first_ops, last_ops = operand_ticks[0], operand_ticks[micro_count]
+    edge_ops = jax.tree.map(
+        lambda early_value, late_value: jnp.where(first_section, late_value, early_value),
+        first_ops,
+        last_ops,
+    )
+    totals = reduce_gradients(operand_ticks[1:micro_count] + [edge_ops], gain_sums)
     section_outputs = jnp.stack(
         [
             jnp.where(first_section, result_ticks[index_micro], result_ticks[index_micro + 1])

time: 2170 us -> 1500 us (0.69)
  waiting for transfers between devices: 1360 us -> 214 us
  Pallas kernels: 0 us -> 540 us
  blocking collectives: 60.8 us -> 0 us
    reduce_scatter x7 -> x0, waiting for transfers between devices: 601 us -> none  [scatter_rows(): lax.psum_scatter(low, ('shard', 'replica'), scatter_dimension=0, tiled=True)]
    pallas_call x0 -> x2, Pallas kernels: none -> 540 us  [the longest x1 314 us: reduce_terms(): pl.pallas_call(functools.partial(reduce_kernel, shards, (tuple(leads), tu...]
    all_gather x12 -> x0, waiting for transfers between devices: 530 us -> none  [the longest x7 430 us: gather_rows(): return lax.all_gather(own, ('shard', 'replica'), axis=0, tiled=True)]
    dot_general x7 -> x10, matrix products: 68.7 us -> 111 us  [row_product(): jnp.einsum('td,tq->dq', left, right, preferred_element_type=jnp.float32)]
    all_gather x4 -> x0, blocking collectives: 39.5 us -> none  [the longest x2 20.4 us: scatter_rows(): lax.all_gather(part, 'replica', axis=0, tiled=True).astype(jnp.float32)]
    split x0 -> x15, local copies, waits for them, and re-layouts: none -> 30.4 us  [forward_layer(): jnp.split(raw, [QH * HD, (QH + KVH) * HD], axis=1)]
    dot_general x18 -> x6, matrix products: 63.3 us -> 37.2 us  [the longest x3 25.3 us: backward_layer(): jnp.einsum('tq,dq->td', qkv_low, w_qkv, preferred_element_type=jnp.float32)]
    dot_general x3 -> x1, matrix products: 39.1 us -> 13.1 us  [backward_layer(): jnp.einsum('ihgd,jhd->hgij', queries, all_keys, preferred_element_type=jn...]
  transfers between devices with their start and end apart: 35 -> 16, of which waited for: 33 -> 13; matrix products, arithmetic and copies ran while one was open for 17% -> 19% of each run, Pallas kernels for 0% -> 0%
where the time goes in v2:
time: 1500 us; the launch traced here: 1480 us
  Pallas kernels  540 us (36%)
  matrix products  496 us (33%)
  waiting for transfers between devices  214 us (14%)
  other arithmetic  129 us (9%)
  local copies, waits for them, and re-layouts  78.5 us (5%)
  between operations  16.5 us (1%)
    pallas_call x1, Pallas kernels, reduce_terms(): pl.pallas_call(functools.partial(reduce_kernel, shards, (tuple(leads), tu...  314 us
    pallas_call x1, Pallas kernels, gather_weights(): pl.pallas_call(functools.partial(gather_kernel, shards, tuple(chunks), co...  226 us
    dot_general x10, matrix products, row_product(): jnp.einsum('td,tq->dq', left, right, preferred_element_type=jnp.float32)  111 us
    all_gather x3, waiting for transfers between devices, forward_layer(): lax.all_gather(key_rows, 'shard', axis=0, tiled=True)  72.9 us
    all_gather x3, waiting for transfers between devices, forward_layer(): lax.all_gather(value_rows, 'shard', axis=0, tiled=True)  58.6 us
    reduce_scatter x3, waiting for transfers between devices, backward_layer(): lax.psum_scatter(value_terms.astype(jnp.bfloat16), 'shard', scatter_dimen...  48.7 us
    dot_general x3, matrix products, backward_layer(): jnp.einsum('ihgd,jhd->hgij', grad_attended, all_values, preferred_element...  40.3 us
    dot_general x3, matrix products, backward_layer(): jnp.einsum('td,fd->tf', branch_grad, w_down, preferred_element_type=jnp.f...  36.2 us
  transfers between devices with their start and end apart: 16, of which 13 were waited for; matrix products, arithmetic and copies ran while one was open for 19% of the time, Pallas kernels for 0%

profile of v2, /device:TPU:13, one launch (start us, length us, event | category | flops | bytes accessed | tf_op | source)
XLA Modules:
  0.0 1484.1 jit_solution(6412530443572851030)
XLA Ops:
  15.4 225.6 %gather_weights.1 = (bf16[1536,3072]{1,0:T(8,128)(2,1)S(1)}, bf16[1536,1536]{1,0:T(8,128)(2,1)S(1)}, bf16[1536,4096]{1,0:T(8,128)(2,1)}, bf16[1536,4096]{1,0:T(8...) custom-call(bf16[384,3072]{1,0:T(8,128)(2,1)S(1)} %pad_maximum_fusion.refs_0_, ...), custom_call_target="tpu_custom_call" | custom-call | tf_op jit(solution)/shard_map/gather_weights/pallas_call | solution.py:205
  270.9 26.1 %all-gather.9.cloned.1.call-done = bf16[1024,768]{0,1:T(8,128)(2,1)} async-done(((bf16[256,768]{0,1:T(8,128)(2,1)}), bf16[1024,768]{0,1:T(8,128)(2,1)}) %all-gather.9.cloned.1.call-update) | async-done | bytes 1572880 | tf_op jit(solution)/shard_map/all_gather | solution.py:581
  297.1 8.9 fusion.14
  306.0 9.5 fusion.11
  315.5 20.1 %all-gather.7.cloned.1.call-done = bf16[1024,768]{1,0:T(8,128)(2,1)} async-done(((bf16[256,768]{1,0:T(8,128)(2,1)}), bf16[1024,768]{1,0:T(8,128)(2,1)}) %all-gather.7.cloned.1.call-update) | async-done | bytes 1572880 | tf_op jit(solution)/shard_map/all_gather | solution.py:582
  348.7 10.9 fusion.132
  376.1 18.7 %collective-permute-done = bf16[256,1536]{1,0:T(8,128)(2,1)S(1)} collective-permute-done((bf16[256,1536]{1,0:T(8,128)(2,1)S(1)}, bf16[256,1536]{1,0:T(8,128)(2,1)S(1)}, u32[]{:S(2)}, u32[]{:S(2)}) %collective-permute-start) | collective-permute-done | bytes 786464 | tf_op jit(solution)/shard_map/ppermute | solution.py:22
  415.1 26.8 %all-gather.13.cloned.1.call-done = bf16[1024,768]{0,1:T(8,128)(2,1)} async-done(((bf16[256,768]{0,1:T(8,128)(2,1)}), bf16[1024,768]{0,1:T(8,128)(2,1)}) %all-gather.13.cloned.1.call-update) | async-done | bytes 1572880 | tf_op jit(solution)/shard_map/all_gather | solution.py:581
  442.0 9.9 fusion.16
  451.9 9.4 fusion.12
  461.3 19.1 %all-gather.11.cloned.1.call-done = bf16[1024,768]{1,0:T(8,128)(2,1)} async-done(((bf16[256,768]{1,0:T(8,128)(2,1)}), bf16[1024,768]{1,0:T(8,128)(2,1)}) %all-gather.11.cloned.1.call-update) | async-done | bytes 1572880 | tf_op jit(solution)/shard_map/all_gather | solution.py:582
  493.7 10.5 fusion.133
  509.5 10.8 multiply_convert_fusion.4
  520.3 10.5 fusion.137
  530.9 10.5 multiply_reduce_fusion.2
  547.9 14.9 %fusion.8 = (f32[8,2,256]{2,1,0:T(2,128)S(1)}, f32[8,1024,256,2]{2,1,3,0:T(8,128)}) fusion(f32[8,2,256]{2,1,0:T(2,128)S(1)} %bitcast.513, f32[8,1024,256,2]{2,1,3,0:T(8,128)} %get-tuple-element.142, pred[256,1024]{0,1:T(8,128)(4,1)} %copy-done.23, bf16[1024,8,96,1]{0,2,3,1:T(8,128)(2,1)} %bitcast.464, bf16[256,8,2,96]{0,3,2,1:T(8,128)(2,1)} %bitcast.496), kind=kOutput, calls=%fused_computation.19 | convolution fusion | flops 826273792 | bytes 36208640 | tf_op jit(solution)/shard_map/ihgd,jhd->hgij/dot_general | solution.py:687
  565.1 11.7 fusion.10
  584.2 9.3 bitcast_convert_fusion.5
  593.6 9.7 fusion.32
  623.8 31.0 %reduce-scatter.9.cloned.1.call-done = bf16[256,768]{0,1:T(8,128)(2,1)} async-done(((bf16[1024,768]{0,1:T(8,128)(2,1)}), bf16[256,768]{0,1:T(8,128)(2,1)}) %reduce-scatter.9.cloned.1.call-update) | async-done | bytes 393232 | tf_op jit(solution)/shard_map/reduce_scatter | solution.py:712
  654.8 9.2 multiply_reduce_fusion.5
  692.6 19.9 %all-gather.17.cloned.1.call-done = bf16[1024,768]{0,1:T(8,128)(2,1)} async-done(((bf16[256,768]{0,1:T(8,128)(2,1)}), bf16[1024,768]{0,1:T(8,128)(2,1)}) %all-gather.17.cloned.1.call-update) | async-done | bytes 1572880 | tf_op jit(solution)/shard_map/all_gather | solution.py:581
  712.5 9.1 fusion.15
  721.6 9.5 fusion.13
  731.1 19.4 %all-gather.15.cloned.1.call-done = bf16[1024,768]{1,0:T(8,128)(2,1)} async-done(((bf16[256,768]{1,0:T(8,128)(2,1)}), bf16[1024,768]{1,0:T(8,128)(2,1)}) %all-gather.15.cloned.1.call-update) | async-done | bytes 1572880 | tf_op jit(solution)/shard_map/all_gather | solution.py:582
  777.4 12.3 multiply_convert_fusion.2
  789.6 9.9 fusion.138
  799.6 12.7 multiply_reduce_fusion.1
  820.0 9.8 fusion.49
  829.8 13.1 fusion.3
  842.9 11.5 fusion.5
  862.8 9.4 fusion.35
  880.7 9.7 bitcast_convert_fusion.4
  893.2 10.6 fusion.95
  903.8 10.4 fusion.94
  915.5 15.8 %reduce-scatter.13.cloned.1.call-done = bf16[256,768]{0,1:T(8,128)(2,1)} async-done(((bf16[1024,768]{0,1:T(8,128)(2,1)}), bf16[256,768]{0,1:T(8,128)(2,1)}) %reduce-scatter.13.cloned.1.call-update) | async-done | bytes 393232 | tf_op jit(solution)/shard_map/reduce_scatter | solution.py:712
  945.0 10.5 fusion.74
  960.3 13.0 multiply_convert_fusion
  981.0 10.9 multiply_reduce_fusion
  996.9 15.7 %fusion = (f32[8,2,256]{2,1,0:T(2,128)}, f32[8,1024,256,2]{2,1,3,0:T(8,128)}) fusion(f32[8,2,256]{2,1,0:T(2,128)} %bitcast.516, f32[8,1024,256,2]{2,1,3,0:T(8,128)} %get-tuple-element.142, pred[256,1024]{0,1:T(8,128)(4,1)S(1)} %copy-done.25, bf16[1024,8,96,1]{0,2,3,1:T(8,128)(2,1)} %bitcast.465, bf16[256,8,2,96]{0,3,2,1:T(8,128)(2,1)S(1)} %bitcast.494), kind=kOutput, calls=%fused_computation.6 | convolution fusion | flops 826273792 | bytes 36208640 | tf_op jit(solution)/shard_map/ihgd,jhd->hgij/dot_general | solution.py:687
  1014.0 11.4 fusion.2
  1041.1 15.6 %add_convert_fusion.1.refs_1_ = bf16[1536,4096]{1,0:T(8,128)(2,1)} fusion(f32[1536,4096]{1,0:T(8,128)} %fusion.95, bf16[256,1536]{1,0:T(8,128)(2,1)S(1)} %copy-done.37, bf16[256,4096]{1,0:T(8,128)(2,1)} %copy-done.88, bf16[256,4096]{1,0:T(8,128)(2,1)} %get-tuple-element.81, pred[]{:T(512)S(6)} %eq.48), kind=kOutput, calls=%fused_computation.1 | convolution fusion | flops 3234856960 | bytes 42729472 | tf_op jit(solution)/shard_map/td,tq->dq/dot_general | solution.py:743
  1056.8 9.3 bitcast_convert_fusion.3
  1066.1 15.5 %add_convert_fusion.refs_2_ = bf16[1536,4096]{1,0:T(8,128)(2,1)} fusion(f32[1536,4096]{1,0:T(8,128)} %fusion.94, bf16[256,1536]{1,0:T(8,128)(2,1)S(1)} %copy-done.37, bf16[256,4096]{1,0:T(8,128)(2,1)} %get-tuple-element.78, bf16[256,4096]{1,0:T(8,128)(2,1)} %copy-done.85, pred[]{:T(512)S(6)} %eq.48), kind=kOutput, calls=%fused_computation | convolution fusion | flops 3234856960 | bytes 42729472 | tf_op jit(solution)/shard_map/td,tq->dq/dot_general | solution.py:743
  1083.9 12.5 fusion.76
  1100.1 16.1 %add_convert_fusion.2.refs_0_ = bf16[4096,1536]{1,0:T(8,128)(2,1)} fusion(f32[4096,1536]{1,0:T(8,128)} %fusion.76, bf16[256,4096]{1,0:T(8,128)(2,1)} %copy-done.65, bf16[256,4096]{1,0:T(8,128)(2,1)} %get-tuple-element.77, pred[]{:T(512)S(6)} %eq.48, bf16[256,1536]{1,0:T(8,128)(2,1)} %collective-permute-done.2, bf16[2,1,256,1536]{3,2,1,0:T(8,128)(2,1)S(1)} %copy-done.40), kind=kOutput, calls=%fused_computation.2 | convolution fusion | flops 3236429824 | bytes 43516928 | tf_op jit(solution)/shard_map/td,tq->dq/dot_general | solution.py:743
  1128.4 11.1 add_convert_fusion.3.refs_4_
  1139.5 314.3 %reduce_terms.1 = (bf16[1024,1536]{1,0:T(8,128)(2,1)}, bf16[384,4096]{1,0:T(8,128)(2,1)}, bf16[384,4096]{1,0:T(8,128)(2,1)}, bf16[16,1024]{1,0:T(8,128)(2,1)}, b...) custom-call(bf16[4096,1536]{1,0:T(8,128)(2,1)} %add_convert_fusion.2, ...), custom_call_target="tpu_custom_call" | custom-call | tf_op jit(solution)/shard_map/reduce_terms/pallas_call | solution.py:510
  (538 shorter events, 315.3 us)
Async XLA Ops:
  7.2 289.9 %all-gather.9.cloned.1.call-start = ((), (), s32[]{:S(2)}) async-start(), calls=%async_computation.7 | async-start | bytes 1966080 | tf_op jit(solution)/shard_map/all_gather | solution.py:581
  15.4 231.4 %copy-start.8 = (bf16[2,1,256,1536]{3,2,1,0:T(8,128)(2,1)S(1)}, bf16[2,1,256,1536]{3,2,1,0:T(8,128)(2,1)}, u32[]{:S(2)}) copy-start(bf16[2,1,256,1536]{3,2,1,0:T(8,128)(2,1)} %param.12) | copy-start | bytes 4718596
  15.4 231.7 %copy-start.130 = (s32[2,1,1024]{2,1,0:T(1,128)S(1)}, s32[2,1,1024]{2,1,0:T(1,128)}, u32[]{:S(2)}) copy-start(s32[2,1,1024]{2,1,0:T(1,128)} %param.13) | copy-start | bytes 24580
  246.8 148.3 %copy-start.98 = (f32[1536]{0:T(1024)}, f32[1536]{0:T(1024)S(1)}, u32[]{:S(2)}) copy-start(f32[1536]{0:T(1024)S(1)} %reshape.821) | copy-start | bytes 18436
  258.5 360.4 %copy-start.79 = (f32[256,48]{0,1:T(8,128)}, f32[256,48]{0,1:T(8,128)S(1)}, u32[]{:S(2)}) copy-start(f32[256,48]{0,1:T(8,128)S(1)} %get-tuple-element.133) | copy-start | bytes 147460
  259.4 76.2 %all-gather.7.cloned.1.call-start = ((), (), s32[]{:S(2)}) async-start(), calls=%async_computation.6 | async-start | bytes 1966080 | tf_op jit(solution)/shard_map/all_gather | solution.py:582
  261.4 180.6 %all-gather.13.cloned.1.call-start = ((), (), s32[]{:S(2)}) async-start(), calls=%async_computation.9 | async-start | bytes 1966080 | tf_op jit(solution)/shard_map/all_gather | solution.py:581
  268.9 37.0 %copy-start.47 = (bf16[256,8,2,48]{0,3,2,1:T(8,128)(2,1)}, bf16[256,8,2,48]{0,3,2,1:T(8,128)(2,1)S(1)}, u32[]{:S(2)}) copy-start(bf16[256,8,2,48]{0,3,2,1:T(8,128)(2,1)S(1)} %get-tuple-element.95) | copy-start | bytes 1179652
  268.9 37.0 %copy-start.49 = (bf16[256,8,2,48]{0,3,2,1:T(8,128)(2,1)}, bf16[256,8,2,48]{0,3,2,1:T(8,128)(2,1)S(1)}, u32[]{:S(2)}) copy-start(bf16[256,8,2,48]{0,3,2,1:T(8,128)(2,1)S(1)} %get-tuple-element.96) | copy-start | bytes 1179652
  270.9 212.4 %copy-start.23 = (pred[256,1024]{0,1:T(8,128)(4,1)}, pred[256,1024]{0,1:T(8,128)(4,1)S(1)}, u32[]{:S(2)}) copy-start(pred[256,1024]{0,1:T(8,128)(4,1)S(1)} %get-tuple-element.129) | copy-start | bytes 786436
  305.9 32.3 %copy-start.108 = (f32[8,2,256]{2,1,0:T(2,128)}, f32[8,2,256]{2,1,0:T(2,128)S(1)}, u32[]{:S(2)}) copy-start(f32[8,2,256]{2,1,0:T(2,128)S(1)} %get-tuple-element.135) | copy-start | bytes 49156
  315.5 31.3 %copy-start.110 = (f32[8,2,256]{2,1,0:T(2,128)}, f32[8,2,256]{2,1,0:T(2,128)S(1)}, u32[]{:S(2)}) copy-start(f32[8,2,256]{2,1,0:T(2,128)S(1)} %fusion.11) | copy-start | bytes 49156
  348.4 18.8 %copy-start.60 = (f32[256,1536]{1,0:T(8,128)}, f32[256,1536]{1,0:T(8,128)S(1)}, u32[]{:S(2)}) copy-start(f32[256,1536]{1,0:T(8,128)S(1)} %get-tuple-element.138) | copy-start | bytes 4718596
  359.6 35.5 %slice-start.10 = ((s8[9437184]{0:T(1024)(128)(4,1)}), s8[4194304]{0:T(1024)(128)(4,1)S(1)}, s32[]{:S(2)}) async-start(s8[9437184]{0:T(1024)(128)(4,1)} %bitcast.444), calls=%async_computation.28 | async-start | bytes 8388608
  359.6 35.5 %slice-start.11 = ((s8[9437184]{0:T(1024)(128)(4,1)}), s8[1048576]{0:T(1024)(128)(4,1)S(1)}, s32[]{:S(2)}) async-start(s8[9437184]{0:T(1024)(128)(4,1)} %bitcast.444), calls=%async_computation.29 | async-start | bytes 2097152
  367.2 27.9 %slice-start.12 = ((s8[9437184]{0:T(1024)(128)(4,1)}), s8[4194304]{0:T(1024)(128)(4,1)S(1)}, s32[]{:S(2)}) async-start(s8[9437184]{0:T(1024)(128)(4,1)} %bitcast.444), calls=%async_computation.30 | async-start | bytes 8388608
  374.8 23.3 %copy-start.97 = (bf16[256,1536]{1,0:T(8,128)(2,1)}, bf16[256,1536]{1,0:T(8,128)(2,1)S(1)}, u32[]{:S(2)}) copy-start(bf16[256,1536]{1,0:T(8,128)(2,1)S(1)} %fusion.31) | copy-start | bytes 2359300
  374.8 20.0 %collective-permute-start = (bf16[256,1536]{1,0:T(8,128)(2,1)S(1)}, bf16[256,1536]{1,0:T(8,128)(2,1)S(1)}, u32[]{:S(2)}, u32[]{:S(2)}) collective-permute-start(bf16[256,1536]{1,0:T(8,128)(2,1)S(1)} %fusion.31), channel_id=1, source_target_pairs={{0,16},{1,17},{2,18},{3,19},{4,20},{5,21},{6,22},{7,23},{8,24},{9,... | collective-permute-start | bytes 2359304 | tf_op jit(solution)/shard_map/ppermute | solution.py:22
  394.8 284.5 %copy-start.14 = (bf16[256,1536]{1,0:T(8,128)(2,1)}, bf16[256,1536]{1,0:T(8,128)(2,1)S(1)}, u32[]{:S(2)}) copy-start(bf16[256,1536]{1,0:T(8,128)(2,1)S(1)} %collective-permute-done) | copy-start | bytes 2359300
  405.0 75.4 %all-gather.11.cloned.1.call-start = ((), (), s32[]{:S(2)}) async-start(), calls=%async_computation.8 | async-start | bytes 1966080 | tf_op jit(solution)/shard_map/all_gather | solution.py:582
  407.0 210.9 %reduce-scatter.7.cloned.1.call-start = ((), (), s32[]{:S(2)}) async-start(), calls=%async_computation.12 | async-start | bytes 1966080 | tf_op jit(solution)/shard_map/reduce_scatter | solution.py:709
  415.1 36.7 %copy-start.55 = (bf16[256,8,2,48]{0,3,2,1:T(8,128)(2,1)}, bf16[256,8,2,48]{0,3,2,1:T(8,128)(2,1)S(1)}, u32[]{:S(2)}) copy-start(bf16[256,8,2,48]{0,3,2,1:T(8,128)(2,1)S(1)} %get-tuple-element.93) | copy-start | bytes 1179652
  451.9 40.0 %slice-start.2 = ((s8[4718592]{0:T(1024)(128)(4,1)}), s8[524288]{0:T(1024)(128)(4,1)S(1)}, s32[]{:S(2)}) async-start(s8[4718592]{0:T(1024)(128)(4,1)} %bitcast.431), calls=%async_computation.20 | async-start | bytes 1048576
  493.5 47.9 %copy-start.11 = (f32[256,1536]{1,0:T(8,128)}, f32[256,1536]{1,0:T(8,128)S(1)}, u32[]{:S(2)}) copy-start(f32[256,1536]{1,0:T(8,128)S(1)} %get-tuple-element.144) | copy-start | bytes 4718596
  493.5 47.8 %copy-start.119 = (f32[256]{0:T(256)}, f32[256]{0:T(256)S(1)}, u32[]{:S(2)}) copy-start(f32[256]{0:T(256)S(1)} %add_rsqrt_fusion.2) | copy-start | bytes 3076
  547.9 36.3 %copy-start.105 = (f32[2,8,256]{2,1,0:T(8,128)}, f32[2,8,256]{2,1,0:T(8,128)S(1)}, u32[]{:S(2)}) copy-start(f32[2,8,256]{2,1,0:T(8,128)S(1)} %log_add_fusion) | copy-start | bytes 49156
  584.1 70.7 %reduce-scatter.9.cloned.1.call-start = ((), (), s32[]{:S(2)}) async-start(), calls=%async_computation.13 | async-start | bytes 1966080 | tf_op jit(solution)/shard_map/reduce_scatter | solution.py:712
  593.5 119.0 %all-gather.17.cloned.1.call-start = ((), (), s32[]{:S(2)}) async-start(), calls=%async_computation.11 | async-start | bytes 1966080 | tf_op jit(solution)/shard_map/all_gather | solution.py:581
  603.3 20.5 %collective-permute-start.1 = (bf16[256,1536]{1,0:T(8,128)(2,1)}, bf16[256,1536]{1,0:T(8,128)(2,1)}, u32[]{:S(2)}, u32[]{:S(2)}) collective-permute-start(bf16[256,1536]{1,0:T(8,128)(2,1)} %fusion.32), channel_id=1, source_target_pairs={{0,16},{1,17},{2,18},{3,19},{4,20},{5,21},{6,22},{7,23},{8,24},{9,... | collective-permute-start | bytes 2359304 | tf_op jit(solution)/shard_map/ppermute | solution.py:22
  610.0 55.2 %slice-start.13 = ((s8[9437184]{0:T(1024)(128)(4,1)}), s8[1048576]{0:T(1024)(128)(4,1)S(1)}, s32[]{:S(2)}) async-start(s8[9437184]{0:T(1024)(128)(4,1)} %bitcast.446), calls=%async_computation.31 | async-start | bytes 2097152
  610.2 44.6 %copy-start.9 = (bf16[2,1,256,1536]{3,2,1,0:T(8,128)(2,1)S(1)}, bf16[2,1,256,1536]{3,2,1,0:T(8,128)(2,1)}, u32[]{:S(2)}) copy-start(bf16[2,1,256,1536]{3,2,1,0:T(8,128)(2,1)} %param.12) | copy-start | bytes 4718596
  610.3 44.6 %copy-start.99 = (f32[1536]{0:T(1024)S(1)}, f32[1536]{0:T(1024)}, u32[]{:S(2)}) copy-start(f32[1536]{0:T(1024)} %copy-done.98) | copy-start | bytes 18436
  610.3 44.5 %copy-start.117 = (f32[256]{0:T(256)S(1)}, f32[256]{0:T(256)}, u32[]{:S(2)}) copy-start(f32[256]{0:T(256)} %copy-done.116) | copy-start | bytes 3076
  676.1 74.4 %all-gather.15.cloned.1.call-start = ((), (), s32[]{:S(2)}) async-start(), calls=%async_computation.10 | async-start | bytes 1966080 | tf_op jit(solution)/shard_map/all_gather | solution.py:582
  679.2 235.0 %reduce-scatter.11.cloned.1.call-start = ((), (), s32[]{:S(2)}) async-start(), calls=%async_computation.14 | async-start | bytes 1966080 | tf_op jit(solution)/shard_map/reduce_scatter | solution.py:709
  684.7 27.8 %copy-start.66 = (pred[256,1024]{0,1:T(8,128)(4,1)S(1)}, pred[256,1024]{0,1:T(8,128)(4,1)}, u32[]{:S(2)}) copy-start(pred[256,1024]{0,1:T(8,128)(4,1)} %get-tuple-element.116) | copy-start | bytes 786436
  687.8 89.5 %collective-permute-start.2 = (bf16[256,1536]{1,0:T(8,128)(2,1)}, bf16[256,1536]{1,0:T(8,128)(2,1)}, u32[]{:S(2)}, u32[]{:S(2)}) collective-permute-start(bf16[256,1536]{1,0:T(8,128)(2,1)} %get-tuple-element.73), channel_id=1, source_target_pairs={{16,0},{17,1},{18,2},{19,3},{20,4},{21,5},{22,6},{23,7},{24,8},{25... | collective-permute-start | bytes 2359304 | tf_op jit(solution)/shard_map/ppermute | solution.py:22
  692.6 29.0 %copy-start.51 = (bf16[256,8,2,48]{0,3,2,1:T(8,128)(2,1)}, bf16[256,8,2,48]{0,3,2,1:T(8,128)(2,1)S(1)}, u32[]{:S(2)}) copy-start(bf16[256,8,2,48]{0,3,2,1:T(8,128)(2,1)S(1)} %get-tuple-element.89) | copy-start | bytes 1179652
  692.6 29.0 %copy-start.53 = (bf16[256,8,2,48]{0,3,2,1:T(8,128)(2,1)}, bf16[256,8,2,48]{0,3,2,1:T(8,128)(2,1)S(1)}, u32[]{:S(2)}) copy-start(bf16[256,8,2,48]{0,3,2,1:T(8,128)(2,1)S(1)} %get-tuple-element.90) | copy-start | bytes 1179652
  721.6 40.0 %slice-start.4 = ((s8[4718592]{0:T(1024)(128)(4,1)}), s8[524288]{0:T(1024)(128)(4,1)S(1)}, s32[]{:S(2)}) async-start(s8[4718592]{0:T(1024)(128)(4,1)} %bitcast.433), calls=%async_computation.22 | async-start | bytes 1048576
  789.6 26.6 %slice-start.6 = ((s8[4718592]{0:T(1024)(128)(4,1)}), s8[4194304]{0:T(1024)(128)(4,1)S(1)}, s32[]{:S(2)}) async-start(s8[4718592]{0:T(1024)(128)(4,1)} %bitcast.435), calls=%async_computation.24 | async-start | bytes 8388608
  858.3 73.0 %reduce-scatter.13.cloned.1.call-start = ((), (), s32[]{:S(2)}) async-start(), calls=%async_computation.15 | async-start | bytes 1966080 | tf_op jit(solution)/shard_map/reduce_scatter | solution.py:712
  890.4 225.9 %reduce-scatter.15.cloned.1.call-start = ((), (), s32[]{:S(2)}) async-start(), calls=%async_computation.16 | async-start | bytes 1966080 | tf_op jit(solution)/shard_map/reduce_scatter | solution.py:709
  915.5 23.8 %copy-start.91 = (bf16[256,8,96]{0,2,1:T(8,128)(2,1)}, bf16[256,8,96]{0,2,1:T(8,128)(2,1)S(1)}, u32[]{:S(2)}) copy-start(bf16[256,8,96]{0,2,1:T(8,128)(2,1)S(1)} %pad_maximum_fusion.22) | copy-start | bytes 1179652
  942.7 17.7 %collective-permute-start.3 = (bf16[256,1536]{1,0:T(8,128)(2,1)S(1)}, bf16[256,1536]{1,0:T(8,128)(2,1)S(1)}, u32[]{:S(2)}, u32[]{:S(2)}) collective-permute-start(bf16[256,1536]{1,0:T(8,128)(2,1)S(1)} %convert_element_type.462), channel_id=1, source_target_pairs={{16,0},{17,1},{18,2},{19,3},{20,4},{21,5},{22,6},{23,7},{24,8},{25... | collective-permute-start | bytes 2359304 | tf_op jit(solution)/shard_map/ppermute | solution.py:22
  960.3 31.5 %copy-start.74 = (bf16[256,1536]{1,0:T(8,128)(2,1)}, bf16[256,1536]{1,0:T(8,128)(2,1)S(1)}, u32[]{:S(2)}) copy-start(bf16[256,1536]{1,0:T(8,128)(2,1)S(1)} %collective-permute-done.3) | copy-start | bytes 2359300
  973.4 21.7 %slice-start.8 = ((s8[4718592]{0:T(1024)(128)(4,1)}), s8[4194304]{0:T(1024)(128)(4,1)S(1)}, s32[]{:S(2)}) async-start(s8[4718592]{0:T(1024)(128)(4,1)} %bitcast.437), calls=%async_computation.26 | async-start | bytes 8388608
  1039.9 79.5 %reduce-scatter.17.cloned.1.call-start = ((), (), s32[]{:S(2)}) async-start(), calls=%async_computation.17 | async-start | bytes 1966080 | tf_op jit(solution)/shard_map/reduce_scatter | solution.py:712
  (141 other events, 1150.0 us)
Sparse Core Ops, SparseCore 0:
  259.5 37.5 all-gather.8
  299.2 36.3 all-gather.6
  405.1 36.8 all-gather.12
  444.0 36.3 all-gather.10
  584.3 33.5 reduce-scatter.6
  620.5 34.2 reduce-scatter.8
  676.2 36.2 all-gather.16
  714.1 36.3 all-gather.14
  858.5 35.8 reduce-scatter.10
  897.0 34.2 reduce-scatter.12
  1040.0 37.0 reduce-scatter.14
  1081.7 37.7 reduce-scatter.16

commit v3 on v2

--- a/solution.py
+++ b/solution.py
@@ -2,6 +2,7 @@
 
 import jax
 import jax.numpy as jnp
+import numpy as np
 from jax import lax
 from jax.experimental import pallas as pl
 from jax.experimental.pallas import tpu as pltpu
@@ -10,32 +11,12 @@
 QH = 16
 KVH = 8
 HD = 96
+PARTS = 4
+LANES = 128
 
 
 EPSILON = 1e-05
 ROPE_BASE = 100000.0
-
-
-def from_behind(x, axis, by):
-    devices = lax.axis_size(axis)
-    pairs = [(i, i + by) for i in range(devices) if 0 <= i + by < devices]
-    return lax.ppermute(x, axis, pairs)
-
-
-def rotate(values, cosine_table, sine_table, turn_sign):
-    half_dim = values.shape[-1] // 2
-    leading = values[..., :half_dim]
-    trailing = values[..., half_dim:]
-    return jnp.concatenate(
-        [
-            leading * cosine_table - turn_sign * trailing * sine_table,
-            trailing * cosine_table + turn_sign * leading * sine_table,
-        ],
-        axis=-1,
-    )
-
-
-PARTS = 4
 
 
 def start_remote(source, target, send_sem, recv_sem, device):
@@ -221,9 +202,6 @@
         compiler_params=pltpu.CompilerParams(collective_id=0, has_side_effects=True, vmem_limit_bytes=24 * 1024 * 1024),
         name="gather_weights",
     )(*pieces)
-
-
-LANES = 128
 
 
 def add_rows(target, left, right, rows):
@@ -522,6 +500,407 @@
     return outs[:count]
 
 
+def tile_order():
+    order = np.zeros(4 * HD, np.int32)
+    for tile in range(3):
+        for lane in range(LANES):
+            upper, low = divmod(lane, LANES // 2)
+            if low < HD // 2:
+                head, item = tile, low
+            else:
+                head, item = 3, 16 * tile + low - HD // 2
+            order[tile * LANES + lane] = head * HD + upper * (HD // 2) + item
+    return order
+
+
+def tile_matrix():
+    order = tile_order()
+    return (np.arange(4 * HD)[:, None] == order[None, :]).astype(np.float32)
+
+
+def to_tiles(x):
+    matrix = jnp.asarray(tile_matrix(), jnp.bfloat16)
+    span = 4 * HD
+    return jnp.concatenate(
+        [
+            jnp.dot(x[:, i : i + span], matrix, preferred_element_type=jnp.float32).astype(x.dtype)
+            for i in range(0, x.shape[1], span)
+        ],
+        axis=1,
+    )
+
+
+def from_tiles(x):
+    matrix = jnp.asarray(tile_matrix().T, jnp.bfloat16)
+    span = 4 * HD
+    return jnp.concatenate(
+        [
+            jnp.dot(x[:, i : i + span], matrix, preferred_element_type=jnp.float32).astype(x.dtype)
+            for i in range(0, x.shape[1], span)
+        ],
+        axis=1,
+    )
+
+
+def rows_to_tiles(x):
+    matrix = jnp.asarray(tile_matrix().T, jnp.bfloat16)
+    groups = x.reshape(-1, 4 * HD, x.shape[1])
+    moved = jnp.einsum("lk,gkn->gln", matrix, groups, preferred_element_type=jnp.float32)
+    return moved.astype(x.dtype).reshape(x.shape)
+
+
+def rope_tables(positions):
+    item = tile_order() % (HD // 2)
+    frequency = ROPE_BASE ** (-(jnp.asarray(item, jnp.float32) * 2.0) / HD)
+    angles = positions.astype(jnp.float32)[:, None] * frequency[None, :]
+    upper = (np.arange(3 * LANES) // (LANES // 2)) % 2 == 1
+    sign = jnp.asarray(np.where(upper, 1.0, -1.0), jnp.float32)
+    return jnp.cos(angles), jnp.sin(angles) * sign[None, :]
+
+
+def spare_lanes(shape):
+    return lax.broadcasted_iota(jnp.int32, shape, 1) % (LANES // 2) >= HD // 2
+
+
+def last_head(tiles):
+    spare = spare_lanes(tiles[0].shape)
+    return sum(
+        pltpu.roll(jnp.where(spare, tiles[i], 0.0), LANES - HD // 2 + 16 * i, 1) for i in range(3)
+    )
+
+
+def merge_heads(heads):
+    spare = spare_lanes(heads[0].shape)
+    return [
+        jnp.where(spare, pltpu.roll(heads[3], HD // 2 - 16 * i, 1), heads[i])
+        for i in range(3)
+    ]
+
+
+def tile(ref, index):
+    return ref[:, index * LANES : (index + 1) * LANES]
+
+
+def put(ref, index, value):
+    ref[:, index * LANES : (index + 1) * LANES] = value
+
+
+def turn(value, cosine, sine):
+    return value * cosine + pltpu.roll(value, LANES // 2, 1) * sine
+
+
+def key_tile(group, i):
+    return group * 6 + i
+
+
+def value_tile(group, i):
+    return group * 6 + 3 + i
+
+
+def fill_bias(bias, own_segment, key_segments, rows):
+    size = key_segments.shape[1]
+    same = own_segment[...] == key_segments[...]
+    query = lax.broadcasted_iota(jnp.int32, (rows, size), 0)
+    key = lax.broadcasted_iota(jnp.int32, (rows, size), 1)
+    bias[...] = jnp.where(same & ((key >= rows) | (key <= query)), 0.0, -1e30)
+
+
+def inside(place, shards):
+    return (place >= 0) & (place < shards)
+
+
+def greet_line(shards, way):
+    place = lax.axis_index("shard")
+    barrier = pltpu.get_barrier_semaphore()
+
+    @pl.when(inside(place - way, shards))
+    def _():
+        pl.semaphore_signal(
+            barrier, inc=1, device_id={"shard": place - way}, device_id_type=pl.DeviceIdType.MESH
+        )
+
+    @pl.when(inside(place + way, shards))
+    def _():
+        pl.semaphore_wait(barrier, 1)
+
+
+def dot(left, right, dims):
+    return lax.dot_general(left, right, (dims, ((), ())), preferred_element_type=jnp.float32)
+
+
+NT = ((1,), (1,))
+NN = ((1,), (0,))
+TN = ((0,), (0,))
+
+
+def attend_kernel(
+    shards, hops, rows, raw, cosine, sine, own_segment, key_segments,
+    queries, window, attended, log_total,
+    held, last, bias, query_heads, send_sem, recv_sem, keep_sem,
+):
+    place = lax.axis_index("shard")
+    greet_line(shards, 1)
+
+    def slot(distance):
+        return held.at[pl.ds(distance * rows, rows), :]
+
+    first_key, first_value = QH * 3 // 4, QH * 3 // 4 + KVH * 3 // 4
+    for group in range(KVH // 4):
+        for i in range(3):
+            value = turn(tile(raw, first_key + group * 3 + i), tile(cosine, i), tile(sine, i))
+            held[pl.ds(0, rows), key_tile(group, i) * LANES : (key_tile(group, i) + 1) * LANES] = value.astype(
+                jnp.bfloat16
+            )
+            value = tile(raw, first_value + group * 3 + i)
+            held[pl.ds(0, rows), value_tile(group, i) * LANES : (value_tile(group, i) + 1) * LANES] = (
+                value.astype(jnp.bfloat16)
+            )
+
+    def send(distance):
+        @pl.when((place + 1 < shards) & (place - distance >= 0))
+        def _():
+            start_remote(
+                slot(distance), slot(distance + 1), send_sem.at[distance], recv_sem.at[distance], {"shard": place + 1}
+            )
+
+    send(0)
+    fill_bias(bias, own_segment, key_segments, rows)
+    for group in range(QH // 4):
+        tiles = []
+        for i in range(3):
+            value = turn(tile(raw, group * 3 + i), tile(cosine, i), tile(sine, i))
+            put(queries, group * 3 + i, value.astype(jnp.bfloat16))
+            tiles.append(value)
+        spare = spare_lanes(tiles[0].shape)
+        for i in range(3):
+            query_heads[group * 4 + i] = jnp.where(spare, 0.0, tiles[i]).astype(jnp.bfloat16)
+        query_heads[group * 4 + 3] = last_head(tiles).astype(jnp.bfloat16)
+
+    for distance in range(1, hops + 1):
+        @pl.when(place - distance >= 0)
+        def _():
+            wait_bytes(slot(distance), recv_sem.at[distance - 1])
+
+        @pl.when(place - distance < 0)
+        def _():
+            held[pl.ds(distance * rows, rows), :] = jnp.zeros((rows, held.shape[1]), held.dtype)
+
+        if distance < hops:
+            send(distance)
+
+    keep = pltpu.make_async_copy(held, window, keep_sem)
+    keep.start()
+    for group in range(KVH // 4):
+        for which, first in enumerate((key_tile(group, 0), value_tile(group, 0))):
+            tiles = [tile(held, first + i).astype(jnp.float32) for i in range(3)]
+            last[group * 2 + which] = last_head(tiles).astype(jnp.bfloat16)
+
+    lane = lax.broadcasted_iota(jnp.int32, (rows, LANES), 1)
+    totals = jnp.zeros((rows, LANES), jnp.float32)
+    for group in range(QH // 4):
+        outs = []
+        for i in range(4):
+            head = group * 4 + i
+            key_head = head // 2
+            wide, item = divmod(key_head, 4)
+            keys = last[wide * 2] if item == 3 else tile(held, key_tile(wide, item))
+            values = last[wide * 2 + 1] if item == 3 else tile(held, value_tile(wide, item))
+            scores = dot(query_heads[head], keys, NT) * HD ** (-0.5) + bias[...]
+            top = jnp.max(scores, axis=1, keepdims=True)
+            exponent = jnp.exp(scores - top)
+            total = jnp.sum(exponent, axis=1, keepdims=True)
+            out = dot(exponent.astype(jnp.bfloat16), values, NN) * (1.0 / total)
+            outs.append(out)
+            totals = jnp.where(lane == head, top + jnp.log(total), totals)
+        for i, merged in enumerate(merge_heads(outs)):
+            put(attended, group * 3 + i, merged.astype(jnp.bfloat16))
+    log_total[...] = totals
+    keep.wait()
+    for distance in range(hops):
+        @pl.when((place + 1 < shards) & (place - distance >= 0))
+        def _():
+            wait_bytes(slot(distance), send_sem.at[distance])
+
+
+def line_hops(shards, rows, longest):
+    return min(shards - 1, -(-(longest - 1) // rows))
+
+
+def attend(raw, cosine, sine, own_segment, key_segments, shards, hops):
+    rows = raw.shape[0]
+    width = QH * HD
+    size = (hops + 1) * rows
+    bf16, f32, dma = jnp.bfloat16, jnp.float32, pltpu.SemaphoreType.DMA
+    vmem = pl.BlockSpec(memory_space=pltpu.VMEM)
+    return pl.pallas_call(
+        functools.partial(attend_kernel, shards, hops, rows),
+        out_shape=[
+            jax.ShapeDtypeStruct((rows, width), bf16),
+            jax.ShapeDtypeStruct((size, width), bf16),
+            jax.ShapeDtypeStruct((rows, width), bf16),
+            jax.ShapeDtypeStruct((rows, LANES), f32),
+        ],
+        in_specs=[vmem] * 5,
+        out_specs=[vmem, pl.BlockSpec(memory_space=pl.ANY), vmem, vmem],
+        scratch_shapes=[
+            pltpu.VMEM((size, width), bf16),
+            pltpu.VMEM((KVH // 2, size, LANES), bf16),
+            pltpu.VMEM((rows, size), f32),
+            pltpu.VMEM((QH, rows, LANES), bf16),
+            dma((hops,)),
+            dma((hops,)),
+            dma,
+        ],
+        compiler_params=pltpu.CompilerParams(
+            collective_id=2, has_side_effects=True, vmem_limit_bytes=40 * 1024 * 1024
+        ),
+        name="attend",
+    )(raw, cosine, sine, own_segment, key_segments)
+
+
+def attend_back_kernel(
+    shards, hops, rows, queries, window, log_total, grads, cosine, sine, own_segment, key_segments,
+    lows,
+    bias, own_part, parts, landing, query_grads, send_sem, recv_sem,
+):
+    place = lax.axis_index("shard")
+    greet_line(shards, -1)
+    fill_bias(bias, own_segment, key_segments, rows)
+    span = 6 * LANES
+
+    def heads_of(ref, group):
+        tiles = [tile(ref, group * 3 + i).astype(jnp.float32) for i in range(3)]
+        spare = spare_lanes(tiles[0].shape)
+        heads = [jnp.where(spare, 0.0, t).astype(jnp.bfloat16) for t in tiles]
+        return heads + [last_head(tiles).astype(jnp.bfloat16)]
+
+    def column(head):
+        lane = lax.broadcasted_iota(jnp.int32, (rows, LANES), 1)
+        return jnp.sum(jnp.where(lane == head, log_total[...], 0.0), axis=1, keepdims=True)
+
+    def wide_group(wide):
+        heads = heads_of(queries, 2 * wide) + heads_of(queries, 2 * wide + 1)
+        grad_heads = heads_of(grads, 2 * wide) + heads_of(grads, 2 * wide + 1)
+        key_grads, value_grads = [], []
+        query_out = []
+        key_tiles = [tile(window, key_tile(wide, i)) for i in range(3)]
+        value_tiles = [tile(window, value_tile(wide, i)) for i in range(3)]
+        key_tiles.append(last_head([t.astype(jnp.float32) for t in key_tiles]).astype(jnp.bfloat16))
+        value_tiles.append(last_head([t.astype(jnp.float32) for t in value_tiles]).astype(jnp.bfloat16))
+        for item in range(4):
+            keys, values = key_tiles[item], value_tiles[item]
+            key_grad = value_grad = None
+            for one in (2 * item, 2 * item + 1):
+                query, grad = heads[one], grad_heads[one]
+                scores = dot(query, keys, NT) * HD ** (-0.5) + bias[...]
+                probs = jnp.exp(scores - column(wide * 8 + one))
+                grad_probs = dot(grad, values, NT)
+                along = jnp.sum(probs * grad_probs, axis=1, keepdims=True)
+                grad_scores = (probs * (grad_probs - along)).astype(jnp.bfloat16)
+                query_out.append(dot(grad_scores, keys, NN) * HD ** (-0.5))
+                key_one = dot(grad_scores, query, TN)
+                value_one = dot(probs.astype(jnp.bfloat16), grad, TN)
+                key_grad = key_one if key_grad is None else key_grad + key_one
+                value_grad = value_one if value_grad is None else value_grad + value_one
+            key_grads.append(key_grad * HD ** (-0.5))
+            value_grads.append(value_grad)
+        for which, grads_of in enumerate((key_grads, value_grads)):
+            for i, merged in enumerate(merge_heads(grads_of)):
+                at = which * 3 + i
+                own_part[:, (wide * 6 + at) * LANES : (wide * 6 + at + 1) * LANES] = merged[:rows]
+                for distance in range(1, hops + 1):
+                    parts[wide, distance - 1, :, at * LANES : (at + 1) * LANES] = merged[
+                        distance * rows : (distance + 1) * rows
+                    ].astype(jnp.bfloat16)
+        for half in range(2):
+            for i, merged in enumerate(merge_heads(query_out[half * 4 : half * 4 + 4])):
+                put(query_grads, (2 * wide + half) * 3 + i, merged)
+
+    def step(wide, k):
+        distance = hops - k + 1
+        source = parts.at[wide, distance - 1]
+        target = landing.at[wide, k - 1]
+        sems = (send_sem.at[wide, k - 1], recv_sem.at[wide, k - 1])
+
+        @pl.when(place - distance >= 0)
+        def _():
+            if k > 1:
+                @pl.when(place + 1 < shards)
+                def _():
+                    arrived = landing.at[wide, k - 2]
+                    wait_bytes(arrived, recv_sem.at[wide, k - 2])
+                    source[...] = (
+                        source[...].astype(jnp.float32) + arrived[...].astype(jnp.float32)
+                    ).astype(jnp.bfloat16)
+
+            start_remote(source, target, *sems, {"shard": place - 1})
+
+    def finish(wide):
+        @pl.when(place + 1 < shards)
+        def _():
+            arrived = landing.at[wide, hops - 1]
+            wait_bytes(arrived, recv_sem.at[wide, hops - 1])
+            own_part[:, wide * span : (wide + 1) * span] += arrived[...].astype(jnp.float32)
+
+        first_key, first_value = QH * 3 // 4, QH * 3 // 4 + KVH * 3 // 4
+        for i in range(3):
+            value = turn(tile(own_part, key_tile(wide, i)), tile(cosine, i), -tile(sine, i))
+            put(lows, first_key + wide * 3 + i, value.astype(jnp.bfloat16))
+            put(lows, first_value + wide * 3 + i, tile(own_part, value_tile(wide, i)).astype(jnp.bfloat16))
+
+    for wide in range(KVH // 4):
+        wide_group(wide)
+        step(wide, 1)
+    for group in range(QH // 4):
+        for i in range(3):
+            value = turn(tile(query_grads, group * 3 + i), tile(cosine, i), -tile(sine, i))
+            put(lows, group * 3 + i, value.astype(jnp.bfloat16))
+    for k in range(2, hops + 1):
+        for wide in range(KVH // 4):
+            step(wide, k)
+    for wide in range(KVH // 4):
+        finish(wide)
+    for wide in range(KVH // 4):
+        for k in range(1, hops + 1):
+            @pl.when(place - (hops - k + 1) >= 0)
+            def _():
+                wait_bytes(parts.at[wide, hops - k], send_sem.at[wide, k - 1])
+
+
+def attend_back(queries, window, log_total, grads, cosine, sine, own_segment, key_segments, shards, hops):
+    rows = queries.shape[0]
+    width = QH * HD
+    size = (hops + 1) * rows
+    bf16, f32, dma = jnp.bfloat16, jnp.float32, pltpu.SemaphoreType.DMA
+    vmem = pl.BlockSpec(memory_space=pltpu.VMEM)
+    wides = KVH // 4
+    return pl.pallas_call(
+        functools.partial(attend_back_kernel, shards, hops, rows),
+        out_shape=jax.ShapeDtypeStruct((rows, 2 * width), bf16),
+        in_specs=[vmem] * 8,
+        out_specs=vmem,
+        scratch_shapes=[
+            pltpu.VMEM((rows, size), f32),
+            pltpu.VMEM((rows, width), f32),
+            pltpu.VMEM((wides, hops, rows, 6 * LANES), bf16),
+            pltpu.VMEM((wides, hops, rows, 6 * LANES), bf16),
+            pltpu.VMEM((rows, width), f32),
+            dma((wides, hops)),
+            dma((wides, hops)),
+        ],
+        compiler_params=pltpu.CompilerParams(
+            collective_id=3, has_side_effects=True, vmem_limit_bytes=48 * 1024 * 1024
+        ),
+        name="attend_back",
+    )(queries, window, log_total, grads, cosine, sine, own_segment, key_segments)
+
+
+def from_behind(x, axis, by):
+    devices = lax.axis_size(axis)
+    pairs = [(i, i + by) for i in range(devices) if 0 <= i + by < devices]
+    return lax.ppermute(x, axis, pairs)
+
+
 def swap(x, bit):
     members = lax.axis_size("replica")
     return lax.ppermute(x, "replica", [(r, r ^ (1 << bit)) for r in range(members)])
@@ -534,91 +913,63 @@
 def gather_layer(pieces):
     norm_attn, w_query, w_key, w_value, w_out, norm_ffn, w_gate, w_up, w_down = pieces
     rows = norm_attn.shape[0]
+    shards = lax.axis_size("shard")
     gains = jnp.concatenate([norm_attn, norm_ffn])
     gains = jnp.pad(gains[None], ((0, 15), (0, gain_width(rows) - 2 * rows)))
-    w_qkv = jnp.concatenate([w_query, w_key, w_value], axis=1)
-    shards = lax.axis_size("shard")
+    w_qkv = to_tiles(jnp.concatenate([w_query, w_key, w_value], axis=1))
     w_qkv, w_out, w_gate, w_up, w_down, gains = gather_weights(
         [w_qkv, w_out, w_gate, w_up, w_down, gains], shards
     )
-    gains = gains.reshape(shards, 16, -1)[:, 0]
+    gains = gains.reshape(shards, 16, -1)[:, 0].astype(jnp.float32)
     norm_attn = gains[:, :rows].reshape(-1)
     norm_ffn = gains[:, rows : 2 * rows].reshape(-1)
-    return norm_attn, w_qkv, w_out, norm_ffn, w_gate, w_up, w_down
-
-
-def forward_layer(inputs, weights, segment, row_start):
+    return norm_attn, w_qkv, rows_to_tiles(w_out), norm_ffn, w_gate, w_up, w_down
+
+
+def sequence_tables(segment, rows, hops):
+    place = lax.axis_index("shard")
+    local_segment = lax.dynamic_slice_in_dim(segment, place * rows, rows)
+    starts = jnp.sum((segment[None, :] < local_segment[:, None]).astype(jnp.int32), axis=1)
+    cosine, sine = rope_tables(place * rows + jnp.arange(rows, dtype=jnp.int32) - starts)
+    padded = jnp.concatenate([jnp.full((hops * rows,), -1, jnp.int32), segment])
+    key_segments = jnp.concatenate(
+        [lax.dynamic_slice_in_dim(padded, (place + hops - d) * rows, rows) for d in range(hops + 1)]
+    )
+    return cosine, sine, local_segment[:, None], key_segments[None, :]
+
+
+def matmul(left, right):
+    return jnp.dot(left, right, preferred_element_type=jnp.float32)
+
+
+def matmul_back(left, right):
+    return jnp.einsum("tq,dq->td", left, right, preferred_element_type=jnp.float32)
+
+
+def row_product(left, right):
+    return jnp.einsum("td,tq->dq", left, right, preferred_element_type=jnp.float32)
+
+
+def forward_layer(inputs, weights, tables, shards, hops):
     norm_attn, w_qkv, w_out, norm_ffn, w_gate, w_up, w_down = weights
-    row_count = inputs.shape[0]
-    seq_length = segment.shape[0]
-    groups = QH // KVH
-    half_dim = HD // 2
-    local_segment = lax.dynamic_slice_in_dim(segment, row_start, row_count)
-    query_index = row_start + jnp.arange(row_count, dtype=jnp.int32)
-    starts = jnp.sum((segment[None, :] < local_segment[:, None]).astype(jnp.int32), axis=1)
-    positions = query_index - starts
-    frequency = ROPE_BASE ** (-(jnp.arange(half_dim, dtype=jnp.float32) * 2.0) / HD)
-    angles = positions.astype(jnp.float32)[:, None, None] * frequency[None, None, :]
-    cosine_table = jnp.cos(angles)
-    sine_table = jnp.sin(angles)
     recip_one = lax.rsqrt(jnp.mean(inputs * inputs, axis=-1, keepdims=True) + EPSILON)
     scaled = inputs * recip_one
-    normed = (scaled * norm_attn.astype(jnp.float32)).astype(jnp.bfloat16)
-    raw = jnp.dot(normed, w_qkv, preferred_element_type=jnp.float32)
-    raw_query, raw_key, raw_value = jnp.split(raw, [QH * HD, (QH + KVH) * HD], axis=1)
-    raw_query = raw_query.reshape(row_count, KVH, groups, HD)
-    queries = rotate(raw_query, cosine_table[:, :, None, :], sine_table[:, :, None, :], 1.0).astype(
-        jnp.bfloat16
-    )
-    raw_key = raw_key.reshape(row_count, KVH, HD)
-    key_rows = (
-        rotate(raw_key, cosine_table, sine_table, 1.0)
-        .astype(jnp.bfloat16)
-        .reshape(row_count, KVH * HD)
-    )
-    value_rows = raw_value.astype(jnp.bfloat16)
-    all_keys, all_values = (
-        lax.all_gather(key_rows, "shard", axis=0, tiled=True),
-        lax.all_gather(value_rows, "shard", axis=0, tiled=True),
-    )
-    all_keys = all_keys.reshape(seq_length, KVH, HD)
-    all_values = all_values.reshape(seq_length, KVH, HD)
-    key_index = jnp.arange(seq_length, dtype=jnp.int32)
-    allowed = (key_index[None, :] <= query_index[:, None]) & (
-        segment[None, :] == local_segment[:, None]
-    )
-    scores = jnp.einsum(
-        "ihgd,jhd->hgij", queries, all_keys, preferred_element_type=jnp.float32
-    ) * HD ** (-0.5)
-    scores = jnp.where(allowed, scores, -1e30)
-    row_top = jnp.max(scores, axis=-1, keepdims=True)
-    exponent = jnp.exp(scores - row_top)
-    row_total = jnp.sum(exponent, axis=-1, keepdims=True)
-    probabilities = exponent / row_total
-    log_total = row_top + jnp.log(row_total)
-    attended = jnp.einsum(
-        "hgij,jhd->ihgd",
-        probabilities.astype(jnp.bfloat16),
-        all_values,
-        preferred_element_type=jnp.float32,
-    )
-    attended = attended.reshape(row_count, QH * HD).astype(jnp.bfloat16)
-    middle = inputs + jnp.dot(attended, w_out, preferred_element_type=jnp.float32)
+    normed = (scaled * norm_attn).astype(jnp.bfloat16)
+    queries, window, attended, log_total = attend(matmul(normed, w_qkv), *tables, shards, hops)
+    middle = inputs + matmul(attended, w_out)
     recip_two = lax.rsqrt(jnp.mean(middle * middle, axis=-1, keepdims=True) + EPSILON)
     scaled_mid = middle * recip_two
-    normed_mid = (scaled_mid * norm_ffn.astype(jnp.float32)).astype(jnp.bfloat16)
-    gate_proj = jnp.dot(normed_mid, w_gate, preferred_element_type=jnp.float32)
-    up_proj = jnp.dot(normed_mid, w_up, preferred_element_type=jnp.float32)
+    normed_mid = (scaled_mid * norm_ffn).astype(jnp.bfloat16)
+    gate_proj = matmul(normed_mid, w_gate)
+    up_proj = matmul(normed_mid, w_up)
     hidden = (jax.nn.silu(gate_proj) * up_proj).astype(jnp.bfloat16)
-    result = middle + jnp.dot(hidden, w_down, preferred_element_type=jnp.float32)
+    result = middle + matmul(hidden, w_down)
     saved = (
         scaled,
         recip_one,
         normed,
         queries,
-        all_keys,
-        all_values,
-        allowed,
+        window,
         log_total,
         attended,
         scaled_mid,
@@ -627,22 +978,19 @@
         gate_proj,
         up_proj,
         hidden,
-        cosine_table,
-        sine_table,
+        tables,
     )
     return (result, saved)
 
 
-def backward_layer(grad_result, weights, saved):
+def backward_layer(grad_result, weights, saved, shards, hops):
     norm_attn, w_qkv, w_out, norm_ffn, w_gate, w_up, w_down = weights
     (
         scaled,
         recip_one,
         normed,
         queries,
-        all_keys,
-        all_values,
-        allowed,
+        window,
         log_total,
         attended,
         scaled_mid,
@@ -651,77 +999,28 @@
         gate_proj,
         up_proj,
         hidden,
-        cosine_table,
-        sine_table,
+        tables,
     ) = saved
-    row_count = grad_result.shape[0]
-    seq_length = all_keys.shape[0]
-    groups = QH // KVH
-    score_scale = HD ** (-0.5)
     branch_grad = grad_result.astype(jnp.bfloat16)
-    grad_hidden = jnp.einsum("td,fd->tf", branch_grad, w_down, preferred_element_type=jnp.float32)
+    grad_hidden = matmul_back(branch_grad, w_down)
     sigmoid_gate = jax.nn.sigmoid(gate_proj)
     gate_low = (
         grad_hidden * up_proj * (sigmoid_gate * (1.0 + gate_proj * (1.0 - sigmoid_gate)))
     ).astype(jnp.bfloat16)
     up_low = (grad_hidden * jax.nn.silu(gate_proj)).astype(jnp.bfloat16)
-    grad_normed_mid = jnp.einsum("tf,df->td", gate_low, w_gate, preferred_element_type=jnp.float32)
-    grad_normed_mid = grad_normed_mid + jnp.einsum(
-        "tf,df->td", up_low, w_up, preferred_element_type=jnp.float32
-    )
+    grad_normed_mid = matmul_back(gate_low, w_gate) + matmul_back(up_low, w_up)
     grad_norm_ffn = jnp.sum(grad_normed_mid * scaled_mid, axis=0)
-    grad_scaled_mid = grad_normed_mid * norm_ffn.astype(jnp.float32)
+    grad_scaled_mid = grad_normed_mid * norm_ffn
     grad_middle = grad_result + recip_two * (
         grad_scaled_mid
         - scaled_mid * jnp.mean(grad_scaled_mid * scaled_mid, axis=-1, keepdims=True)
     )
     attn_grad = grad_middle.astype(jnp.bfloat16)
-    grad_attended = jnp.einsum("td,qd->tq", attn_grad, w_out, preferred_element_type=jnp.float32)
-    grad_attended = grad_attended.astype(jnp.bfloat16).reshape(row_count, KVH, groups, HD)
-    scores = (
-        jnp.einsum("ihgd,jhd->hgij", queries, all_keys, preferred_element_type=jnp.float32)
-        * score_scale
-    )
-    scores = jnp.where(allowed, scores, -1e30)
-    probabilities = jnp.exp(scores - log_total)
-    grad_probs = jnp.einsum(
-        "ihgd,jhd->hgij", grad_attended, all_values, preferred_element_type=jnp.float32
-    )
-    row_dot = jnp.sum(probabilities * grad_probs, axis=-1, keepdims=True)
-    grad_scores = (probabilities * (grad_probs - row_dot)).astype(jnp.bfloat16)
-    grad_queries = (
-        jnp.einsum("hgij,jhd->ihgd", grad_scores, all_keys, preferred_element_type=jnp.float32)
-        * score_scale
-    )
-    key_terms = (
-        jnp.einsum("hgij,ihgd->jhd", grad_scores, queries, preferred_element_type=jnp.float32)
-        * score_scale
-    )
-    value_terms = jnp.einsum(
-        "hgij,ihgd->jhd",
-        probabilities.astype(jnp.bfloat16),
-        grad_attended,
-        preferred_element_type=jnp.float32,
-    )
-    key_terms = key_terms.reshape(seq_length, KVH * HD)
-    value_terms = value_terms.reshape(seq_length, KVH * HD)
-    grad_keys, grad_values = (
-        lax.psum_scatter(
-            key_terms.astype(jnp.bfloat16), "shard", scatter_dimension=0, tiled=True
-        ).astype(jnp.float32),
-        lax.psum_scatter(
-            value_terms.astype(jnp.bfloat16), "shard", scatter_dimension=0, tiled=True
-        ).astype(jnp.float32),
-    )
-    query_low = rotate(grad_queries, cosine_table[:, :, None, :], sine_table[:, :, None, :], -1.0)
-    query_low = query_low.reshape(row_count, QH * HD).astype(jnp.bfloat16)
-    key_low = rotate(grad_keys.reshape(row_count, KVH, HD), cosine_table, sine_table, -1.0)
-    key_low = key_low.reshape(row_count, KVH * HD).astype(jnp.bfloat16)
-    value_low = grad_values.astype(jnp.bfloat16)
-    qkv_low = jnp.concatenate([query_low, key_low, value_low], axis=1)
-    grad_normed = jnp.einsum("tq,dq->td", qkv_low, w_qkv, preferred_element_type=jnp.float32)
+    grad_attended = matmul_back(attn_grad, w_out).astype(jnp.bfloat16)
+    qkv_low = attend_back(queries, window, log_total, grad_attended, *tables, shards, hops)
+    grad_normed = matmul_back(qkv_low, w_qkv)
     grad_norm_attn = jnp.sum(grad_normed * scaled, axis=0)
-    grad_scaled = grad_normed * norm_attn.astype(jnp.float32)
+    grad_scaled = grad_normed * norm_attn
     grad_inputs = grad_middle + recip_one * (
         grad_scaled - scaled * jnp.mean(grad_scaled * scaled, axis=-1, keepdims=True)
     )
@@ -737,10 +1036,6 @@
         branch_grad,
     )
     return (grad_inputs, (grad_norm_attn, grad_norm_ffn), operands)
-
-
-def row_product(left, right):
-    return jnp.einsum("td,tq->dq", left, right, preferred_element_type=jnp.float32)
 
 
 def reduce_gradients(operand_pairs, gains):
@@ -754,14 +1049,12 @@
         up_low,
         hidden,
         branch_grad,
-    ) = zip(*operand_pairs)
+    ) = (jnp.concatenate(parts, axis=0) for parts in zip(*operand_pairs))
     shards = lax.axis_size("shard")
     rows = gains[0].shape[0] // shards
 
-    def product(lefts, rights):
-        return sum(row_product(left, right) for left, right in zip(lefts, rights)).astype(
-            jnp.bfloat16
-        )
+    def product(left, right):
+        return row_product(left, right).astype(jnp.bfloat16)
 
     gain_term = jnp.stack([gain.reshape(shards, rows) for gain in gains], axis=1)
     gain_term = gain_term.reshape(shards, 1, 2 * rows).astype(jnp.bfloat16)
@@ -772,7 +1065,7 @@
         product(normed_mid, up_low),
         gain_term.reshape(shards * 16, -1),
     ]
-    trailing = [product(normed, qkv_low), product(attended, attn_grad)]
+    trailing = [product(normed, from_tiles(qkv_low)), product(from_tiles(attended), attn_grad)]
     totals = [total.astype(jnp.float32) for total in reduce_terms(leading, trailing, shards)]
     members = lax.axis_size("replica")
     for bit in range(PARTS.bit_length() - 1, members.bit_length() - 1):
@@ -789,12 +1082,6 @@
         up,
         down,
     )
-
-
-def add_terms(earlier, later):
-    if earlier is None:
-        return later
-    return tuple((left_term + right_term for left_term, right_term in zip(earlier, later)))
 
 
 def body(
@@ -814,33 +1101,38 @@
     micro_count = tokens.shape[0]
     row_count = tokens.shape[2]
     width = tokens.shape[3]
+    seq_length = segments.shape[2]
+    shards = lax.axis_size("shard")
+    hops = line_hops(shards, row_count, seq_length // 2)
     first_section = lax.axis_index("section") == 0
-    row_start = lax.axis_index("shard") * row_count
-    pieces = (
-        norm_attn[0],
-        w_query[0],
-        w_key[0],
-        w_value[0],
-        w_out[0],
-        norm_ffn[0],
-        w_gate[0],
-        w_up[0],
-        w_down[0],
-    )
-    held_weights = gather_layer(pieces)
+
+    def choose(early, late):
+        return jax.tree.map(lambda a, b: jnp.where(first_section, a, b), early, late)
+
+    weights = gather_layer(
+        (
+            norm_attn[0],
+            w_query[0],
+            w_key[0],
+            w_value[0],
+            w_out[0],
+            norm_ffn[0],
+            w_gate[0],
+            w_up[0],
+            w_down[0],
+        )
+    )
+    all_tables = [sequence_tables(segments[m, 0], row_count, hops) for m in range(micro_count)]
     saved_ticks = []
     result_ticks = []
     arriving = jnp.zeros((row_count, width), jnp.bfloat16)
     for tick_index in range(micro_count + 1):
-        weights = held_weights
         own_input = tokens[min(tick_index, micro_count - 1), 0].astype(jnp.float32)
         layer_input = jnp.where(first_section, own_input, arriving.astype(jnp.float32))
-        segment = jnp.where(
-            first_section,
-            segments[min(tick_index, micro_count - 1), 0],
-            segments[max(tick_index - 1, 0), 0],
+        tables = choose(
+            all_tables[min(tick_index, micro_count - 1)], all_tables[max(tick_index - 1, 0)]
         )
-        result, saved = forward_layer(layer_input, weights, segment, row_start)
+        result, saved = forward_layer(layer_input, weights, tables, shards, hops)
         result_low = result.astype(jnp.bfloat16)
         result_ticks.append(result_low)
         saved_ticks.append(saved)
@@ -851,32 +1143,22 @@
     operand_ticks = []
     returning = jnp.zeros((row_count, width), jnp.bfloat16)
     for tick_index in range(micro_count + 1):
-        weights = held_weights
         later_grad = cotangent[min(tick_index, micro_count - 1), 0].astype(jnp.float32)
         incoming = jnp.where(first_section, returning.astype(jnp.float32), later_grad)
         active = jnp.where(first_section, tick_index >= 1, tick_index < micro_count)
         incoming = jnp.where(active, incoming, 0.0)
         if 0 < tick_index < micro_count:
-            saved = jax.tree.map(
-                lambda early_value, late_value: jnp.where(first_section, early_value, late_value),
-                saved_ticks[tick_index - 1],
-                saved_ticks[tick_index + 1],
-            )
+            saved = choose(saved_ticks[tick_index - 1], saved_ticks[tick_index + 1])
         else:
             saved = saved_ticks[1 if tick_index == 0 else micro_count - 1]
-        grad_inputs, gains, operands = backward_layer(incoming, weights, saved)
+        grad_inputs, gains, operands = backward_layer(incoming, weights, saved, shards, hops)
         flow_ticks.append(grad_inputs)
         if tick_index < micro_count:
             returning = from_behind(grad_inputs.astype(jnp.bfloat16), "section", -1)
-        gain_sums = add_terms(gain_sums, gains)
+        gain_sums = gains if gain_sums is None else jax.tree.map(jnp.add, gain_sums, gains)
         operand_ticks.append(operands)
-    first_ops, last_ops = operand_ticks[0], operand_ticks[micro_count]
-    edge_ops = jax.tree.map(
-        lambda early_value, late_value: jnp.where(first_section, late_value, early_value),
-        first_ops,
-        last_ops,
-    )
-    totals = reduce_gradients(operand_ticks[1:micro_count] + [edge_ops], gain_sums)
+    edge_operands = choose(operand_ticks[micro_count], operand_ticks[0])
+    totals = reduce_gradients(operand_ticks[1:micro_count] + [edge_operands], gain_sums)
     section_outputs = jnp.stack(
         [
             jnp.where(first_section, result_ticks[index_micro], result_ticks[index_micro + 1])
@@ -889,18 +1171,8 @@
             for index_micro in range(micro_count)
         ]
     )
-    return (
-        section_outputs[None, :, None],
-        input_grads[None, :, None],
-        totals[0][None],
-        totals[1][None],
-        totals[2][None],
-        totals[3][None],
-        totals[4][None],
-        totals[5][None],
-        totals[6][None],
-        totals[7][None],
-        totals[8][None],
+    return (section_outputs[None, :, None], input_grads[None, :, None]) + tuple(
+        total[None] for total in totals
     )
 
 

time: 1500 us -> 1210 us (0.81)
  Pallas kernels: 540 us -> 799 us
  matrix products: 496 us -> 287 us
  waiting for transfers between devices: 214 us -> 27 us
  other arithmetic: 129 us -> 55.1 us
  local copies, waits for them, and re-layouts: 78.5 us -> 22.5 us
    pallas_call x0 -> x6, Pallas kernels: none -> 262 us  [the longest x3 148 us: attend_back(): pl.pallas_call(functools.partial(attend_back_kernel, shards, hops, rows),...]
    dot_general x49 -> x51, matrix products: 385 us -> 245 us  [the longest x15 125 us: matmul_back(): jnp.einsum('tq,dq->td', left, right, preferred_element_type=jnp.float32)]
    all_gather x6 -> x0, waiting for transfers between devices: 132 us -> none  [the longest x3 72.9 us: forward_layer(): lax.all_gather(key_rows, 'shard', axis=0, tiled=True)]
    dot_general x10 -> x5, matrix products: 111 us -> 41.8 us  [row_product(): jnp.einsum('td,tq->dq', left, right, preferred_element_type=jnp.float32)]
    reduce_scatter x6 -> x0, waiting for transfers between devices: 55.3 us -> none  [the longest x3 48.7 us: backward_layer(): lax.psum_scatter(value_terms.astype(jnp.bfloat16), 'shard', scatter_dimen...]
    convert_element_type x10 -> x7, other arithmetic: 35.2 us -> 4.49 us  [the longest x1 2.44 us: backward_layer(): attn_grad = grad_middle.astype(jnp.bfloat16)]
    split x15 -> x0, local copies, waits for them, and re-layouts: 30.4 us -> none  [forward_layer(): jnp.split(raw, [QH * HD, (QH + KVH) * HD], axis=1)]
    reduce_sum x6 -> x2, other arithmetic: 29 us -> 0.49 us  [sequence_tables(): jnp.sum((segment[None, :] < local_segment[:, None]).astype(jnp.int32), ax...]
  transfers between devices with their start and end apart: 16 -> 4, of which waited for: 13 -> 2; matrix products, arithmetic and copies ran while one was open for 19% -> 6% of each run, Pallas kernels for 0% -> 7%
where the time goes in v3:
time: 1210 us; the launch traced here: 1200 us
  Pallas kernels  799 us (66%)
  matrix products  287 us (24%)
  other arithmetic  55.1 us (5%)
  waiting for transfers between devices  27 us (2%)
  local copies, waits for them, and re-layouts  22.5 us (2%)
    pallas_call x1, Pallas kernels, reduce_terms(): pl.pallas_call(functools.partial(reduce_kernel, shards, (tuple(leads), tu...  312 us
    pallas_call x1, Pallas kernels, gather_weights(): pl.pallas_call(functools.partial(gather_kernel, shards, tuple(chunks), co...  226 us
    pallas_call x3, Pallas kernels, attend_back(): pl.pallas_call(functools.partial(attend_back_kernel, shards, hops, rows),...  148 us
    dot_general x15, matrix products, matmul_back(): jnp.einsum('tq,dq->td', left, right, preferred_element_type=jnp.float32)  125 us
    pallas_call x3, Pallas kernels, attend(): pl.pallas_call(functools.partial(attend_kernel, shards, hops, rows), out_...  114 us
    dot_general x15, matrix products, matmul(): return jnp.dot(left, right, preferred_element_type=jnp.float32)  97.7 us
    dot_general x5, matrix products, row_product(): jnp.einsum('td,tq->dq', left, right, preferred_element_type=jnp.float32)  41.8 us
    ppermute x4, waiting for transfers between devices, from_behind(): return lax.ppermute(x, axis, pairs)  27 us
  transfers between devices with their start and end apart: 4, of which 2 were waited for; matrix products, arithmetic and copies ran while one was open for 6% of the time, Pallas kernels for 7%

profile of v3, /device:TPU:13, one launch (start us, length us, event | category | flops | bytes accessed | tf_op | source)
XLA Modules:
  0.0 1203.1 jit_solution(16294127258092578178)
XLA Ops:
  15.2 225.6 %gather_weights.1 = (bf16[1536,3072]{1,0:T(8,128)(2,1)S(1)}, bf16[1536,1536]{1,0:T(8,128)(2,1)S(1)}, bf16[1536,4096]{1,0:T(8,128)(2,1)}, bf16[1536,4096]{1,0:T(8...) custom-call(bf16[384,3072]{1,0:T(8,128)(2,1)S(1)} %fusion.60.refs_0_, ...), custom_call_target="tpu_custom_call" | custom-call | tf_op jit(solution)/shard_map/gather_weights/pallas_call | solution.py:186
  243.0 3.6 copy-done.17
  246.7 5.3 convolution_convert_fusion.5
  255.0 3.9 fusion.98
  258.9 38.5 %attend.3 = (bf16[256,1536]{1,0:T(8,128)(2,1)S(1)}, bf16[768,1536]{1,0:T(8,128)(2,1)S(1)}, bf16[256,1536]{1,0:T(8,128)(2,1)S(1)}, f32[256,128]{1,0:T(8,128)S(1)}) custom-call(f32[256,3072]{1,0:T(8,128)S(1)} %fusion.102.raw, f32[256,384]{1,0:T(8,128)S(1)} %get-tuple-element.154.cosine, f32[256,384]{1,0:T(8,128)S(1)} %get-tuple-element.144.sine, ...), custom_call_target="tpu_custom_call" | custom-call | tf_op jit(solution)/shard_map/attend/pallas_call | solution.py:735
  299.3 7.5 fusion.129
  306.9 11.9 multiply_convert_fusion.8
  318.9 4.3 fusion.10
  324.8 18.2 %collective-permute-done = bf16[256,1536]{1,0:T(8,128)(2,1)S(1)} collective-permute-done((bf16[256,1536]{1,0:T(8,128)(2,1)}, bf16[256,1536]{1,0:T(8,128)(2,1)S(1)}, u32[]{:S(2)}, u32[]{:S(2)}) %collective-permute-start) | collective-permute-done | bytes 786464 | tf_op jit(solution)/shard_map/ppermute | solution.py:901
  346.4 5.5 fusion.130.raw
  351.9 41.6 %attend.4 = (bf16[256,1536]{1,0:T(8,128)(2,1)S(1)}, bf16[768,1536]{1,0:T(8,128)(2,1)S(1)}, bf16[256,1536]{1,0:T(8,128)(2,1)S(1)}, f32[256,128]{1,0:T(8,128)S(1)}) custom-call(f32[256,3072]{1,0:T(8,128)S(1)} %fusion.130.raw, f32[256,384]{1,0:T(8,128)S(1)} %get-tuple-element.147.cosine, f32[256,384]{1,0:T(8,128)S(1)} %get-tuple-element.143.sine, ...), custom_call_target="tpu_custom_call" | custom-call | tf_op jit(solution)/shard_map/attend/pallas_call | solution.py:735
  395.4 10.9 fusion.132
  406.3 4.9 fusion.131
  411.3 11.2 multiply_convert_fusion.4
  422.5 9.7 fusion.11
  433.5 6.5 fusion.134
  440.0 10.2 multiply_reduce_fusion.2
  452.3 4.4 convolution_convert_fusion.8.grads
  456.7 52.0 %attend_back.3 = bf16[256,3072]{1,0:T(8,128)(2,1)S(1)} custom-call(bf16[256,1536]{1,0:T(8,128)(2,1)S(1)} %get-tuple-element.44.queries, bf16[768,1536]{1,0:T(8,128)(2,1)} %copy-done.1, f32[256,128]{1,0:T(8,128)S(1)} %get-tuple-element.46.log_total, bf16[256,1536]{1,0:T(8,128)(2,1)S(1)} %convolution_convert_fusion.8.grads, ...), custom_call_target="tpu_custom_call" | custom-call | tf_op jit(solution)/shard_map/attend_back/pallas_call | solution.py:877
  511.4 7.2 multiply_reduce_fusion.5
  520.6 4.6 collective-permute-start.2
  525.2 3.9 fusion.123.raw
  529.2 33.7 %attend.5 = (bf16[256,1536]{1,0:T(8,128)(2,1)S(1)}, bf16[768,1536]{1,0:T(8,128)(2,1)S(1)}, bf16[256,1536]{1,0:T(8,128)(2,1)S(1)}, f32[256,128]{1,0:T(8,128)S(1)}) custom-call(f32[256,3072]{1,0:T(8,128)S(1)} %fusion.123.raw, f32[256,384]{1,0:T(8,128)S(1)} %get-tuple-element.155.cosine, f32[256,384]{1,0:T(8,128)S(1)} %get-tuple-element.145.sine, ...), custom_call_target="tpu_custom_call" | custom-call | tf_op jit(solution)/shard_map/attend/pallas_call | solution.py:735
  562.9 4.2 multiply_reduce_fusion.12
  568.5 7.2 fusion.133
  575.7 12.9 %broadcast_select_fusion.3 = (bf16[256,4096]{1,0:T(8,128)(2,1)}, bf16[256,4096]{1,0:T(8,128)(2,1)S(1)}, f32[256,4096]{1,0:T(8,128)}) fusion(bf16[256,4096]{1,0:T(8,128)(2,1)S(1)} %copy-done.91, pred[]{:T(512)S(6)} %eq.3, f32[256,4096]{1,0:T(8,128)S(1)} %fusion.133, bf16[256,1536]{1,0:T(8,128)(2,1)S(1)} %get-tuple-element.110, ...), kind=kOutput, calls=%fused_computation.67 | convolution fusion | flops 3228565504 | bytes 28049408 | tf_op jit(solution)/shard_map/dot_general | solution.py:942
  588.6 8.9 fusion.14
  605.3 11.1 multiply_convert_fusion.2
  616.4 9.9 fusion.135
  626.4 11.6 multiply_reduce_fusion.1
  640.4 4.1 convolution_convert_fusion.7.grads
  644.5 52.6 %attend_back.4 = bf16[256,3072]{1,0:T(8,128)(2,1)S(1)} custom-call(bf16[256,1536]{1,0:T(8,128)(2,1)S(1)} %get-tuple-element.177.queries, bf16[768,1536]{1,0:T(8,128)(2,1)} %broadcast_select_fusion.window, f32[256,128]{1,0:T(8,128)S(1)} %copy-done.16, bf16[256,1536]{1,0:T(8,128)(2,1)S(1)} %convolution_convert_fusion.7.grads, f32[256,384]{1,0:T(8,128)S(1)} %copy-done.10, ...), custom_call_target="tpu_custom_call" | custom-call | tf_op jit(solution)/shard_map/attend_back/pallas_call | solution.py:877
  697.2 7.0 multiply_reduce_fusion.4
  715.1 8.8 collective-permute-done.3
  723.9 13.1 %broadcast_select_fusion.1 = (bf16[256,4096]{1,0:T(8,128)(2,1)}, bf16[256,4096]{1,0:T(8,128)(2,1)}, bf16[256,4096]{1,0:T(8,128)(2,1)}, bf16[256,4096]{1,0:T(8,128)(2,1)}) fusion(bf16[256,4096]{1,0:T(8,128)(2,1)} %get-tuple-element.126, pred[]{:T(512)S(6)} %eq.3, f32[256,4096]{1,0:T(8,128)} %fusion.131, bf16[256,4096]{1,0:T(8,128)(2,1)} %get-tuple-element.127, ...), kind=kOutput, calls=%fused_computation.65 | convolution fusion | flops 3238920192 | bytes 35128320 | tf_op jit(solution)/shard_map/tq,dq->td/dot_general | solution.py:946
  737.0 7.3 fusion.136
  744.3 9.5 multiply_reduce_fusion
  753.8 5.1 broadcast_select_fusion.10
  758.9 4.3 convolution_convert_fusion.6.grads
  763.3 43.5 %attend_back.5 = bf16[256,3072]{1,0:T(8,128)(2,1)S(1)} custom-call(bf16[256,1536]{1,0:T(8,128)(2,1)S(1)} %get-tuple-element.44.queries, bf16[768,1536]{1,0:T(8,128)(2,1)} %copy-done.1, f32[256,128]{1,0:T(8,128)S(1)} %get-tuple-element.46.log_total, bf16[256,1536]{1,0:T(8,128)(2,1)S(1)} %convolution_convert_fusion.6.grads, ...), custom_call_target="tpu_custom_call" | custom-call | tf_op jit(solution)/shard_map/attend_back/pallas_call | solution.py:877
  809.0 7.7 multiply_reduce_fusion.3
  823.9 9.8 convolution_convert_fusion.refs_2_
  833.8 9.6 convolution_convert_fusion.1.refs_1_
  843.4 7.6 convolution_convert_fusion.3.refs_4_
  851.1 9.9 convolution_convert_fusion.2.refs_0_
  861.1 4.8 convolution_convert_fusion.4.refs_5_
  865.9 311.7 %reduce_terms.1 = (bf16[1024,1536]{1,0:T(8,128)(2,1)}, bf16[384,4096]{1,0:T(8,128)(2,1)}, bf16[384,4096]{1,0:T(8,128)(2,1)}, bf16[16,1024]{1,0:T(8,128)(2,1)}, b...) custom-call(bf16[4096,1536]{1,0:T(8,128)(2,1)} %convolution_convert_, ...), custom_call_target="tpu_custom_call" | custom-call | tf_op jit(solution)/shard_map/reduce_terms/pallas_call | solution.py:488
  1194.0 4.1 bitcast_convert_fusion
  (317 shorter events, 88.9 us)
Async XLA Ops:
  2.9 249.1 %copy-start.77 = (f32[256]{0:T(256)}, f32[256]{0:T(256)S(1)}, u32[]{:S(2)}) copy-start(f32[256]{0:T(256)S(1)} %add_rsqrt_fusion.5) | copy-start | bytes 3076
  15.2 231.5 %copy-start.76 = (bf16[384,384,1]{1,0,2:T(8,128)(2,1)S(1)}, bf16[384,384,1]{1,0,2:T(8,128)(2,1)}, u32[]{:S(2)}) copy-start(bf16[384,384,1]{1,0,2:T(8,128)(2,1)} %constant.107) | copy-start | bytes 884740
  252.0 45.4 %copy-start.39 = (bf16[4,1536,384]{1,2,0:T(8,128)(2,1)}, bf16[4,1536,384]{1,2,0:T(8,128)(2,1)S(1)}, u32[]{:S(2)}) copy-start(bf16[4,1536,384]{1,2,0:T(8,128)(2,1)S(1)} %convolution_convert_fusion.5) | copy-start | bytes 14155780
  299.3 19.5 %copy-start.53 = (f32[256,1536]{1,0:T(8,128)}, f32[256,1536]{1,0:T(8,128)S(1)}, u32[]{:S(2)}) copy-start(f32[256,1536]{1,0:T(8,128)S(1)} %get-tuple-element.161) | copy-start | bytes 4718596
  299.3 19.5 %slice-start.8 = ((s8[12582912]{0:T(1024)(128)(4,1)}), s8[4194304]{0:T(1024)(128)(4,1)S(1)}, s32[]{:S(2)}) async-start(s8[12582912]{0:T(1024)(128)(4,1)} %bitcast.283), calls=%async_computation.8 | async-start | bytes 8388608
  299.3 19.5 %slice-start.9 = ((s8[12582912]{0:T(1024)(128)(4,1)}), s8[4194304]{0:T(1024)(128)(4,1)S(1)}, s32[]{:S(2)}) async-start(s8[12582912]{0:T(1024)(128)(4,1)} %bitcast.283), calls=%async_computation.9 | async-start | bytes 8388608
  306.9 12.0 copy-start.84
  306.9 12.0 slice-start.10
  323.2 19.8 %collective-permute-start = (bf16[256,1536]{1,0:T(8,128)(2,1)}, bf16[256,1536]{1,0:T(8,128)(2,1)S(1)}, u32[]{:S(2)}, u32[]{:S(2)}) collective-permute-start(bf16[256,1536]{1,0:T(8,128)(2,1)} %fusion.10), channel_id=1, source_target_pairs={{0,16},{1,17},{2,18},{3,19},{4,20},{5,21},{6,22},{7,23},{8,24},{9,... | collective-permute-start | bytes 2359304 | tf_op jit(solution)/shard_map/ppermute | solution.py:901
  344.8 48.7 %slice-start.3 = ((s8[4718592]{0:T(1024)(128)(4,1)}), s8[4194304]{0:T(1024)(128)(4,1)S(1)}, s32[]{:S(2)}) async-start(s8[4718592]{0:T(1024)(128)(4,1)} %bitcast.263), calls=%async_computation.3 | async-start | bytes 8388608
  346.4 47.1 %slice-start.4 = ((s8[4718592]{0:T(1024)(128)(4,1)}), s8[524288]{0:T(1024)(128)(4,1)S(1)}, s32[]{:S(2)}) async-start(s8[4718592]{0:T(1024)(128)(4,1)} %bitcast.263), calls=%async_computation.4 | async-start | bytes 1048576
  351.9 41.6 %copy-start.24 = (bf16[2,1,256,1536]{3,2,1,0:T(8,128)(2,1)S(1)}, bf16[2,1,256,1536]{3,2,1,0:T(8,128)(2,1)}, u32[]{:S(2)}) copy-start(bf16[2,1,256,1536]{3,2,1,0:T(8,128)(2,1)} %param.20) | copy-start | bytes 4718596
  351.9 41.6 %copy-start.36 = (bf16[256,1536]{1,0:T(8,128)(2,1)S(1)}, bf16[256,1536]{1,0:T(8,128)(2,1)}, u32[]{:S(2)}) copy-start(bf16[256,1536]{1,0:T(8,128)(2,1)} %copy-done.35) | copy-start | bytes 2359300
  395.1 55.1 %copy-start.31 = (f32[256,1536]{1,0:T(8,128)}, f32[256,1536]{1,0:T(8,128)S(1)}, u32[]{:S(2)}) copy-start(f32[256,1536]{1,0:T(8,128)S(1)} %get-tuple-element.165) | copy-start | bytes 4718596
  395.1 11.2 slice-start.5
  395.3 11.0 copy-start.66
  395.3 11.0 slice-start.6
  395.4 11.0 slice-start.7
  422.5 11.0 copy-start.87
  432.2 79.2 %collective-permute-start.1 = (bf16[256,1536]{1,0:T(8,128)(2,1)}, bf16[256,1536]{1,0:T(8,128)(2,1)}, u32[]{:S(2)}, u32[]{:S(2)}) collective-permute-start(bf16[256,1536]{1,0:T(8,128)(2,1)} %fusion.11), channel_id=1, source_target_pairs={{0,16},{1,17},{2,18},{3,19},{4,20},{5,21},{6,22},{7,23},{8,24},{9,... | collective-permute-start | bytes 2359304 | tf_op jit(solution)/shard_map/ppermute | solution.py:901
  452.3 66.3 %copy-start.30 = (f32[256,1536]{1,0:T(8,128)}, f32[256,1536]{1,0:T(8,128)S(1)}, u32[]{:S(2)}) copy-start(f32[256,1536]{1,0:T(8,128)S(1)} %bitcast_add_fusion) | copy-start | bytes 4718596
  456.7 68.5 %slice-start = ((s8[9437184]{0:T(1024)(128)(4,1)}), s8[1048576]{0:T(1024)(128)(4,1)S(1)}, s32[]{:S(2)}) async-start(s8[9437184]{0:T(1024)(128)(4,1)} %bitcast.256), calls=%async_computation | async-start | bytes 2097152
  508.7 9.9 copy-start.2
  511.4 13.8 %slice-start.1 = ((s8[9437184]{0:T(1024)(128)(4,1)}), s8[4194304]{0:T(1024)(128)(4,1)S(1)}, s32[]{:S(2)}) async-start(s8[9437184]{0:T(1024)(128)(4,1)} %bitcast.256), calls=%async_computation.1 | async-start | bytes 8388608
  511.4 13.8 %slice-start.2 = ((s8[9437184]{0:T(1024)(128)(4,1)}), s8[4194304]{0:T(1024)(128)(4,1)S(1)}, s32[]{:S(2)}) async-start(s8[9437184]{0:T(1024)(128)(4,1)} %bitcast.256), calls=%async_computation.2 | async-start | bytes 8388608
  520.6 83.6 %collective-permute-start.2 = (bf16[256,1536]{1,0:T(8,128)(2,1)}, bf16[256,1536]{1,0:T(8,128)(2,1)S(1)}, u32[]{:S(2)}, u32[]{:S(2)}) collective-permute-start(bf16[256,1536]{1,0:T(8,128)(2,1)} %get-tuple-element.120), channel_id=1, source_target_pairs={{16,0},{17,1},{18,2},{19,3},{20,4},{21,5},{22,6},{23,7},{24,8},{25... | collective-permute-start | bytes 2359304 | tf_op jit(solution)/shard_map/ppermute | solution.py:901
  567.1 21.5 %copy-start.56 = (f32[256,1536]{1,0:T(8,128)}, f32[256,1536]{1,0:T(8,128)S(1)}, u32[]{:S(2)}) copy-start(f32[256,1536]{1,0:T(8,128)S(1)} %get-tuple-element.169) | copy-start | bytes 4718596
  575.7 12.9 %copy-start.85 = (f32[256,4096]{1,0:T(8,128)}, f32[256,4096]{1,0:T(8,128)S(1)}, u32[]{:S(2)}) copy-start(f32[256,4096]{1,0:T(8,128)S(1)} %fusion.133) | copy-start | bytes 12582916
  588.6 9.0 copy-start.15
  588.6 9.0 copy-start.78
  605.3 11.1 copy-start.60
  616.4 9.9 copy-start.55
  626.4 11.6 copy-start.48
  644.5 52.6 %copy-start.25 = (bf16[2,1,256,1536]{3,2,1,0:T(8,128)(2,1)S(1)}, bf16[2,1,256,1536]{3,2,1,0:T(8,128)(2,1)}, u32[]{:S(2)}) copy-start(bf16[2,1,256,1536]{3,2,1,0:T(8,128)(2,1)} %param.20) | copy-start | bytes 4718596
  707.5 16.4 %collective-permute-start.3 = (bf16[256,1536]{1,0:T(8,128)(2,1)S(1)}, bf16[256,1536]{1,0:T(8,128)(2,1)}, u32[]{:S(2)}, u32[]{:S(2)}) collective-permute-start(bf16[256,1536]{1,0:T(8,128)(2,1)S(1)} %convert_element_type.305), channel_id=1, source_target_pairs={{16,0},{17,1},{18,2},{19,3},{20,4},{21,5},{22,6},{23,7},{24,8},{25... | collective-permute-start | bytes 2359304 | tf_op jit(solution)/shard_map/ppermute | solution.py:901
  713.8 10.1 copy-start.42
  763.3 43.6 %copy-start.3 = (bf16[256,3072]{1,0:T(8,128)(2,1)S(1)}, bf16[256,3072]{1,0:T(8,128)(2,1)}, u32[]{:S(2)}) copy-start(bf16[256,3072]{1,0:T(8,128)(2,1)} %copy-done.2) | copy-start | bytes 4718596
  809.0 8.5 copy-start.22
  823.9 9.8 copy-start.88
  823.9 9.8 copy-start.93
  833.7 9.7 copy-start.65
  833.7 9.7 copy-start.69
  851.1 10.0 copy-start.63
  851.1 10.0 copy-start.70
  851.1 10.0 copy-start.72
  851.1 10.0 copy-start.73
  851.1 10.0 copy-start.74
  851.1 10.0 copy-start.75
  (62 other events, 242.5 us)

commit v4 on v3

--- a/solution.py
+++ b/solution.py
@@ -609,14 +609,28 @@
     return (place >= 0) & (place < shards)
 
 
+def line_place(shards):
+    place = lax.axis_index("shard")
+    mirrored = lax.axis_index("replica") % 2 == 1
+    return jnp.where(mirrored, shards - 1 - place, place)
+
+
+def line_device(place, shards):
+    mirrored = lax.axis_index("replica") % 2 == 1
+    return {"shard": jnp.where(mirrored, shards - 1 - place, place)}
+
+
 def greet_line(shards, way):
-    place = lax.axis_index("shard")
+    place = line_place(shards)
     barrier = pltpu.get_barrier_semaphore()
 
     @pl.when(inside(place - way, shards))
     def _():
         pl.semaphore_signal(
-            barrier, inc=1, device_id={"shard": place - way}, device_id_type=pl.DeviceIdType.MESH
+            barrier,
+            inc=1,
+            device_id=line_device(place - way, shards),
+            device_id_type=pl.DeviceIdType.MESH,
         )
 
     @pl.when(inside(place + way, shards))
@@ -638,7 +652,7 @@
     queries, window, attended, log_total,
     held, last, bias, query_heads, send_sem, recv_sem, keep_sem,
 ):
-    place = lax.axis_index("shard")
+    place = line_place(shards)
     greet_line(shards, 1)
 
     def slot(distance):
@@ -660,7 +674,11 @@
         @pl.when((place + 1 < shards) & (place - distance >= 0))
         def _():
             start_remote(
-                slot(distance), slot(distance + 1), send_sem.at[distance], recv_sem.at[distance], {"shard": place + 1}
+                slot(distance),
+                slot(distance + 1),
+                send_sem.at[distance],
+                recv_sem.at[distance],
+                line_device(place + 1, shards),
             )
 
     send(0)
@@ -676,7 +694,7 @@
             query_heads[group * 4 + i] = jnp.where(spare, 0.0, tiles[i]).astype(jnp.bfloat16)
         query_heads[group * 4 + 3] = last_head(tiles).astype(jnp.bfloat16)
 
-    for distance in range(1, hops + 1):
+    def receive(distance):
         @pl.when(place - distance >= 0)
         def _():
             wait_bytes(slot(distance), recv_sem.at[distance - 1])
@@ -688,29 +706,53 @@
         if distance < hops:
             send(distance)
 
+    def scores_values(head, first, size):
+        wide, item = divmod(head // 2, 4)
+        span = pl.ds(first, size)
+        if item == 3:
+            keys, values = last[wide * 2, span], last[wide * 2 + 1, span]
+        else:
+            at = [spot(wide, item) * LANES for spot in (key_tile, value_tile)]
+            keys, values = (held[span, lane : lane + LANES] for lane in at)
+        return dot(query_heads[head], keys, NT) * HD ** (-0.5) + bias[:, first : first + size], values
+
+    def fill_last(first, size):
+        for wide in range(KVH // 4):
+            for which, at in enumerate((key_tile(wide, 0), value_tile(wide, 0))):
+                tiles = [
+                    held[pl.ds(first, size), (at + i) * LANES : (at + i + 1) * LANES].astype(jnp.float32)
+                    for i in range(3)
+                ]
+                last[wide * 2 + which, pl.ds(first, size)] = last_head(tiles).astype(jnp.bfloat16)
+
+    for distance in range(1, hops):
+        receive(distance)
+    near = hops * rows
+    fill_last(0, near)
+    state = []
+    for head in range(QH):
+        scores, values = scores_values(head, 0, near)
+        top = jnp.max(scores, axis=1, keepdims=True)
+        exponent = jnp.exp(scores - top)
+        total = jnp.sum(exponent, axis=1, keepdims=True)
+        state.append((top, total, dot(exponent.astype(jnp.bfloat16), values, NN)))
+    receive(hops)
     keep = pltpu.make_async_copy(held, window, keep_sem)
     keep.start()
-    for group in range(KVH // 4):
-        for which, first in enumerate((key_tile(group, 0), value_tile(group, 0))):
-            tiles = [tile(held, first + i).astype(jnp.float32) for i in range(3)]
-            last[group * 2 + which] = last_head(tiles).astype(jnp.bfloat16)
-
+    fill_last(near, rows)
     lane = lax.broadcasted_iota(jnp.int32, (rows, LANES), 1)
     totals = jnp.zeros((rows, LANES), jnp.float32)
     for group in range(QH // 4):
         outs = []
-        for i in range(4):
-            head = group * 4 + i
-            key_head = head // 2
-            wide, item = divmod(key_head, 4)
-            keys = last[wide * 2] if item == 3 else tile(held, key_tile(wide, item))
-            values = last[wide * 2 + 1] if item == 3 else tile(held, value_tile(wide, item))
-            scores = dot(query_heads[head], keys, NT) * HD ** (-0.5) + bias[...]
-            top = jnp.max(scores, axis=1, keepdims=True)
+        for head in range(group * 4, group * 4 + 4):
+            before, total, out = state[head]
+            scores, values = scores_values(head, near, rows)
+            top = jnp.maximum(before, jnp.max(scores, axis=1, keepdims=True))
             exponent = jnp.exp(scores - top)
-            total = jnp.sum(exponent, axis=1, keepdims=True)
-            out = dot(exponent.astype(jnp.bfloat16), values, NN) * (1.0 / total)
-            outs.append(out)
+            shrink = jnp.exp(before - top)
+            total = total * shrink + jnp.sum(exponent, axis=1, keepdims=True)
+            out = out * shrink + dot(exponent.astype(jnp.bfloat16), values, NN)
+            outs.append(out * (1.0 / total))
             totals = jnp.where(lane == head, top + jnp.log(total), totals)
         for i, merged in enumerate(merge_heads(outs)):
             put(attended, group * 3 + i, merged.astype(jnp.bfloat16))
@@ -763,7 +805,7 @@
     lows,
     bias, own_part, parts, landing, query_grads, send_sem, recv_sem,
 ):
-    place = lax.axis_index("shard")
+    place = line_place(shards)
     greet_line(shards, -1)
     fill_bias(bias, own_segment, key_segments, rows)
     span = 6 * LANES
@@ -833,7 +875,7 @@
                         source[...].astype(jnp.float32) + arrived[...].astype(jnp.float32)
                     ).astype(jnp.bfloat16)
 
-            start_remote(source, target, *sems, {"shard": place - 1})
+            start_remote(source, target, *sems, line_device(place - 1, shards))
 
     def finish(wide):
         @pl.when(place + 1 < shards)
@@ -906,6 +948,18 @@
     return lax.ppermute(x, "replica", [(r, r ^ (1 << bit)) for r in range(members)])
 
 
+def mirror(x):
+    members, shards = lax.axis_size("replica"), lax.axis_size("shard")
+    pairs = [
+        (r * shards + s, r * shards + shards - 1 - s)
+        for r in range(1, members, 2)
+        for s in range(shards)
+        if 2 * s != shards - 1
+    ]
+    moved = lax.ppermute(x, ("replica", "shard"), pairs)
+    return jnp.where(lax.axis_index("replica") % 2 == 1, moved, x)
+
+
 def gain_width(rows):
     return -(-2 * rows // (PARTS * LANES)) * PARTS * LANES
 
@@ -927,7 +981,7 @@
 
 
 def sequence_tables(segment, rows, hops):
-    place = lax.axis_index("shard")
+    place = line_place(lax.axis_size("shard"))
     local_segment = lax.dynamic_slice_in_dim(segment, place * rows, rows)
     starts = jnp.sum((segment[None, :] < local_segment[:, None]).astype(jnp.int32), axis=1)
     cosine, sine = rope_tables(place * rows + jnp.arange(rows, dtype=jnp.int32) - starts)
@@ -1109,6 +1163,7 @@
     def choose(early, late):
         return jax.tree.map(lambda a, b: jnp.where(first_section, a, b), early, late)
 
+    tokens, cotangent = mirror(tokens), mirror(cotangent)
     weights = gather_layer(
         (
             norm_attn[0],
@@ -1159,16 +1214,15 @@
         operand_ticks.append(operands)
     edge_operands = choose(operand_ticks[micro_count], operand_ticks[0])
     totals = reduce_gradients(operand_ticks[1:micro_count] + [edge_operands], gain_sums)
-    section_outputs = jnp.stack(
-        [
-            jnp.where(first_section, result_ticks[index_micro], result_ticks[index_micro + 1])
-            for index_micro in range(micro_count)
-        ]
+    section_outputs = mirror(
+        jnp.stack(
+            [choose(result_ticks[index], result_ticks[index + 1]) for index in range(micro_count)]
+        )
     )
     input_grads = jnp.stack(
         [
-            jnp.where(first_section, flow_ticks[index_micro + 1], flow_ticks[index_micro])
-            for index_micro in range(micro_count)
+            mirror(choose(flow_ticks[index + 1], flow_ticks[index]))
+            for index in range(micro_count)
         ]
     )
     return (section_outputs[None, :, None], input_grads[None, :, None]) + tuple(

time: 1210 us -> 1170 us (0.967)
  Pallas kernels: 799 us -> 745 us
  waiting for transfers between devices: 27 us -> 14.1 us
    pallas_call x3, Pallas kernels: 148 us -> 96.8 us  [attend_back(): pl.pallas_call(functools.partial(attend_back_kernel, shards, hops, rows),...]
    pallas_call x3, Pallas kernels: 114 us -> 79.6 us  [attend(): pl.pallas_call(functools.partial(attend_kernel, shards, hops, rows), out_...]
    pallas_call x1, Pallas kernels: 226 us -> 252 us  [gather_weights(): pl.pallas_call(functools.partial(gather_kernel, shards, tuple(chunks), co...]
    ppermute x4, waiting for transfers between devices: 27 us -> 14.1 us  [from_behind(): return lax.ppermute(x, axis, pairs)]
    ppermute x0 -> x5, starting transfers between devices: none -> 12.9 us  [mirror(): moved = lax.ppermute(x, ('replica', 'shard'), pairs)]
    select_n x11 -> x14, other arithmetic: 16.9 us -> 24.4 us  [choose(): jnp.where(first_section, a, b)]
  transfers between devices with their start and end apart: 4 -> 9, of which waited for: 2 -> 2; matrix products, arithmetic and copies ran while one was open for 6% -> 26% of each run, Pallas kernels for 7% -> 62%
where the time goes in v4:
time: 1170 us; the launch traced here: 1160 us
  Pallas kernels  745 us (64%)
  matrix products  297 us (25%)
  other arithmetic  61.2 us (5%)
  local copies, waits for them, and re-layouts  22 us (2%)
  starting transfers between devices  21.5 us (2%)
  waiting for transfers between devices  14.1 us (1%)
    pallas_call x1, Pallas kernels, reduce_terms(): pl.pallas_call(functools.partial(reduce_kernel, shards, (tuple(leads), tu...  317 us
    pallas_call x1, Pallas kernels, gather_weights(): pl.pallas_call(functools.partial(gather_kernel, shards, tuple(chunks), co...  252 us
    dot_general x15, matrix products, matmul_back(): jnp.einsum('tq,dq->td', left, right, preferred_element_type=jnp.float32)  128 us
    dot_general x15, matrix products, matmul(): return jnp.dot(left, right, preferred_element_type=jnp.float32)  104 us
    pallas_call x3, Pallas kernels, attend_back(): pl.pallas_call(functools.partial(attend_back_kernel, shards, hops, rows),...  96.8 us
    pallas_call x3, Pallas kernels, attend(): pl.pallas_call(functools.partial(attend_kernel, shards, hops, rows), out_...  79.6 us
    dot_general x5, matrix products, row_product(): jnp.einsum('td,tq->dq', left, right, preferred_element_type=jnp.float32)  41.7 us
    select_n x14, other arithmetic, choose(): jnp.where(first_section, a, b)  24.4 us
  transfers between devices with their start and end apart: 9, of which 2 were waited for; matrix products, arithmetic and copies ran while one was open for 26% of the time, Pallas kernels for 62%

profile of v4, /device:TPU:13, one launch (start us, length us, event | category | flops | bytes accessed | tf_op | source)
XLA Modules:
  0.0 1164.2 jit_solution(1663406372741397838)
XLA Ops:
  20.0 252.1 %gather_weights.1 = (bf16[1536,3072]{1,0:T(8,128)(2,1)S(1)}, bf16[1536,1536]{1,0:T(8,128)(2,1)S(1)}, bf16[1536,4096]{1,0:T(8,128)(2,1)}, bf16[1536,4096]{1,0:T(8...) custom-call(bf16[384,3072]{1,0:T(8,128)(2,1)S(1)} %fusion.60.refs_0_, ...), custom_call_target="tpu_custom_call" | custom-call | tf_op jit(solution)/shard_map/gather_weights/pallas_call | solution.py:186
  274.3 3.6 copy-done.13
  278.5 3.9 fusion.98
  282.5 6.7 convolution_convert_fusion.5
  293.8 31.6 %attend.3 = (bf16[256,1536]{1,0:T(8,128)(2,1)S(1)}, bf16[768,1536]{1,0:T(8,128)(2,1)S(1)}, bf16[256,1536]{1,0:T(8,128)(2,1)S(1)}, f32[256,128]{1,0:T(8,128)S(1)}) custom-call(f32[256,3072]{1,0:T(8,128)S(1)} %fusion.102.raw, f32[256,384]{1,0:T(8,128)S(1)} %get-tuple-element.154.cosine, f32[256,384]{1,0:T(8,128)S(1)} %get-tuple-element.144.sine, ...), custom_call_target="tpu_custom_call" | custom-call | tf_op jit(solution)/shard_map/attend/pallas_call | solution.py:777
  325.4 3.8 multiply_reduce_fusion.16
  329.2 7.1 fusion.129
  336.4 12.2 %multiply_convert_fusion.8 = (bf16[256,4096]{1,0:T(8,128)(2,1)}, f32[256,4096]{1,0:T(8,128)}) fusion(f32[256,4096]{1,0:T(8,128)S(1)} %fusion.129, bf16[1536,4096]{1,0:T(8,128)(2,1)} %get-tuple-element.40, f32[256,1536]{1,0:T(8,128)S(1)} %get-tuple-element.161, f32[1536]{0:T(1024)S(1)} %mul.417, f32[256]{0:T(256)S(1)} %add_rsqrt_fusion.4), kind=kOutput, calls=%fused_computation.41 | convolution fusion | flops 3228696576 | bytes 24648704 | tf_op jit(solution)/shard_map/dot_general | solution.py:996
  348.6 8.7 fusion.10
  360.5 11.4 collective-permute-done.1
  375.2 23.9 %attend.4 = (bf16[256,1536]{1,0:T(8,128)(2,1)S(1)}, bf16[768,1536]{1,0:T(8,128)(2,1)S(1)}, bf16[256,1536]{1,0:T(8,128)(2,1)S(1)}, f32[256,128]{1,0:T(8,128)S(1)}) custom-call(f32[256,3072]{1,0:T(8,128)S(1)} %fusion.130.raw, f32[256,384]{1,0:T(8,128)S(1)} %get-tuple-element.147.cosine, f32[256,384]{1,0:T(8,128)S(1)} %get-tuple-element.143.sine, ...), custom_call_target="tpu_custom_call" | custom-call | tf_op jit(solution)/shard_map/attend/pallas_call | solution.py:777
  399.1 5.0 multiply_reduce_fusion.14
  404.4 11.0 fusion.132
  415.4 4.9 fusion.131
  420.3 11.5 multiply_convert_fusion.4
  431.8 9.5 fusion.11
  442.6 9.8 fusion.134
  452.4 11.5 multiply_reduce_fusion.2
  466.3 4.4 convolution_convert_fusion.8.grads
  470.8 32.3 %attend_back.3 = bf16[256,3072]{1,0:T(8,128)(2,1)S(1)} custom-call(bf16[256,1536]{1,0:T(8,128)(2,1)S(1)} %get-tuple-element.44.queries, bf16[768,1536]{1,0:T(8,128)(2,1)} %copy-done.3, f32[256,128]{1,0:T(8,128)S(1)} %get-tuple-element.46.log_total, bf16[256,1536]{1,0:T(8,128)(2,1)S(1)} %convolution_convert_fusion.8.grads, ...), custom_call_target="tpu_custom_call" | custom-call | tf_op jit(solution)/shard_map/attend_back/pallas_call | solution.py:919
  504.9 7.9 multiply_reduce_fusion.5
  515.4 3.9 collective-permute-start.5
  519.3 5.6 fusion.123.raw
  524.8 24.2 %attend.5 = (bf16[256,1536]{1,0:T(8,128)(2,1)S(1)}, bf16[768,1536]{1,0:T(8,128)(2,1)S(1)}, bf16[256,1536]{1,0:T(8,128)(2,1)S(1)}, f32[256,128]{1,0:T(8,128)S(1)}) custom-call(f32[256,3072]{1,0:T(8,128)S(1)} %fusion.123.raw, f32[256,384]{1,0:T(8,128)S(1)} %get-tuple-element.155.cosine, f32[256,384]{1,0:T(8,128)S(1)} %get-tuple-element.145.sine, ...), custom_call_target="tpu_custom_call" | custom-call | tf_op jit(solution)/shard_map/attend/pallas_call | solution.py:777
  553.2 6.6 fusion.133
  559.9 13.5 %broadcast_select_fusion.3 = (bf16[256,4096]{1,0:T(8,128)(2,1)}, bf16[256,4096]{1,0:T(8,128)(2,1)S(1)}, f32[256,4096]{1,0:T(8,128)}) fusion(bf16[256,4096]{1,0:T(8,128)(2,1)} %get-tuple-element.162, pred[]{:T(512)S(6)} %eq.21, f32[256,4096]{1,0:T(8,128)S(1)} %fusion.133, bf16[256,1536]{1,0:T(8,128)(2,1)S(1)} %get-tuple-element.110, ...), kind=kOutput, calls=%fused_computation.67 | convolution fusion | flops 3228565504 | bytes 28049408 | tf_op jit(solution)/shard_map/dot_general | solution.py:996
  573.4 8.0 fusion.14
  591.5 10.6 multiply_convert_fusion.2
  602.1 8.4 fusion.135
  610.5 11.1 multiply_reduce_fusion.1
  622.1 4.1 convolution_convert_fusion.7.grads
  626.3 32.4 %attend_back.4 = bf16[256,3072]{1,0:T(8,128)(2,1)S(1)} custom-call(bf16[256,1536]{1,0:T(8,128)(2,1)S(1)} %broadcast_select_fusion.14.queries, bf16[768,1536]{1,0:T(8,128)(2,1)} %broadcast_select_fusion.window, f32[256,128]{1,0:T(8,128)S(1)} %copy-done.12, bf16[256,1536]{1,0:T(8,128)(2,1)S(1)} %convolution_convert_fusion.7.grads, f32[256,384]{1,0:T(8,128)S(1)} %copy-done.10, ...), custom_call_target="tpu_custom_call" | custom-call | tf_op jit(solution)/shard_map/attend_back/pallas_call | solution.py:919
  658.8 7.1 multiply_reduce_fusion.4
  681.9 13.1 %broadcast_select_fusion.1 = (bf16[256,4096]{1,0:T(8,128)(2,1)}, bf16[256,4096]{1,0:T(8,128)(2,1)}, bf16[256,4096]{1,0:T(8,128)(2,1)}, bf16[256,4096]{1,0:T(8,128)(2,1)}) fusion(bf16[256,4096]{1,0:T(8,128)(2,1)} %get-tuple-element.126, pred[]{:T(512)S(6)} %eq.21, f32[256,4096]{1,0:T(8,128)} %fusion.131, bf16[256,4096]{1,0:T(8,128)(2,1)} %get-tuple-element.127, ...), kind=kOutput, calls=%fused_computation.65 | convolution fusion | flops 3238920192 | bytes 35128320 | tf_op jit(solution)/shard_map/tq,dq->td/dot_general | solution.py:1000
  695.1 7.3 fusion.136
  702.4 9.5 multiply_reduce_fusion
  712.0 5.1 broadcast_select_fusion.12
  718.2 3.8 convolution_convert_fusion.6.grads
  722.1 32.1 %attend_back.5 = bf16[256,3072]{1,0:T(8,128)(2,1)S(1)} custom-call(bf16[256,1536]{1,0:T(8,128)(2,1)S(1)} %get-tuple-element.44.queries, bf16[768,1536]{1,0:T(8,128)(2,1)} %copy-done.3, f32[256,128]{1,0:T(8,128)S(1)} %get-tuple-element.46.log_total, bf16[256,1536]{1,0:T(8,128)(2,1)S(1)} %convolution_convert_fusion.6.grads, ...), custom_call_target="tpu_custom_call" | custom-call | tf_op jit(solution)/shard_map/attend_back/pallas_call | solution.py:919
  755.8 7.7 multiply_reduce_fusion.3
  764.3 4.5 add_select_fusion
  776.1 9.7 convolution_convert_fusion.refs_2_
  785.8 9.7 convolution_convert_fusion.1.refs_1_
  795.5 7.6 convolution_convert_fusion.3.refs_4_
  803.2 9.9 convolution_convert_fusion.2.refs_0_
  813.1 4.8 convolution_convert_fusion.4.refs_5_
  817.9 316.8 %reduce_terms.1 = (bf16[1024,1536]{1,0:T(8,128)(2,1)}, bf16[384,4096]{1,0:T(8,128)(2,1)}, bf16[384,4096]{1,0:T(8,128)(2,1)}, bf16[16,1024]{1,0:T(8,128)(2,1)}, b...) custom-call(bf16[4096,1536]{1,0:T(8,128)(2,1)} %convolution_convert_, ...), custom_call_target="tpu_custom_call" | custom-call | tf_op jit(solution)/shard_map/reduce_terms/pallas_call | solution.py:488
  1141.2 3.6 bitcast_convert_fusion
  (330 shorter events, 108.1 us)
Async XLA Ops:
  0.7 288.5 %collective-permute-start = (bf16[2,1,256,1536]{3,2,1,0:T(8,128)(2,1)}, bf16[2,1,256,1536]{3,2,1,0:T(8,128)(2,1)}, u32[]{:S(2)}, u32[]{:S(2)}) collective-permute-start(bf16[2,1,256,1536]{3,2,1,0:T(8,128)(2,1)} %param.20), channel_id=1, source_target_pairs={{4,7},{5,6},{6,5},{7,4},{12,15},{13,14},{14,13},{15,12},{20,23},{2... | collective-permute-start | bytes 4718600 | tf_op jit(solution)/shard_map/ppermute | solution.py:959
  4.0 354.9 %collective-permute-start.4 = (bf16[2,1,256,1536]{3,2,1,0:T(8,128)(2,1)}, bf16[2,1,256,1536]{3,2,1,0:T(8,128)(2,1)}, u32[]{:S(2)}, u32[]{:S(2)}) collective-permute-start(bf16[2,1,256,1536]{3,2,1,0:T(8,128)(2,1)} %param.31), channel_id=1, source_target_pairs={{4,7},{5,6},{6,5},{7,4},{12,15},{13,14},{14,13},{15,12},{20,23},{2... | collective-permute-start | bytes 4718600 | tf_op jit(solution)/shard_map/ppermute | solution.py:959
  20.0 258.5 %copy-start.83 = (f32[384]{0:T(512)S(1)}, f32[384]{0:T(512)}, u32[]{:S(2)}) copy-start(f32[384]{0:T(512)} %constant.132) | copy-start | bytes 4612
  20.0 258.5 %copy-start.84 = (f32[384]{0:T(512)S(1)}, f32[384]{0:T(512)}, u32[]{:S(2)}) copy-start(f32[384]{0:T(512)} %constant.108.clone) | copy-start | bytes 4612
  20.0 262.4 %copy-start.66 = (bf16[384,384,1]{1,0,2:T(8,128)(2,1)S(1)}, bf16[384,384,1]{1,0,2:T(8,128)(2,1)}, u32[]{:S(2)}) copy-start(bf16[384,384,1]{1,0,2:T(8,128)(2,1)} %constant.133) | copy-start | bytes 884740
  277.9 307.2 %copy-start.67 = (f32[1536]{0:T(1024)}, f32[1536]{0:T(1024)S(1)}, u32[]{:S(2)}) copy-start(f32[1536]{0:T(1024)S(1)} %mul.402) | copy-start | bytes 18436
  278.5 12.5 %slice-start = ((s8[9437184]{0:T(1024)(128)(4,1)}), s8[4194304]{0:T(1024)(128)(4,1)S(1)}, s32[]{:S(2)}) async-start(s8[9437184]{0:T(1024)(128)(4,1)} %bitcast.269), calls=%async_computation | async-start | bytes 8388608
  290.7 294.4 %copy-start.14 = (bf16[2,1,256,1536]{3,2,1,0:T(8,128)(2,1)}, bf16[2,1,256,1536]{3,2,1,0:T(8,128)(2,1)S(1)}, u32[]{:S(2)}) copy-start(bf16[2,1,256,1536]{3,2,1,0:T(8,128)(2,1)S(1)} %broadcast_select_fusion.7) | copy-start | bytes 4718596
  329.2 19.4 %copy-start.44 = (f32[256,1536]{1,0:T(8,128)}, f32[256,1536]{1,0:T(8,128)S(1)}, u32[]{:S(2)}) copy-start(f32[256,1536]{1,0:T(8,128)S(1)} %get-tuple-element.161) | copy-start | bytes 4718596
  336.4 12.2 %copy-start.88 = (f32[256,4096]{1,0:T(8,128)}, f32[256,4096]{1,0:T(8,128)S(1)}, u32[]{:S(2)}) copy-start(f32[256,4096]{1,0:T(8,128)S(1)} %fusion.129) | copy-start | bytes 12582916
  348.6 10.3 copy-start.43
  357.4 14.5 %collective-permute-start.1 = (bf16[256,1536]{1,0:T(8,128)(2,1)S(1)}, bf16[256,1536]{1,0:T(8,128)(2,1)S(1)}, u32[]{:S(2)}, u32[]{:S(2)}) collective-permute-start(bf16[256,1536]{1,0:T(8,128)(2,1)S(1)} %fusion.10), channel_id=1, source_target_pairs={{0,16},{1,17},{2,18},{3,19},{4,20},{5,21},{6,22},{7,23},{8,24},{9,... | collective-permute-start | bytes 2359304 | tf_op jit(solution)/shard_map/ppermute | solution.py:943
  360.5 230.1 %copy-start.20 = (bf16[2,1,256,1536]{3,2,1,0:T(8,128)(2,1)}, bf16[2,1,256,1536]{3,2,1,0:T(8,128)(2,1)S(1)}, u32[]{:S(2)}) copy-start(bf16[2,1,256,1536]{3,2,1,0:T(8,128)(2,1)S(1)} %broadcast_select_fusion.6) | copy-start | bytes 4718596
  371.9 141.5 %copy-start.28 = (bf16[256,1536]{1,0:T(8,128)(2,1)}, bf16[256,1536]{1,0:T(8,128)(2,1)S(1)}, u32[]{:S(2)}) copy-start(bf16[256,1536]{1,0:T(8,128)(2,1)S(1)} %collective-permute-done.1) | copy-start | bytes 2359300
  372.2 141.1 %copy-start.70 = (f32[256]{0:T(256)}, f32[256]{0:T(256)S(1)}, u32[]{:S(2)}) copy-start(f32[256]{0:T(256)S(1)} %add_rsqrt_fusion.3) | copy-start | bytes 3076
  404.1 27.7 %copy-start.25 = (f32[256,1536]{1,0:T(8,128)}, f32[256,1536]{1,0:T(8,128)S(1)}, u32[]{:S(2)}) copy-start(f32[256,1536]{1,0:T(8,128)S(1)} %get-tuple-element.165) | copy-start | bytes 4718596
  404.1 59.8 %copy-start.72 = (f32[256]{0:T(256)}, f32[256]{0:T(256)S(1)}, u32[]{:S(2)}) copy-start(f32[256]{0:T(256)S(1)} %add_rsqrt_fusion.2) | copy-start | bytes 3076
  404.1 11.2 slice-start.5
  404.4 11.0 copy-start.56
  404.4 11.0 slice-start.6
  404.4 11.0 slice-start.7
  441.3 63.6 %collective-permute-start.2 = (bf16[256,1536]{1,0:T(8,128)(2,1)}, bf16[256,1536]{1,0:T(8,128)(2,1)}, u32[]{:S(2)}, u32[]{:S(2)}) collective-permute-start(bf16[256,1536]{1,0:T(8,128)(2,1)} %fusion.11), channel_id=1, source_target_pairs={{0,16},{1,17},{2,18},{3,19},{4,20},{5,21},{6,22},{7,23},{8,24},{9,... | collective-permute-start | bytes 2359304 | tf_op jit(solution)/shard_map/ppermute | solution.py:943
  470.7 32.3 %copy-start.53 = (bf16[256,1536]{1,0:T(8,128)(2,1)S(1)}, bf16[256,1536]{1,0:T(8,128)(2,1)}, u32[]{:S(2)}) copy-start(bf16[256,1536]{1,0:T(8,128)(2,1)} %copy-done.52) | copy-start | bytes 2359300
  504.9 76.5 %copy-start.30 = (bf16[1,256,1536]{2,1,0:T(8,128)(2,1)}, bf16[1,256,1536]{2,1,0:T(8,128)(2,1)S(1)}, u32[]{:S(2)}) copy-start(bf16[1,256,1536]{2,1,0:T(8,128)(2,1)S(1)} %select_bitcast_fusion.3) | copy-start | bytes 2359300
  513.4 71.8 %copy-start.77 = (f32[256]{0:T(256)}, f32[256]{0:T(256)S(1)}, u32[]{:S(2)}) copy-start(f32[256]{0:T(256)S(1)} %get-tuple-element.157) | copy-start | bytes 3076
  513.4 35.6 %slice-start.3 = ((s8[4718592]{0:T(1024)(128)(4,1)}), s8[4194304]{0:T(1024)(128)(4,1)S(1)}, s32[]{:S(2)}) async-start(s8[4718592]{0:T(1024)(128)(4,1)} %bitcast.276), calls=%async_computation.3 | async-start | bytes 8388608
  515.4 75.3 %collective-permute-start.5 = (bf16[256,1536]{1,0:T(8,128)(2,1)}, bf16[256,1536]{1,0:T(8,128)(2,1)S(1)}, u32[]{:S(2)}, u32[]{:S(2)}) collective-permute-start(bf16[256,1536]{1,0:T(8,128)(2,1)} %get-tuple-element.120), channel_id=1, source_target_pairs={{16,0},{17,1},{18,2},{19,3},{20,4},{21,5},{22,6},{23,7},{24,8},{25... | collective-permute-start | bytes 2359304 | tf_op jit(solution)/shard_map/ppermute | solution.py:943
  519.2 29.8 %slice-start.4 = ((s8[4718592]{0:T(1024)(128)(4,1)}), s8[524288]{0:T(1024)(128)(4,1)S(1)}, s32[]{:S(2)}) async-start(s8[4718592]{0:T(1024)(128)(4,1)} %bitcast.276), calls=%async_computation.4 | async-start | bytes 1048576
  551.8 21.5 %copy-start.46 = (f32[256,1536]{1,0:T(8,128)}, f32[256,1536]{1,0:T(8,128)S(1)}, u32[]{:S(2)}) copy-start(f32[256,1536]{1,0:T(8,128)S(1)} %get-tuple-element.169) | copy-start | bytes 4718596
  559.9 13.5 %copy-start.89 = (f32[256,4096]{1,0:T(8,128)}, f32[256,4096]{1,0:T(8,128)S(1)}, u32[]{:S(2)}) copy-start(f32[256,4096]{1,0:T(8,128)S(1)} %fusion.133) | copy-start | bytes 12582916
  582.8 569.5 %collective-permute-start.3 = (bf16[2,256,1536]{2,1,0:T(8,128)(2,1)}, bf16[2,256,1536]{2,1,0:T(8,128)(2,1)}, u32[]{:S(2)}, u32[]{:S(2)}) collective-permute-start(bf16[2,256,1536]{2,1,0:T(8,128)(2,1)} %pad_maximum_fusion), channel_id=1, source_target_pairs={{4,7},{5,6},{6,5},{7,4},{12,15},{13,14},{14,13},{15,12},{20,23},{2... | collective-permute-start | bytes 4718600 | tf_op jit(solution)/shard_map/ppermute | solution.py:959
  591.5 10.6 copy-start.48
  610.5 11.1 copy-start.21
  610.5 11.1 copy-start.35
  626.2 32.5 %copy-start.15 = (bf16[2,1,256,1536]{3,2,1,0:T(8,128)(2,1)S(1)}, bf16[2,1,256,1536]{3,2,1,0:T(8,128)(2,1)}, u32[]{:S(2)}) copy-start(bf16[2,1,256,1536]{3,2,1,0:T(8,128)(2,1)} %copy-done.14) | copy-start | bytes 4718596
  626.2 32.5 %copy-start.68 = (f32[1536]{0:T(1024)S(1)}, f32[1536]{0:T(1024)}, u32[]{:S(2)}) copy-start(f32[1536]{0:T(1024)} %copy-done.67) | copy-start | bytes 18436
  626.3 32.5 %copy-start.76 = (f32[256]{0:T(256)S(1)}, f32[256]{0:T(256)}, u32[]{:S(2)}) copy-start(f32[256]{0:T(256)} %copy-done.74) | copy-start | bytes 3076
  626.3 32.5 %copy-start.78 = (f32[256]{0:T(256)S(1)}, f32[256]{0:T(256)}, u32[]{:S(2)}) copy-start(f32[256]{0:T(256)} %copy-done.77) | copy-start | bytes 3076
  669.1 12.8 %collective-permute-start.7 = (bf16[256,1536]{1,0:T(8,128)(2,1)S(1)}, bf16[256,1536]{1,0:T(8,128)(2,1)S(1)}, u32[]{:S(2)}, u32[]{:S(2)}) collective-permute-start(bf16[256,1536]{1,0:T(8,128)(2,1)S(1)} %convert_element_type.305), channel_id=1, source_target_pairs={{16,0},{17,1},{18,2},{19,3},{20,4},{21,5},{22,6},{23,7},{24,8},{25... | collective-permute-start | bytes 2359304 | tf_op jit(solution)/shard_map/ppermute | solution.py:943
  675.9 482.8 %collective-permute-start.6 = (f32[256,1536]{1,0:T(8,128)}, f32[256,1536]{1,0:T(8,128)}, u32[]{:S(2)}, u32[]{:S(2)}) collective-permute-start(f32[256,1536]{1,0:T(8,128)} %get-tuple-element.115), channel_id=1, source_target_pairs={{4,7},{5,6},{6,5},{7,4},{12,15},{13,14},{14,13},{15,12},{20,23},{2... | collective-permute-start | bytes 4718600 | tf_op jit(solution)/shard_map/ppermute | solution.py:959
  681.9 13.1 %copy-start.61 = (bf16[256,1536]{1,0:T(8,128)(2,1)}, bf16[256,1536]{1,0:T(8,128)(2,1)S(1)}, u32[]{:S(2)}) copy-start(bf16[256,1536]{1,0:T(8,128)(2,1)S(1)} %collective-permute-done.7) | copy-start | bytes 2359300
  722.0 32.2 %copy-start.5 = (bf16[256,3072]{1,0:T(8,128)(2,1)S(1)}, bf16[256,3072]{1,0:T(8,128)(2,1)}, u32[]{:S(2)}) copy-start(bf16[256,3072]{1,0:T(8,128)(2,1)} %copy-done.4) | copy-start | bytes 4718596
  768.8 391.5 %collective-permute-start.8 = (f32[256,1536]{1,0:T(8,128)}, f32[256,1536]{1,0:T(8,128)}, u32[]{:S(2)}, u32[]{:S(2)}) collective-permute-start(f32[256,1536]{1,0:T(8,128)} %add_select_fusion), channel_id=1, source_target_pairs={{4,7},{5,6},{6,5},{7,4},{12,15},{13,14},{14,13},{15,12},{20,23},{2... | collective-permute-start | bytes 4718600 | tf_op jit(solution)/shard_map/ppermute | solution.py:959
  803.1 10.0 copy-start.51
  803.1 10.0 copy-start.59
  803.1 9.9 copy-start.62
  803.1 9.9 copy-start.63
  803.2 9.9 copy-start.64
  (66 other events, 339.6 us)

commit v5 on v4

--- a/solution.py
+++ b/solution.py
@@ -794,7 +794,7 @@
             dma,
         ],
         compiler_params=pltpu.CompilerParams(
-            collective_id=2, has_side_effects=True, vmem_limit_bytes=40 * 1024 * 1024
+            collective_id=2, has_side_effects=True, vmem_limit_bytes=62 * 1024 * 1024
         ),
         name="attend",
     )(raw, cosine, sine, own_segment, key_segments)
@@ -931,10 +931,200 @@
             dma((wides, hops)),
         ],
         compiler_params=pltpu.CompilerParams(
-            collective_id=3, has_side_effects=True, vmem_limit_bytes=48 * 1024 * 1024
+            collective_id=3, has_side_effects=True, vmem_limit_bytes=62 * 1024 * 1024
         ),
         name="attend_back",
     )(queries, window, log_total, grads, cosine, sine, own_segment, key_segments)
+
+
+def sigmoid(value):
+    return 1.0 / (1.0 + jnp.exp(-value))
+
+
+def feed_kernel(
+    inputs,
+    attended,
+    w_out,
+    gain,
+    w_gate,
+    w_up,
+    w_down,
+    middle,
+    normed,
+    gate,
+    up,
+    hidden,
+    result,
+    total,
+):
+    step = pl.program_id(0)
+
+    @pl.when(step == 0)
+    def _():
+        value = inputs[...] + dot(attended[...], w_out[...], NN)
+        middle[...] = value
+        recip = lax.rsqrt(jnp.mean(value * value, axis=-1, keepdims=True) + EPSILON)
+        normed[...] = (value * recip * gain[...]).astype(jnp.bfloat16)
+        total[...] = value
+
+    gate_value = dot(normed[...], w_gate[...], NN)
+    up_value = dot(normed[...], w_up[...], NN)
+    low = (gate_value * sigmoid(gate_value) * up_value).astype(jnp.bfloat16)
+    gate[...] = gate_value.astype(jnp.bfloat16)
+    up[...] = up_value.astype(jnp.bfloat16)
+    hidden[...] = low
+    total[...] += dot(low, w_down[...], NN)
+
+    @pl.when(step == pl.num_programs(0) - 1)
+    def _():
+        result[...] = total[...].astype(jnp.bfloat16)
+
+
+def whole(shape):
+    return pl.BlockSpec(shape, lambda i: (0, 0), pipeline_mode=pl.Buffered(1))
+
+
+def feed_forward(inputs, attended, w_out, gain, w_gate, w_up, w_down, block=1024):
+    rows, width = inputs.shape
+    units = w_gate.shape[1]
+    f32, bf16 = jnp.float32, jnp.bfloat16
+    columns = pl.BlockSpec((rows, block), lambda i: (0, i))
+    weight = pl.BlockSpec((width, block), lambda i: (0, i))
+    return pl.pallas_call(
+        feed_kernel,
+        grid=(units // block,),
+        out_shape=[
+            jax.ShapeDtypeStruct((rows, width), f32),
+            jax.ShapeDtypeStruct((rows, width), bf16),
+            jax.ShapeDtypeStruct((rows, units), bf16),
+            jax.ShapeDtypeStruct((rows, units), bf16),
+            jax.ShapeDtypeStruct((rows, units), bf16),
+            jax.ShapeDtypeStruct((rows, width), bf16),
+        ],
+        in_specs=[
+            whole((rows, width)),
+            whole(attended.shape),
+            whole(w_out.shape),
+            whole((1, width)),
+            weight,
+            weight,
+            pl.BlockSpec((block, width), lambda i: (i, 0)),
+        ],
+        out_specs=[
+            whole((rows, width)),
+            whole((rows, width)),
+            columns,
+            columns,
+            columns,
+            whole((rows, width)),
+        ],
+        scratch_shapes=[pltpu.VMEM((rows, width), f32)],
+        compiler_params=pltpu.CompilerParams(vmem_limit_bytes=62 * 1024 * 1024),
+        cost_estimate=pl.CostEstimate(
+            flops=6 * rows * width * units + 2 * rows * width * width,
+            bytes_accessed=6 * width * units + 2 * width * width + 6 * rows * units + 14 * rows * width,
+            transcendentals=rows * units,
+        ),
+        name="feed_forward",
+    )(inputs, attended, w_out, gain[None], w_gate, w_up, w_down)
+
+
+def feed_back_kernel(
+    grads,
+    middle,
+    gain,
+    w_out,
+    gate,
+    up,
+    w_gate,
+    w_up,
+    w_down,
+    gate_low,
+    up_low,
+    grad_middle,
+    attn_grad,
+    grad_attended,
+    gain_grad,
+    branch,
+    total,
+):
+    step = pl.program_id(0)
+
+    @pl.when(step == 0)
+    def _():
+        branch[...] = grads[...].astype(jnp.bfloat16)
+        total[...] = jnp.zeros_like(total)
+
+    grad_hidden = dot(branch[...], w_down[...], NT)
+    gate_value, up_value = gate[...].astype(jnp.float32), up[...].astype(jnp.float32)
+    share = sigmoid(gate_value)
+    one = (grad_hidden * up_value * (share * (1.0 + gate_value * (1.0 - share)))).astype(jnp.bfloat16)
+    two = (grad_hidden * (gate_value * share)).astype(jnp.bfloat16)
+    gate_low[...] = one
+    up_low[...] = two
+    total[...] += dot(one, w_gate[...], NT) + dot(two, w_up[...], NT)
+
+    @pl.when(step == pl.num_programs(0) - 1)
+    def _():
+        value = middle[...]
+        recip = lax.rsqrt(jnp.mean(value * value, axis=-1, keepdims=True) + EPSILON)
+        scaled = value * recip
+        grad = total[...]
+        gain_grad[...] = jnp.sum(grad * scaled, axis=0, keepdims=True)
+        grad = grad * gain[...]
+        grad = grads[...] + recip * (
+            grad - scaled * jnp.mean(grad * scaled, axis=-1, keepdims=True)
+        )
+        grad_middle[...] = grad
+        attn_grad[...] = grad.astype(jnp.bfloat16)
+        grad_attended[...] = dot(attn_grad[...], w_out[...], NT).astype(jnp.bfloat16)
+
+
+def feed_back(grads, middle, gain, w_out, gate, up, w_gate, w_up, w_down, block=1024):
+    rows, width = grads.shape
+    units = w_gate.shape[1]
+    f32, bf16 = jnp.float32, jnp.bfloat16
+    columns = pl.BlockSpec((rows, block), lambda i: (0, i))
+    weight = pl.BlockSpec((width, block), lambda i: (0, i))
+    return pl.pallas_call(
+        feed_back_kernel,
+        grid=(units // block,),
+        out_shape=[
+            jax.ShapeDtypeStruct((rows, units), bf16),
+            jax.ShapeDtypeStruct((rows, units), bf16),
+            jax.ShapeDtypeStruct((rows, width), f32),
+            jax.ShapeDtypeStruct((rows, width), bf16),
+            jax.ShapeDtypeStruct((rows, w_out.shape[0]), bf16),
+            jax.ShapeDtypeStruct((1, width), f32),
+        ],
+        in_specs=[
+            whole((rows, width)),
+            whole((rows, width)),
+            whole((1, width)),
+            whole(w_out.shape),
+            columns,
+            columns,
+            weight,
+            weight,
+            pl.BlockSpec((block, width), lambda i: (i, 0)),
+        ],
+        out_specs=[
+            columns,
+            columns,
+            whole((rows, width)),
+            whole((rows, width)),
+            whole((rows, w_out.shape[0])),
+            whole((1, width)),
+        ],
+        scratch_shapes=[pltpu.VMEM((rows, width), bf16), pltpu.VMEM((rows, width), f32)],
+        compiler_params=pltpu.CompilerParams(vmem_limit_bytes=62 * 1024 * 1024),
+        cost_estimate=pl.CostEstimate(
+            flops=6 * rows * width * units + 2 * rows * width * width,
+            bytes_accessed=6 * width * units + 2 * width * width + 8 * rows * units + 16 * rows * width,
+            transcendentals=rows * units,
+        ),
+        name="feed_back",
+    )(grads, middle, gain[None], w_out, gate, up, w_gate, w_up, w_down)
 
 
 def from_behind(x, axis, by):
@@ -1010,14 +1200,9 @@
     scaled = inputs * recip_one
     normed = (scaled * norm_attn).astype(jnp.bfloat16)
     queries, window, attended, log_total = attend(matmul(normed, w_qkv), *tables, shards, hops)
-    middle = inputs + matmul(attended, w_out)
-    recip_two = lax.rsqrt(jnp.mean(middle * middle, axis=-1, keepdims=True) + EPSILON)
-    scaled_mid = middle * recip_two
-    normed_mid = (scaled_mid * norm_ffn).astype(jnp.bfloat16)
-    gate_proj = matmul(normed_mid, w_gate)
-    up_proj = matmul(normed_mid, w_up)
-    hidden = (jax.nn.silu(gate_proj) * up_proj).astype(jnp.bfloat16)
-    result = middle + matmul(hidden, w_down)
+    middle, normed_mid, gate, up, hidden, result = feed_forward(
+        inputs, attended, w_out, norm_ffn, w_gate, w_up, w_down
+    )
     saved = (
         scaled,
         recip_one,
@@ -1026,11 +1211,10 @@
         window,
         log_total,
         attended,
-        scaled_mid,
-        recip_two,
+        middle,
         normed_mid,
-        gate_proj,
-        up_proj,
+        gate,
+        up,
         hidden,
         tables,
     )
@@ -1047,30 +1231,17 @@
         window,
         log_total,
         attended,
-        scaled_mid,
-        recip_two,
+        middle,
         normed_mid,
-        gate_proj,
-        up_proj,
+        gate,
+        up,
         hidden,
         tables,
     ) = saved
     branch_grad = grad_result.astype(jnp.bfloat16)
-    grad_hidden = matmul_back(branch_grad, w_down)
-    sigmoid_gate = jax.nn.sigmoid(gate_proj)
-    gate_low = (
-        grad_hidden * up_proj * (sigmoid_gate * (1.0 + gate_proj * (1.0 - sigmoid_gate)))
-    ).astype(jnp.bfloat16)
-    up_low = (grad_hidden * jax.nn.silu(gate_proj)).astype(jnp.bfloat16)
-    grad_normed_mid = matmul_back(gate_low, w_gate) + matmul_back(up_low, w_up)
-    grad_norm_ffn = jnp.sum(grad_normed_mid * scaled_mid, axis=0)
-    grad_scaled_mid = grad_normed_mid * norm_ffn
-    grad_middle = grad_result + recip_two * (
-        grad_scaled_mid
-        - scaled_mid * jnp.mean(grad_scaled_mid * scaled_mid, axis=-1, keepdims=True)
-    )
-    attn_grad = grad_middle.astype(jnp.bfloat16)
-    grad_attended = matmul_back(attn_grad, w_out).astype(jnp.bfloat16)
+    gate_low, up_low, grad_middle, attn_grad, grad_attended, grad_norm_ffn = feed_back(
+        grad_result, middle, norm_ffn, w_out, gate, up, w_gate, w_up, w_down
+    )
     qkv_low = attend_back(queries, window, log_total, grad_attended, *tables, shards, hops)
     grad_normed = matmul_back(qkv_low, w_qkv)
     grad_norm_attn = jnp.sum(grad_normed * scaled, axis=0)
@@ -1089,7 +1260,7 @@
         hidden,
         branch_grad,
     )
-    return (grad_inputs, (grad_norm_attn, grad_norm_ffn), operands)
+    return (grad_inputs, (grad_norm_attn, grad_norm_ffn[0]), operands)
 
 
 def reduce_gradients(operand_pairs, gains):
@@ -1163,7 +1334,6 @@
     def choose(early, late):
         return jax.tree.map(lambda a, b: jnp.where(first_section, a, b), early, late)
 
-    tokens, cotangent = mirror(tokens), mirror(cotangent)
     weights = gather_layer(
         (
             norm_attn[0],
@@ -1177,20 +1347,28 @@
             w_down[0],
         )
     )
+    later, gathered = lax.optimization_barrier((tokens[1:], weights[0]))
+    weights = (gathered,) + weights[1:]
+    tokens = jnp.concatenate([mirror(tokens[:1]), mirror(later)]) if micro_count > 1 else mirror(tokens)
     all_tables = [sequence_tables(segments[m, 0], row_count, hops) for m in range(micro_count)]
     saved_ticks = []
     result_ticks = []
+    later_grads = []
     arriving = jnp.zeros((row_count, width), jnp.bfloat16)
     for tick_index in range(micro_count + 1):
         own_input = tokens[min(tick_index, micro_count - 1), 0].astype(jnp.float32)
         layer_input = jnp.where(first_section, own_input, arriving.astype(jnp.float32))
+        if tick_index > 0:
+            layer_input, later_grads[-1] = lax.optimization_barrier((layer_input, later_grads[-1]))
         tables = choose(
             all_tables[min(tick_index, micro_count - 1)], all_tables[max(tick_index - 1, 0)]
         )
-        result, saved = forward_layer(layer_input, weights, tables, shards, hops)
-        result_low = result.astype(jnp.bfloat16)
+        result_low, saved = forward_layer(layer_input, weights, tables, shards, hops)
         result_ticks.append(result_low)
         saved_ticks.append(saved)
+        if tick_index < micro_count:
+            grad, attended = lax.optimization_barrier((cotangent[tick_index, 0], saved[6]))
+            later_grads.append(mirror(grad))
         if tick_index < micro_count:
             arriving = from_behind(result_low, "section", 1)
     flow_ticks = []
@@ -1198,7 +1376,7 @@
     operand_ticks = []
     returning = jnp.zeros((row_count, width), jnp.bfloat16)
     for tick_index in range(micro_count + 1):
-        later_grad = cotangent[min(tick_index, micro_count - 1), 0].astype(jnp.float32)
+        later_grad = later_grads[min(tick_index, micro_count - 1)].astype(jnp.float32)
         incoming = jnp.where(first_section, returning.astype(jnp.float32), later_grad)
         active = jnp.where(first_section, tick_index >= 1, tick_index < micro_count)
         incoming = jnp.where(active, incoming, 0.0)

time: 1170 us -> 1170 us (level)
  matrix products: 297 us -> 100 us
  Pallas kernels: 745 us -> 885 us
  waiting for transfers between devices: 14.1 us -> 42.3 us
  local copies, waits for them, and re-layouts: 22 us -> 34.6 us
    pallas_call x0 -> x6, Pallas kernels: none -> 147 us  [the longest x3 75.7 us: feed_back(): pl.pallas_call(feed_back_kernel, grid=(units // block,), out_shape=[jax.S...]
    dot_general x15 -> x3, matrix products: 128 us -> 21.7 us  [matmul_back(): jnp.einsum('tq,dq->td', left, right, preferred_element_type=jnp.float32)]
    dot_general x15 -> x3, matrix products: 104 us -> 17 us  [matmul(): return jnp.dot(left, right, preferred_element_type=jnp.float32)]
    pallas_call x1, Pallas kernels: 252 us -> 227 us  [gather_weights(): pl.pallas_call(functools.partial(gather_kernel, shards, tuple(chunks), co...]
    ppermute x5 -> x7, waiting for transfers between devices: 0.01 us -> 24 us  [mirror(): moved = lax.ppermute(x, ('replica', 'shard'), pairs)]
    pallas_call x3, Pallas kernels: 79.6 us -> 91.7 us  [attend(): pl.pallas_call(functools.partial(attend_kernel, shards, hops, rows), out_...]
    select_n x14 -> x18, other arithmetic: 24.4 us -> 25.6 us  [choose(): jnp.where(first_section, a, b)]
  transfers between devices with their start and end apart: 9 -> 11, of which waited for: 2 -> 3; matrix products, arithmetic and copies ran while one was open for 26% -> 13% of each run, Pallas kernels for 62% -> 66%
where the time goes in v5:
time: 1170 us; the launch traced here: 1160 us
  Pallas kernels  885 us (76%)
  matrix products  100 us (9%)
  other arithmetic  66.6 us (6%)
  waiting for transfers between devices  42.3 us (4%)
  local copies, waits for them, and re-layouts  34.6 us (3%)
  starting transfers between devices  28.5 us (2%)
    pallas_call x1, Pallas kernels, reduce_terms(): pl.pallas_call(functools.partial(reduce_kernel, shards, (tuple(leads), tu...  314 us
    pallas_call x1, Pallas kernels, gather_weights(): pl.pallas_call(functools.partial(gather_kernel, shards, tuple(chunks), co...  227 us
    pallas_call x3, Pallas kernels, attend_back(): pl.pallas_call(functools.partial(attend_back_kernel, shards, hops, rows),...  105 us
    pallas_call x3, Pallas kernels, attend(): pl.pallas_call(functools.partial(attend_kernel, shards, hops, rows), out_...  91.7 us
    pallas_call x3, Pallas kernels, feed_back(): pl.pallas_call(feed_back_kernel, grid=(units // block,), out_shape=[jax.S...  75.7 us
    pallas_call x3, Pallas kernels, feed_forward(): pl.pallas_call(feed_kernel, grid=(units // block,), out_shape=[jax.ShapeD...  71.2 us
    dot_general x5, matrix products, row_product(): jnp.einsum('td,tq->dq', left, right, preferred_element_type=jnp.float32)  43.9 us
    select_n x18, other arithmetic, choose(): jnp.where(first_section, a, b)  25.6 us
  transfers between devices with their start and end apart: 11, of which 3 were waited for; matrix products, arithmetic and copies ran while one was open for 13% of the time, Pallas kernels for 66%

profile of v5, /device:TPU:13, one launch (start us, length us, event | category | flops | bytes accessed | tf_op | source)
XLA Modules:
  0.0 1159.5 jit_solution(12039888239101405805)
XLA Ops:
  0.7 2.7 fusion.109
  3.4 3.2 collective-permute-start
  17.8 227.4 %gather_weights.1 = (bf16[1536,3072]{1,0:T(8,128)(2,1)S(1)}, bf16[1536,1536]{1,0:T(8,128)(2,1)S(1)}, bf16[1536,4096]{1,0:T(8,128)(2,1)}, bf16[1536,4096]{1,0:T(8...) custom-call(bf16[384,3072]{1,0:T(8,128)(2,1)S(1)} %copy-done.5, bf16[384,1536]{1,0:T(8,128)(2,1)S(1)} %bitcast.167, ...), custom_call_target="tpu_custom_call" | custom-call | tf_op jit(solution)/shard_map/gather_weights/pallas_call | solution.py:186
  245.2 2.2 copy-done
  247.4 3.6 copy-done.7
  251.1 2.7 collective-permute-start.1
  256.6 6.7 convolution_convert_fusion.5
  264.0 4.2 fusion.84
  272.8 4.4 fusion.86.raw
  277.2 28.6 %attend.3 = (bf16[256,1536]{1,0:T(8,128)(2,1)}, bf16[768,1536]{1,0:T(8,128)(2,1)}, bf16[256,1536]{1,0:T(8,128)(2,1)}, f32[256,128]{1,0:T(8,128)}) custom-call(f32[256,3072]{1,0:T(8,128)} %fusion.86.raw, f32[256,384]{1,0:T(8,128)} %get-tuple-element.235.cosine, f32[256,384]{1,0:T(8,128)} %get-tuple-element.225.sine, s32[256,1]{1,0:T(8,128)} %copy.89.own_segment, ...), custom_call_target="tpu_custom_call" | custom-call | tf_op jit(solution)/shard_map/attend/pallas_call | solution.py:777
  307.7 23.7 %feed_forward.3 = (f32[256,1536]{1,0:T(8,128)}, bf16[256,1536]{1,0:T(8,128)(2,1)}, bf16[256,4096]{1,0:T(8,128)(2,1)}, bf16[256,4096]{1,0:T(8,128)(2,1)}, bf16[25...) custom-call(f32[256,1536]{1,0:T(8,128)} %select_bitcast_fusion.3.inputs, bf16[256,1536]{1,0:T(8,128)(2,1)} %get-tuple-element.82.attended, ...), custom_call_target="tpu_custom_call" | custom-call | flops 10871635968 | bytes 54263808 | tf_op jit(solution)/shard_map/feed_forward/pallas_call | solution.py:993
  335.6 12.5 %collective-permute-done.2 = bf16[256,1536]{1,0:T(8,128)(2,1)} collective-permute-done((bf16[256,1536]{1,0:T(8,128)(2,1)}, bf16[256,1536]{1,0:T(8,128)(2,1)}, u32[]{:S(2)}, u32[]{:S(2)}) %collective-permute-start.2) | collective-permute-done | bytes 786464 | tf_op jit(solution)/shard_map/ppermute | solution.py:1133
  350.9 8.2 fusion.112.raw
  359.1 33.5 %attend.4 = (bf16[256,1536]{1,0:T(8,128)(2,1)}, bf16[768,1536]{1,0:T(8,128)(2,1)}, bf16[256,1536]{1,0:T(8,128)(2,1)}, f32[256,128]{1,0:T(8,128)}) custom-call(f32[256,3072]{1,0:T(8,128)} %fusion.112.raw, f32[256,384]{1,0:T(8,128)} %get-tuple-element.228.cosine, f32[256,384]{1,0:T(8,128)} %get-tuple-element.224.sine, ...), custom_call_target="tpu_custom_call" | custom-call | tf_op jit(solution)/shard_map/attend/pallas_call | solution.py:777
  392.6 23.7 %feed_forward.4 = (f32[256,1536]{1,0:T(8,128)}, bf16[256,1536]{1,0:T(8,128)(2,1)}, bf16[256,4096]{1,0:T(8,128)(2,1)}, bf16[256,4096]{1,0:T(8,128)(2,1)}, bf16[25...) custom-call(f32[256,1536]{1,0:T(8,128)} %copy-done.9, bf16[256,1536]{1,0:T(8,128)(2,1)} %get-tuple-element.91.attended, ...), custom_call_target="tpu_custom_call" | custom-call | flops 10871635968 | bytes 54263808 | tf_op jit(solution)/shard_map/feed_forward/pallas_call | solution.py:993
  420.9 25.2 %feed_back.3 = (bf16[256,4096]{1,0:T(8,128)(2,1)}, bf16[256,4096]{1,0:T(8,128)(2,1)}, f32[256,1536]{1,0:T(8,128)}, bf16[256,1536]{1,0:T(8,128)(2,1)}, bf16[256,1536]{1,0:T(8,128)(2,1)}, /*index=5*/f32[1,1536]{1,0:T(1,128)}) custom-call(f32[256,1536]{1,0:T(8,128)} %select_select_fusion.grads, f32[256,1536]{1,0:T(8,128)} %get-tuple-element.98.middle, ...), custom_call_target="tpu_custom_call" | custom-call | flops 10871635968 | bytes 57147392 | tf_op jit(solution)/shard_map/feed_back/pallas_call | solution.py:1089
  446.2 33.4 %attend_back.3 = bf16[256,3072]{1,0:T(8,128)(2,1)} custom-call(bf16[256,1536]{1,0:T(8,128)(2,1)} %get-tuple-element.102.queries, bf16[768,1536]{1,0:T(8,128)(2,1)} %get-tuple-element.103.window, f32[256,128]{1,0:T(8,128)} %get-tuple-element.104.log_total, bf16[256,1536]{1,0:T(8,128)(2,1)} %get-tuple-element.105.grads, f32[256,384]{1,0:T(8,128)} %get-tuple-element.228.cosine, ...), custom_call_target="tpu_custom_call" | custom-call | tf_op jit(solution)/shard_map/attend_back/pallas_call | solution.py:919
  479.6 6.1 multiply_reduce_fusion.2
  487.7 5.9 collective-permute-start.7
  493.6 2.1 broadcast_select_fusion.7
  497.6 4.4 fusion.106.raw
  502.1 29.5 %attend.5 = (bf16[256,1536]{1,0:T(8,128)(2,1)}, bf16[768,1536]{1,0:T(8,128)(2,1)}, bf16[256,1536]{1,0:T(8,128)(2,1)}, f32[256,128]{1,0:T(8,128)}) custom-call(f32[256,3072]{1,0:T(8,128)} %fusion.106.raw, f32[256,384]{1,0:T(8,128)} %get-tuple-element.236.cosine, f32[256,384]{1,0:T(8,128)} %get-tuple-element.226.sine, s32[256,1]{1,0:T(8,128)} %copy-done.57, ...), custom_call_target="tpu_custom_call" | custom-call | tf_op jit(solution)/shard_map/attend/pallas_call | solution.py:777
  531.6 23.8 %feed_forward.5 = (f32[256,1536]{1,0:T(8,128)}, bf16[256,1536]{1,0:T(8,128)(2,1)}, bf16[256,4096]{1,0:T(8,128)(2,1)}, bf16[256,4096]{1,0:T(8,128)(2,1)}, bf16[25...) custom-call(f32[256,1536]{1,0:T(8,128)} %copy-done.12, bf16[256,1536]{1,0:T(8,128)(2,1)} %get-tuple-element.95.attended, ...), custom_call_target="tpu_custom_call" | custom-call | flops 10871635968 | bytes 54263808 | tf_op jit(solution)/shard_map/feed_forward/pallas_call | solution.py:993
  555.5 2.2 broadcast_select_fusion.16.queries
  557.7 3.3 broadcast_select_fusion.4.up
  568.3 2.8 fusion.107
  571.1 25.3 %feed_back.4 = (bf16[256,4096]{1,0:T(8,128)(2,1)}, bf16[256,4096]{1,0:T(8,128)(2,1)}, f32[256,1536]{1,0:T(8,128)}, bf16[256,1536]{1,0:T(8,128)(2,1)}, bf16[256,1536]{1,0:T(8,128)(2,1)}, /*index=5*/f32[1,1536]{1,0:T(1,128)}) custom-call(f32[256,1536]{1,0:T(8,128)} %get-tuple-element.198.grads, f32[256,1536]{1,0:T(8,128)} %broadcast_select_fusion.17.middle, ...), custom_call_target="tpu_custom_call" | custom-call | flops 10871635968 | bytes 57147392 | tf_op jit(solution)/shard_map/feed_back/pallas_call | solution.py:1089
  596.4 33.9 %attend_back.4 = bf16[256,3072]{1,0:T(8,128)(2,1)} custom-call(bf16[256,1536]{1,0:T(8,128)(2,1)} %broadcast_select_fusion.16.queries, bf16[768,1536]{1,0:T(8,128)(2,1)} %broadcast_select_fusion.window, f32[256,128]{1,0:T(8,128)} %broadcast_select_fusion.18.log_total, bf16[256,1536]{1,0:T(8,128)(2,1)} %get-tuple-element.120.grads, ...), custom_call_target="tpu_custom_call" | custom-call | tf_op jit(solution)/shard_map/attend_back/pallas_call | solution.py:919
  630.4 7.8 multiply_reduce_fusion.1
  638.3 1.9 broadcast_select_fusion.15
  645.7 3.5 collective-permute-start.6
  652.8 5.8 collective-permute-done.9
  666.2 25.2 %feed_back.5 = (bf16[256,4096]{1,0:T(8,128)(2,1)}, bf16[256,4096]{1,0:T(8,128)(2,1)}, f32[256,1536]{1,0:T(8,128)}, bf16[256,1536]{1,0:T(8,128)(2,1)}, bf16[256,1536]{1,0:T(8,128)(2,1)}, /*index=5*/f32[1,1536]{1,0:T(1,128)}) custom-call(f32[256,1536]{1,0:T(8,128)} %fusion.9.grads, f32[256,1536]{1,0:T(8,128)} %get-tuple-element.98.middle, ...), custom_call_target="tpu_custom_call" | custom-call | flops 10871635968 | bytes 57147392 | tf_op jit(solution)/shard_map/feed_back/pallas_call | solution.py:1089
  691.4 37.5 %attend_back.5 = bf16[256,3072]{1,0:T(8,128)(2,1)} custom-call(bf16[256,1536]{1,0:T(8,128)(2,1)} %get-tuple-element.102.queries, bf16[768,1536]{1,0:T(8,128)(2,1)} %get-tuple-element.103.window, f32[256,128]{1,0:T(8,128)} %get-tuple-element.104.log_total, bf16[256,1536]{1,0:T(8,128)(2,1)} %get-tuple-element.122.grads, f32[256,384]{1,0:T(8,128)} %get-tuple-element.228.cosine, ...), custom_call_target="tpu_custom_call" | custom-call | tf_op jit(solution)/shard_map/attend_back/pallas_call | solution.py:919
  730.8 7.8 multiply_reduce_fusion
  744.7 10.1 convolution_convert_fusion.3.refs_4_
  756.9 9.6 convolution_convert_fusion.refs_2_
  766.5 9.6 convolution_convert_fusion.1.refs_1_
  776.2 9.8 convolution_convert_fusion.2.refs_0_
  786.0 4.8 convolution_convert_fusion.4.refs_5_
  790.8 314.2 %reduce_terms.1 = (bf16[1024,1536]{1,0:T(8,128)(2,1)}, bf16[384,4096]{1,0:T(8,128)(2,1)}, bf16[384,4096]{1,0:T(8,128)(2,1)}, bf16[16,1024]{1,0:T(8,128)(2,1)}, b...) custom-call(bf16[4096,1536]{1,0:T(8,128)(2,1)} %convolution_convert_, ...), custom_call_target="tpu_custom_call" | custom-call | tf_op jit(solution)/shard_map/reduce_terms/pallas_call | solution.py:488
  1105.0 2.4 convert_element_type.242
  1107.6 3.6 bitcast_convert_fusion
  1111.2 3.5 bitcast_convert_fusion.1
  1114.7 3.6 bitcast_convert_fusion.2
  1119.1 3.2 collective-permute-start.10
  1128.8 2.8 select_bitcast_fusion.2
  1133.2 24.0 %collective-permute-done.10 = f32[256,1536]{1,0:T(8,128)S(1)} collective-permute-done((f32[256,1536]{1,0:T(8,128)S(1)}, f32[256,1536]{1,0:T(8,128)S(1)}, u32[]{:S(2)}, u32[]{:S(2)}) %collective-permute-start.10) | collective-permute-done | bytes 1572896 | tf_op jit(solution)/shard_map/ppermute | solution.py:1149
  (309 shorter events, 81.2 us)
Async XLA Ops:
  3.4 265.7 %collective-permute-start = (bf16[1,1,256,1536]{3,2,1,0:T(8,128)(2,1)}, bf16[1,1,256,1536]{3,2,1,0:T(8,128)(2,1)}, u32[]{:S(2)}, u32[]{:S(2)}) collective-permute-start(bf16[1,1,256,1536]{3,2,1,0:T(8,128)(2,1)} %get-tuple-element.210), channel_id=1, source_target_pairs={{4,7},{5,6},{6,5},{7,4},{12,15},{13,14},{14,13},{15,12},{20,23},{2... | collective-permute-start | bytes 2359304 | tf_op jit(solution)/shard_map/ppermute | solution.py:1149
  17.8 236.0 %copy-start.77 = (s32[2,1,1024]{2,1,0:T(1,128)S(1)}, s32[2,1,1024]{2,1,0:T(1,128)}, u32[]{:S(2)}) copy-start(s32[2,1,1024]{2,1,0:T(1,128)} %param.21) | copy-start | bytes 24580
  17.8 238.8 %copy-start.73 = (bf16[384,384,1]{1,0,2:T(8,128)(2,1)S(1)}, bf16[384,384,1]{1,0,2:T(8,128)(2,1)}, u32[]{:S(2)}) copy-start(bf16[384,384,1]{1,0,2:T(8,128)(2,1)} %constant.122) | copy-start | bytes 884740
  251.1 84.5 %collective-permute-start.1 = (bf16[1,1,256,1536]{3,2,1,0:T(8,128)(2,1)}, bf16[1,1,256,1536]{3,2,1,0:T(8,128)(2,1)}, u32[]{:S(2)}, u32[]{:S(2)}) collective-permute-start(bf16[1,1,256,1536]{3,2,1,0:T(8,128)(2,1)} %get-tuple-element.88), channel_id=1, source_target_pairs={{4,7},{5,6},{6,5},{7,4},{12,15},{13,14},{14,13},{15,12},{20,23},{2... | collective-permute-start | bytes 2359304 | tf_op jit(solution)/shard_map/ppermute | solution.py:1149
  256.6 11.5 copy-start.51
  256.6 16.2 %slice-start = ((s8[9437184]{0:T(1024)(128)(4,1)}), s8[4194304]{0:T(1024)(128)(4,1)S(1)}, s32[]{:S(2)}) async-start(s8[9437184]{0:T(1024)(128)(4,1)} %bitcast.169), calls=%async_computation | async-start | bytes 8388608
  256.6 16.2 %slice-start.1 = ((s8[9437184]{0:T(1024)(128)(4,1)}), s8[1048576]{0:T(1024)(128)(4,1)S(1)}, s32[]{:S(2)}) async-start(s8[9437184]{0:T(1024)(128)(4,1)} %bitcast.169), calls=%async_computation.1 | async-start | bytes 2097152
  264.0 8.8 slice-start.2
  305.8 28.6 %collective-permute-start.3 = (bf16[256,1536]{1,0:T(8,128)(2,1)S(1)}, bf16[256,1536]{1,0:T(8,128)(2,1)}, u32[]{:S(2)}, u32[]{:S(2)}) collective-permute-start(bf16[256,1536]{1,0:T(8,128)(2,1)S(1)} %get-tuple-element.89), channel_id=1, source_target_pairs={{4,7},{5,6},{6,5},{7,4},{12,15},{13,14},{14,13},{15,12},{20,23},{2... | collective-permute-start | bytes 2359304 | tf_op jit(solution)/shard_map/ppermute | solution.py:1149
  307.7 25.9 %copy-start.58 = (s32[256,1]{1,0:T(8,128)S(1)}, s32[256,1]{1,0:T(8,128)}, u32[]{:S(2)}) copy-start(s32[256,1]{1,0:T(8,128)} %copy.89.own_segment) | copy-start | bytes 3076
  331.4 16.7 %copy-start.25 = (bf16[1,1,256,1536]{3,2,1,0:T(8,128)(2,1)S(1)}, bf16[1,1,256,1536]{3,2,1,0:T(8,128)(2,1)}, u32[]{:S(2)}) copy-start(bf16[1,1,256,1536]{3,2,1,0:T(8,128)(2,1)} %get-tuple-element.88) | copy-start | bytes 2359300
  331.4 16.7 %collective-permute-start.2 = (bf16[256,1536]{1,0:T(8,128)(2,1)}, bf16[256,1536]{1,0:T(8,128)(2,1)}, u32[]{:S(2)}, u32[]{:S(2)}) collective-permute-start(bf16[256,1536]{1,0:T(8,128)(2,1)} %get-tuple-element.87), channel_id=1, source_target_pairs={{0,16},{1,17},{2,18},{3,19},{4,20},{5,21},{6,22},{7,23},{8,24},{9,... | collective-permute-start | bytes 2359304 | tf_op jit(solution)/shard_map/ppermute | solution.py:1133
  333.0 16.7 %copy-start.57 = (s32[256,1]{1,0:T(8,128)}, s32[256,1]{1,0:T(8,128)S(1)}, u32[]{:S(2)}) copy-start(s32[256,1]{1,0:T(8,128)S(1)} %copy.90.own_segment) | copy-start | bytes 3076
  335.6 83.9 %copy-start.27 = (bf16[256,1536]{1,0:T(8,128)(2,1)}, bf16[256,1536]{1,0:T(8,128)(2,1)S(1)}, u32[]{:S(2)}) copy-start(bf16[256,1536]{1,0:T(8,128)(2,1)S(1)} %broadcast_select_fusion.8) | copy-start | bytes 2359300
  350.9 8.2 copy-start.60
  416.3 77.3 %collective-permute-start.5 = (bf16[256,1536]{1,0:T(8,128)(2,1)}, bf16[256,1536]{1,0:T(8,128)(2,1)}, u32[]{:S(2)}, u32[]{:S(2)}) collective-permute-start(bf16[256,1536]{1,0:T(8,128)(2,1)} %get-tuple-element.93), channel_id=1, source_target_pairs={{4,7},{5,6},{6,5},{7,4},{12,15},{13,14},{14,13},{15,12},{20,23},{2... | collective-permute-start | bytes 2359304 | tf_op jit(solution)/shard_map/ppermute | solution.py:1149
  418.2 77.5 %collective-permute-start.4 = (bf16[256,1536]{1,0:T(8,128)(2,1)}, bf16[256,1536]{1,0:T(8,128)(2,1)}, u32[]{:S(2)}, u32[]{:S(2)}) collective-permute-start(bf16[256,1536]{1,0:T(8,128)(2,1)} %get-tuple-element.92), channel_id=1, source_target_pairs={{0,16},{1,17},{2,18},{3,19},{4,20},{5,21},{6,22},{7,23},{8,24},{9,... | collective-permute-start | bytes 2359304 | tf_op jit(solution)/shard_map/ppermute | solution.py:1133
  446.1 33.5 %copy-start.10 = (f32[256,1536]{1,0:T(8,128)S(1)}, f32[256,1536]{1,0:T(8,128)}, u32[]{:S(2)}) copy-start(f32[256,1536]{1,0:T(8,128)} %copy-done.9) | copy-start | bytes 4718596
  479.6 18.0 %slice-start.3 = ((s8[9437184]{0:T(1024)(128)(4,1)}), s8[4194304]{0:T(1024)(128)(4,1)S(1)}, s32[]{:S(2)}) async-start(s8[9437184]{0:T(1024)(128)(4,1)} %bitcast.171), calls=%async_computation.3 | async-start | bytes 8388608
  479.6 18.0 %slice-start.4 = ((s8[9437184]{0:T(1024)(128)(4,1)}), s8[1048576]{0:T(1024)(128)(4,1)S(1)}, s32[]{:S(2)}) async-start(s8[9437184]{0:T(1024)(128)(4,1)} %bitcast.171), calls=%async_computation.4 | async-start | bytes 2097152
  485.8 11.8 %slice-start.5 = ((s8[9437184]{0:T(1024)(128)(4,1)}), s8[4194304]{0:T(1024)(128)(4,1)S(1)}, s32[]{:S(2)}) async-start(s8[9437184]{0:T(1024)(128)(4,1)} %bitcast.171), calls=%async_computation.5 | async-start | bytes 8388608
  487.7 8.1 copy-start.26
  487.7 80.7 %collective-permute-start.7 = (bf16[256,1536]{1,0:T(8,128)(2,1)}, bf16[256,1536]{1,0:T(8,128)(2,1)}, u32[]{:S(2)}, u32[]{:S(2)}) collective-permute-start(bf16[256,1536]{1,0:T(8,128)(2,1)} %get-tuple-element.201), channel_id=1, source_target_pairs={{16,0},{17,1},{18,2},{19,3},{20,4},{21,5},{22,6},{23,7},{24,8},{25... | collective-permute-start | bytes 2359304 | tf_op jit(solution)/shard_map/ppermute | solution.py:1133
  630.3 7.9 copy-start.13
  630.3 7.9 copy-start.18
  630.3 7.9 copy-start.30
  630.4 7.9 copy-start.55
  640.3 18.3 %collective-permute-start.9 = (bf16[256,1536]{1,0:T(8,128)(2,1)S(1)}, bf16[256,1536]{1,0:T(8,128)(2,1)S(1)}, u32[]{:S(2)}, u32[]{:S(2)}) collective-permute-start(bf16[256,1536]{1,0:T(8,128)(2,1)S(1)} %convert_element_type.218), channel_id=1, source_target_pairs={{16,0},{17,1},{18,2},{19,3},{20,4},{21,5},{22,6},{23,7},{24,8},{25... | collective-permute-start | bytes 2359304 | tf_op jit(solution)/shard_map/ppermute | solution.py:1133
  641.9 489.6 %collective-permute-start.8 = (f32[256,1536]{1,0:T(8,128)}, f32[256,1536]{1,0:T(8,128)}, u32[]{:S(2)}, u32[]{:S(2)}) collective-permute-start(f32[256,1536]{1,0:T(8,128)} %get-tuple-element.199), channel_id=1, source_target_pairs={{4,7},{5,6},{6,5},{7,4},{12,15},{13,14},{14,13},{15,12},{20,23},{2... | collective-permute-start | bytes 4718600 | tf_op jit(solution)/shard_map/ppermute | solution.py:1149
  645.7 482.8 %collective-permute-start.6 = (bf16[2,256,1536]{2,1,0:T(8,128)(2,1)}, bf16[2,256,1536]{2,1,0:T(8,128)(2,1)}, u32[]{:S(2)}, u32[]{:S(2)}) collective-permute-start(bf16[2,256,1536]{2,1,0:T(8,128)(2,1)} %pad_maximum_fusion), channel_id=1, source_target_pairs={{4,7},{5,6},{6,5},{7,4},{12,15},{13,14},{14,13},{15,12},{20,23},{2... | collective-permute-start | bytes 4718600 | tf_op jit(solution)/shard_map/ppermute | solution.py:1149
  651.1 7.5 copy-start.35
  651.1 7.5 copy-start.36
  730.8 7.8 copy-start.8
  744.7 10.2 copy-start.39
  744.7 10.2 copy-start.40
  744.7 10.2 copy-start.46
  744.7 10.1 copy-start.47
  756.9 9.6 copy-start.86
  766.5 9.6 copy-start.42
  766.5 9.6 copy-start.62
  766.5 9.6 copy-start.67
  766.5 9.6 copy-start.85
  776.1 9.9 copy-start.69
  776.1 9.8 copy-start.70
  776.1 9.8 copy-start.71
  776.1 9.8 copy-start.72
  776.1 9.8 copy-start.90
  1119.1 38.1 %collective-permute-start.10 = (f32[256,1536]{1,0:T(8,128)S(1)}, f32[256,1536]{1,0:T(8,128)S(1)}, u32[]{:S(2)}, u32[]{:S(2)}) collective-permute-start(f32[256,1536]{1,0:T(8,128)S(1)} %add_select_fusion), channel_id=1, source_target_pairs={{4,7},{5,6},{6,5},{7,4},{12,15},{13,14},{14,13},{15,12},{20,23},{2... | collective-permute-start | bytes 4718600 | tf_op jit(solution)/shard_map/ppermute | solution.py:1149
  (63 other events, 207.2 us)

commit v6 on v5

--- a/solution.py
+++ b/solution.py
@@ -1263,7 +1263,7 @@
     return (grad_inputs, (grad_norm_attn, grad_norm_ffn[0]), operands)
 
 
-def reduce_gradients(operand_pairs, gains):
+def reduce_gradients(operand_pairs, gains, last_grads):
     (
         normed,
         qkv_low,
@@ -1284,18 +1284,25 @@
     gain_term = jnp.stack([gain.reshape(shards, rows) for gain in gains], axis=1)
     gain_term = gain_term.reshape(shards, 1, 2 * rows).astype(jnp.bfloat16)
     gain_term = jnp.pad(gain_term, ((0, 0), (0, 15), (0, gain_width(rows) - 2 * rows)))
+    gain_term, last_grads = lax.optimization_barrier((gain_term, last_grads))
+    cut = up_low.shape[1] // 4 * 3
     leading = [
         product(hidden, branch_grad),
         product(normed_mid, gate_low),
-        product(normed_mid, up_low),
+        product(normed_mid, up_low[:, :cut]),
         gain_term.reshape(shards * 16, -1),
     ]
-    trailing = [product(normed, from_tiles(qkv_low)), product(from_tiles(attended), attn_grad)]
+    trailing = [
+        product(normed_mid, up_low[:, cut:]),
+        product(from_tiles(attended), attn_grad),
+        product(normed, from_tiles(qkv_low)),
+    ]
     totals = [total.astype(jnp.float32) for total in reduce_terms(leading, trailing, shards)]
     members = lax.axis_size("replica")
     for bit in range(PARTS.bit_length() - 1, members.bit_length() - 1):
         totals = [total + swap(total, bit) for total in totals]
-    down, gate, up, own_gains, qkv, out = totals
+    down, gate, up, own_gains, up_rest, out, qkv = totals
+    up = jnp.concatenate([up, up_rest], axis=1)
     return (
         own_gains[0, :rows],
         qkv[:, : QH * HD],
@@ -1306,7 +1313,7 @@
         gate,
         up,
         down,
-    )
+    ), last_grads
 
 
 def body(
@@ -1391,18 +1398,16 @@
         gain_sums = gains if gain_sums is None else jax.tree.map(jnp.add, gain_sums, gains)
         operand_ticks.append(operands)
     edge_operands = choose(operand_ticks[micro_count], operand_ticks[0])
-    totals = reduce_gradients(operand_ticks[1:micro_count] + [edge_operands], gain_sums)
+    flows = [mirror(choose(flow_ticks[m + 1], flow_ticks[m])) for m in range(micro_count)]
+    totals, flows[-1] = reduce_gradients(
+        operand_ticks[1:micro_count] + [edge_operands], gain_sums, flows[-1]
+    )
     section_outputs = mirror(
         jnp.stack(
             [choose(result_ticks[index], result_ticks[index + 1]) for index in range(micro_count)]
         )
     )
-    input_grads = jnp.stack(
-        [
-            mirror(choose(flow_ticks[index + 1], flow_ticks[index]))
-            for index in range(micro_count)
-        ]
-    )
+    input_grads = jnp.stack(flows)
     return (section_outputs[None, :, None], input_grads[None, :, None]) + tuple(
         total[None] for total in totals
     )

time: 1170 us -> 1150 us (0.983)
  waiting for transfers between devices: 42.3 us -> 18.3 us
    ppermute x7, waiting for transfers between devices: 24 us -> 0.02 us  [mirror(): moved = lax.ppermute(x, ('replica', 'shard'), pairs)]
    unnamed x203 -> x216, local copies, waits for them, and re-layouts: 23.3 us -> 26.5 us
    dot_general x5 -> x6, matrix products: 43.9 us -> 44.5 us  [row_product(): jnp.einsum('td,tq->dq', left, right, preferred_element_type=jnp.float32)]
  transfers between devices with their start and end apart: 11 -> 11, of which waited for: 3 -> 2; matrix products, arithmetic and copies ran while one was open for 13% -> 11% of each run, Pallas kernels for 66% -> 40%
where the time goes in v6:
time: 1150 us; the launch traced here: 1140 us
  Pallas kernels  887 us (77%)
  matrix products  97.9 us (9%)
  other arithmetic  70.1 us (6%)
  local copies, waits for them, and re-layouts  38 us (3%)
  starting transfers between devices  29.8 us (3%)
  waiting for transfers between devices  18.3 us (2%)
    pallas_call x1, Pallas kernels, reduce_terms(): pl.pallas_call(functools.partial(reduce_kernel, shards, (tuple(leads), tu...  315 us
    pallas_call x1, Pallas kernels, gather_weights(): pl.pallas_call(functools.partial(gather_kernel, shards, tuple(chunks), co...  227 us
    pallas_call x3, Pallas kernels, attend_back(): pl.pallas_call(functools.partial(attend_back_kernel, shards, hops, rows),...  106 us
    pallas_call x3, Pallas kernels, attend(): pl.pallas_call(functools.partial(attend_kernel, shards, hops, rows), out_...  91.5 us
    pallas_call x3, Pallas kernels, feed_back(): pl.pallas_call(feed_back_kernel, grid=(units // block,), out_shape=[jax.S...  75.8 us
    pallas_call x3, Pallas kernels, feed_forward(): pl.pallas_call(feed_kernel, grid=(units // block,), out_shape=[jax.ShapeD...  71.2 us
    dot_general x6, matrix products, row_product(): jnp.einsum('td,tq->dq', left, right, preferred_element_type=jnp.float32)  44.5 us
    select_n x18, other arithmetic, choose(): jnp.where(first_section, a, b)  26.9 us
  transfers between devices with their start and end apart: 11, of which 2 were waited for; matrix products, arithmetic and copies ran while one was open for 11% of the time, Pallas kernels for 40%

profile of v6, /device:TPU:13, one launch (start us, length us, event | category | flops | bytes accessed | tf_op | source)
XLA Modules:
  0.0 1143.1 jit_solution(3019195838044454220)
XLA Ops:
  0.7 2.7 fusion.111
  3.4 3.2 collective-permute-start
  17.8 227.4 %gather_weights.1 = (bf16[1536,3072]{1,0:T(8,128)(2,1)S(1)}, bf16[1536,1536]{1,0:T(8,128)(2,1)S(1)}, bf16[1536,4096]{1,0:T(8,128)(2,1)}, bf16[1536,4096]{1,0:T(8...) custom-call(bf16[384,3072]{1,0:T(8,128)(2,1)S(1)} %copy-done.5, bf16[384,1536]{1,0:T(8,128)(2,1)S(1)} %bitcast.168, ...), custom_call_target="tpu_custom_call" | custom-call | tf_op jit(solution)/shard_map/gather_weights/pallas_call | solution.py:186
  245.2 2.2 copy-done
  247.4 3.7 copy-done.7
  251.1 2.7 collective-permute-start.1
  256.6 6.7 convolution_convert_fusion.5
  264.0 4.2 fusion.85
  272.8 4.4 fusion.87.raw
  277.2 28.6 %attend.3 = (bf16[256,1536]{1,0:T(8,128)(2,1)}, bf16[768,1536]{1,0:T(8,128)(2,1)}, bf16[256,1536]{1,0:T(8,128)(2,1)}, f32[256,128]{1,0:T(8,128)}) custom-call(f32[256,3072]{1,0:T(8,128)} %fusion.87.raw, f32[256,384]{1,0:T(8,128)} %get-tuple-element.241.cosine, f32[256,384]{1,0:T(8,128)} %get-tuple-element.231.sine, s32[256,1]{1,0:T(8,128)} %copy.89.own_segment, ...), custom_call_target="tpu_custom_call" | custom-call | tf_op jit(solution)/shard_map/attend/pallas_call | solution.py:777
  307.7 23.7 %feed_forward.3 = (f32[256,1536]{1,0:T(8,128)}, bf16[256,1536]{1,0:T(8,128)(2,1)}, bf16[256,4096]{1,0:T(8,128)(2,1)}, bf16[256,4096]{1,0:T(8,128)(2,1)}, bf16[25...) custom-call(f32[256,1536]{1,0:T(8,128)} %select_bitcast_fusion.2.inputs, bf16[256,1536]{1,0:T(8,128)(2,1)} %get-tuple-element.85.attended, ...), custom_call_target="tpu_custom_call" | custom-call | flops 10871635968 | bytes 54263808 | tf_op jit(solution)/shard_map/feed_forward/pallas_call | solution.py:993
  335.7 12.5 %collective-permute-done.2 = bf16[256,1536]{1,0:T(8,128)(2,1)} collective-permute-done((bf16[256,1536]{1,0:T(8,128)(2,1)}, bf16[256,1536]{1,0:T(8,128)(2,1)}, u32[]{:S(2)}, u32[]{:S(2)}) %collective-permute-start.2) | collective-permute-done | bytes 786464 | tf_op jit(solution)/shard_map/ppermute | solution.py:1133
  351.0 8.2 fusion.114.raw
  359.2 33.4 %attend.4 = (bf16[256,1536]{1,0:T(8,128)(2,1)}, bf16[768,1536]{1,0:T(8,128)(2,1)}, bf16[256,1536]{1,0:T(8,128)(2,1)}, f32[256,128]{1,0:T(8,128)}) custom-call(f32[256,3072]{1,0:T(8,128)} %fusion.114.raw, f32[256,384]{1,0:T(8,128)} %get-tuple-element.234.cosine, f32[256,384]{1,0:T(8,128)} %get-tuple-element.230.sine, ...), custom_call_target="tpu_custom_call" | custom-call | tf_op jit(solution)/shard_map/attend/pallas_call | solution.py:777
  392.6 23.7 %feed_forward.4 = (f32[256,1536]{1,0:T(8,128)}, bf16[256,1536]{1,0:T(8,128)(2,1)}, bf16[256,4096]{1,0:T(8,128)(2,1)}, bf16[256,4096]{1,0:T(8,128)(2,1)}, bf16[25...) custom-call(f32[256,1536]{1,0:T(8,128)} %copy-done.9, bf16[256,1536]{1,0:T(8,128)(2,1)} %get-tuple-element.94.attended, ...), custom_call_target="tpu_custom_call" | custom-call | flops 10871635968 | bytes 54263808 | tf_op jit(solution)/shard_map/feed_forward/pallas_call | solution.py:993
  420.9 25.3 %feed_back.3 = (bf16[256,4096]{1,0:T(8,128)(2,1)}, bf16[256,4096]{1,0:T(8,128)(2,1)}, f32[256,1536]{1,0:T(8,128)}, bf16[256,1536]{1,0:T(8,128)(2,1)}, bf16[256,1536]{1,0:T(8,128)(2,1)}, /*index=5*/f32[1,1536]{1,0:T(1,128)}) custom-call(f32[256,1536]{1,0:T(8,128)} %select_select_fusion.grads, f32[256,1536]{1,0:T(8,128)} %get-tuple-element.101.middle, ...), custom_call_target="tpu_custom_call" | custom-call | flops 10871635968 | bytes 57147392 | tf_op jit(solution)/shard_map/feed_back/pallas_call | solution.py:1089
  446.2 33.5 %attend_back.3 = bf16[256,3072]{1,0:T(8,128)(2,1)} custom-call(bf16[256,1536]{1,0:T(8,128)(2,1)} %get-tuple-element.105.queries, bf16[768,1536]{1,0:T(8,128)(2,1)} %get-tuple-element.106.window, f32[256,128]{1,0:T(8,128)} %get-tuple-element.107.log_total, bf16[256,1536]{1,0:T(8,128)(2,1)} %get-tuple-element.108.grads, f32[256,384]{1,0:T(8,128)} %get-tuple-element.234.cosine, ...), custom_call_target="tpu_custom_call" | custom-call | tf_op jit(solution)/shard_map/attend_back/pallas_call | solution.py:919
  479.7 6.1 multiply_reduce_fusion.3
  487.8 5.9 collective-permute-start.7
  493.7 2.1 broadcast_select_fusion.8
  497.7 4.4 fusion.108.raw
  502.1 29.5 %attend.5 = (bf16[256,1536]{1,0:T(8,128)(2,1)}, bf16[768,1536]{1,0:T(8,128)(2,1)}, bf16[256,1536]{1,0:T(8,128)(2,1)}, f32[256,128]{1,0:T(8,128)}) custom-call(f32[256,3072]{1,0:T(8,128)} %fusion.108.raw, f32[256,384]{1,0:T(8,128)} %get-tuple-element.242.cosine, f32[256,384]{1,0:T(8,128)} %get-tuple-element.232.sine, s32[256,1]{1,0:T(8,128)} %copy-done.62, ...), custom_call_target="tpu_custom_call" | custom-call | tf_op jit(solution)/shard_map/attend/pallas_call | solution.py:777
  531.7 23.8 %feed_forward.5 = (f32[256,1536]{1,0:T(8,128)}, bf16[256,1536]{1,0:T(8,128)(2,1)}, bf16[256,4096]{1,0:T(8,128)(2,1)}, bf16[256,4096]{1,0:T(8,128)(2,1)}, bf16[25...) custom-call(f32[256,1536]{1,0:T(8,128)} %copy-done.12, bf16[256,1536]{1,0:T(8,128)(2,1)} %get-tuple-element.98.attended, ...), custom_call_target="tpu_custom_call" | custom-call | flops 10871635968 | bytes 54263808 | tf_op jit(solution)/shard_map/feed_forward/pallas_call | solution.py:993
  555.5 2.2 broadcast_select_fusion.17.queries
  557.8 3.3 broadcast_select_fusion.4.up
  568.4 2.9 fusion.109
  571.3 25.3 %feed_back.4 = (bf16[256,4096]{1,0:T(8,128)(2,1)}, bf16[256,4096]{1,0:T(8,128)(2,1)}, f32[256,1536]{1,0:T(8,128)}, bf16[256,1536]{1,0:T(8,128)(2,1)}, bf16[256,1536]{1,0:T(8,128)(2,1)}, /*index=5*/f32[1,1536]{1,0:T(1,128)}) custom-call(f32[256,1536]{1,0:T(8,128)} %get-tuple-element.204.grads, f32[256,1536]{1,0:T(8,128)} %broadcast_select_fusion.18.middle, ...), custom_call_target="tpu_custom_call" | custom-call | flops 10871635968 | bytes 57147392 | tf_op jit(solution)/shard_map/feed_back/pallas_call | solution.py:1089
  596.5 33.9 %attend_back.4 = bf16[256,3072]{1,0:T(8,128)(2,1)} custom-call(bf16[256,1536]{1,0:T(8,128)(2,1)} %broadcast_select_fusion.17.queries, bf16[768,1536]{1,0:T(8,128)(2,1)} %broadcast_select_fusion.window, f32[256,128]{1,0:T(8,128)} %broadcast_select_fusion.19.log_total, bf16[256,1536]{1,0:T(8,128)(2,1)} %get-tuple-element.123.grads, ...), custom_call_target="tpu_custom_call" | custom-call | tf_op jit(solution)/shard_map/attend_back/pallas_call | solution.py:919
  630.5 7.8 multiply_reduce_fusion.2
  645.9 3.5 collective-permute-start.6
  653.0 5.7 collective-permute-done.9
  665.2 25.2 %feed_back.5 = (bf16[256,4096]{1,0:T(8,128)(2,1)}, bf16[256,4096]{1,0:T(8,128)(2,1)}, f32[256,1536]{1,0:T(8,128)}, bf16[256,1536]{1,0:T(8,128)(2,1)}, bf16[256,1536]{1,0:T(8,128)(2,1)}, /*index=5*/f32[1,1536]{1,0:T(1,128)}) custom-call(f32[256,1536]{1,0:T(8,128)} %fusion.9.grads, f32[256,1536]{1,0:T(8,128)} %get-tuple-element.101.middle, ...), custom_call_target="tpu_custom_call" | custom-call | flops 10871635968 | bytes 57147392 | tf_op jit(solution)/shard_map/feed_back/pallas_call | solution.py:1089
  690.4 38.7 %attend_back.5 = bf16[256,3072]{1,0:T(8,128)(2,1)} custom-call(bf16[256,1536]{1,0:T(8,128)(2,1)} %get-tuple-element.105.queries, bf16[768,1536]{1,0:T(8,128)(2,1)} %get-tuple-element.106.window, f32[256,128]{1,0:T(8,128)} %get-tuple-element.107.log_total, bf16[256,1536]{1,0:T(8,128)(2,1)} %get-tuple-element.124.grads, f32[256,384]{1,0:T(8,128)} %get-tuple-element.234.cosine, ...), custom_call_target="tpu_custom_call" | custom-call | tf_op jit(solution)/shard_map/attend_back/pallas_call | solution.py:919
  731.0 5.6 multiply_reduce_fusion
  743.1 4.5 collective-permute-start.10
  747.7 7.6 convolution_convert_fusion.2.refs_6_
  758.1 7.6 convolution_convert_fusion.3.refs_2_
  765.7 9.7 convolution_convert_fusion.refs_1_
  775.4 9.8 convolution_convert_fusion.1.refs_0_
  786.9 5.1 convolution_convert_fusion.6.refs_4_
  793.6 4.8 convolution_convert_fusion.4.refs_5_
  798.4 2.8 select_bitcast_fusion.1
  802.8 2.8 broadcast_select_fusion.7
  806.2 314.6 %reduce_terms.1 = (bf16[1024,1536]{1,0:T(8,128)(2,1)}, bf16[384,4096]{1,0:T(8,128)(2,1)}, bf16[384,3072]{1,0:T(8,128)(2,1)}, bf16[16,1024]{1,0:T(8,128)(2,1)}, b...) custom-call(bf16[4096,1536]{1,0:T(8,128)(2,1)} %convolution_convert_, ...), custom_call_target="tpu_custom_call" | custom-call | tf_op jit(solution)/shard_map/reduce_terms/pallas_call | solution.py:488
  1120.9 2.2 convert_element_type.247
  1127.4 3.6 bitcast_convert_fusion
  1131.0 3.5 bitcast_convert_fusion.1
  1137.5 3.5 fusion.8
  (324 shorter events, 86.8 us)
Async XLA Ops:
  3.4 265.8 %collective-permute-start = (bf16[1,1,256,1536]{3,2,1,0:T(8,128)(2,1)}, bf16[1,1,256,1536]{3,2,1,0:T(8,128)(2,1)}, u32[]{:S(2)}, u32[]{:S(2)}) collective-permute-start(bf16[1,1,256,1536]{3,2,1,0:T(8,128)(2,1)} %get-tuple-element.216), channel_id=1, source_target_pairs={{4,7},{5,6},{6,5},{7,4},{12,15},{13,14},{14,13},{15,12},{20,23},{2... | collective-permute-start | bytes 2359304 | tf_op jit(solution)/shard_map/ppermute | solution.py:1149
  17.8 236.0 %copy-start.84 = (s32[2,1,1024]{2,1,0:T(1,128)S(1)}, s32[2,1,1024]{2,1,0:T(1,128)}, u32[]{:S(2)}) copy-start(s32[2,1,1024]{2,1,0:T(1,128)} %param.21) | copy-start | bytes 24580
  17.8 238.8 %copy-start.81 = (bf16[384,384,1]{1,0,2:T(8,128)(2,1)S(1)}, bf16[384,384,1]{1,0,2:T(8,128)(2,1)}, u32[]{:S(2)}) copy-start(bf16[384,384,1]{1,0,2:T(8,128)(2,1)} %constant.122) | copy-start | bytes 884740
  251.1 84.5 %collective-permute-start.1 = (bf16[1,1,256,1536]{3,2,1,0:T(8,128)(2,1)}, bf16[1,1,256,1536]{3,2,1,0:T(8,128)(2,1)}, u32[]{:S(2)}, u32[]{:S(2)}) collective-permute-start(bf16[1,1,256,1536]{3,2,1,0:T(8,128)(2,1)} %get-tuple-element.91), channel_id=1, source_target_pairs={{4,7},{5,6},{6,5},{7,4},{12,15},{13,14},{14,13},{15,12},{20,23},{2... | collective-permute-start | bytes 2359304 | tf_op jit(solution)/shard_map/ppermute | solution.py:1149
  256.6 11.6 %copy-start.57 = (bf16[2,1,256,1536]{3,2,1,0:T(8,128)(2,1)S(1)}, bf16[2,1,256,1536]{3,2,1,0:T(8,128)(2,1)}, u32[]{:S(2)}) copy-start(bf16[2,1,256,1536]{3,2,1,0:T(8,128)(2,1)} %param.31) | copy-start | bytes 4718596
  256.6 16.2 %slice-start = ((s8[9437184]{0:T(1024)(128)(4,1)}), s8[4194304]{0:T(1024)(128)(4,1)S(1)}, s32[]{:S(2)}) async-start(s8[9437184]{0:T(1024)(128)(4,1)} %bitcast.170), calls=%async_computation | async-start | bytes 8388608
  256.6 16.2 %slice-start.1 = ((s8[9437184]{0:T(1024)(128)(4,1)}), s8[1048576]{0:T(1024)(128)(4,1)S(1)}, s32[]{:S(2)}) async-start(s8[9437184]{0:T(1024)(128)(4,1)} %bitcast.170), calls=%async_computation.1 | async-start | bytes 2097152
  264.0 8.8 slice-start.2
  305.8 28.6 %collective-permute-start.3 = (bf16[256,1536]{1,0:T(8,128)(2,1)S(1)}, bf16[256,1536]{1,0:T(8,128)(2,1)}, u32[]{:S(2)}, u32[]{:S(2)}) collective-permute-start(bf16[256,1536]{1,0:T(8,128)(2,1)S(1)} %get-tuple-element.92), channel_id=1, source_target_pairs={{4,7},{5,6},{6,5},{7,4},{12,15},{13,14},{14,13},{15,12},{20,23},{2... | collective-permute-start | bytes 2359304 | tf_op jit(solution)/shard_map/ppermute | solution.py:1149
  307.7 26.0 %copy-start.63 = (s32[256,1]{1,0:T(8,128)S(1)}, s32[256,1]{1,0:T(8,128)}, u32[]{:S(2)}) copy-start(s32[256,1]{1,0:T(8,128)} %copy.89.own_segment) | copy-start | bytes 3076
  331.4 16.7 %copy-start.28 = (bf16[1,1,256,1536]{3,2,1,0:T(8,128)(2,1)S(1)}, bf16[1,1,256,1536]{3,2,1,0:T(8,128)(2,1)}, u32[]{:S(2)}) copy-start(bf16[1,1,256,1536]{3,2,1,0:T(8,128)(2,1)} %get-tuple-element.91) | copy-start | bytes 2359300
  331.4 16.7 %collective-permute-start.2 = (bf16[256,1536]{1,0:T(8,128)(2,1)}, bf16[256,1536]{1,0:T(8,128)(2,1)}, u32[]{:S(2)}, u32[]{:S(2)}) collective-permute-start(bf16[256,1536]{1,0:T(8,128)(2,1)} %get-tuple-element.90), channel_id=1, source_target_pairs={{0,16},{1,17},{2,18},{3,19},{4,20},{5,21},{6,22},{7,23},{8,24},{9,... | collective-permute-start | bytes 2359304 | tf_op jit(solution)/shard_map/ppermute | solution.py:1133
  333.0 16.8 %copy-start.62 = (s32[256,1]{1,0:T(8,128)}, s32[256,1]{1,0:T(8,128)S(1)}, u32[]{:S(2)}) copy-start(s32[256,1]{1,0:T(8,128)S(1)} %copy.90.own_segment) | copy-start | bytes 3076
  335.6 83.9 %copy-start.30 = (bf16[256,1536]{1,0:T(8,128)(2,1)}, bf16[256,1536]{1,0:T(8,128)(2,1)S(1)}, u32[]{:S(2)}) copy-start(bf16[256,1536]{1,0:T(8,128)(2,1)S(1)} %broadcast_select_fusion.9) | copy-start | bytes 2359300
  351.0 8.2 copy-start.67
  416.3 77.4 %collective-permute-start.5 = (bf16[256,1536]{1,0:T(8,128)(2,1)}, bf16[256,1536]{1,0:T(8,128)(2,1)}, u32[]{:S(2)}, u32[]{:S(2)}) collective-permute-start(bf16[256,1536]{1,0:T(8,128)(2,1)} %get-tuple-element.96), channel_id=1, source_target_pairs={{4,7},{5,6},{6,5},{7,4},{12,15},{13,14},{14,13},{15,12},{20,23},{2... | collective-permute-start | bytes 2359304 | tf_op jit(solution)/shard_map/ppermute | solution.py:1149
  418.2 77.6 %collective-permute-start.4 = (bf16[256,1536]{1,0:T(8,128)(2,1)}, bf16[256,1536]{1,0:T(8,128)(2,1)}, u32[]{:S(2)}, u32[]{:S(2)}) collective-permute-start(bf16[256,1536]{1,0:T(8,128)(2,1)} %get-tuple-element.95), channel_id=1, source_target_pairs={{0,16},{1,17},{2,18},{3,19},{4,20},{5,21},{6,22},{7,23},{8,24},{9,... | collective-permute-start | bytes 2359304 | tf_op jit(solution)/shard_map/ppermute | solution.py:1133
  446.2 33.5 %copy-start.10 = (f32[256,1536]{1,0:T(8,128)S(1)}, f32[256,1536]{1,0:T(8,128)}, u32[]{:S(2)}) copy-start(f32[256,1536]{1,0:T(8,128)} %copy-done.9) | copy-start | bytes 4718596
  479.7 18.0 %slice-start.3 = ((s8[9437184]{0:T(1024)(128)(4,1)}), s8[4194304]{0:T(1024)(128)(4,1)S(1)}, s32[]{:S(2)}) async-start(s8[9437184]{0:T(1024)(128)(4,1)} %bitcast.172), calls=%async_computation.3 | async-start | bytes 8388608
  479.7 18.0 %slice-start.4 = ((s8[9437184]{0:T(1024)(128)(4,1)}), s8[1048576]{0:T(1024)(128)(4,1)S(1)}, s32[]{:S(2)}) async-start(s8[9437184]{0:T(1024)(128)(4,1)} %bitcast.172), calls=%async_computation.4 | async-start | bytes 2097152
  485.8 11.9 %slice-start.5 = ((s8[9437184]{0:T(1024)(128)(4,1)}), s8[4194304]{0:T(1024)(128)(4,1)S(1)}, s32[]{:S(2)}) async-start(s8[9437184]{0:T(1024)(128)(4,1)} %bitcast.172), calls=%async_computation.5 | async-start | bytes 8388608
  487.8 8.0 copy-start.29
  487.8 80.6 %collective-permute-start.7 = (bf16[256,1536]{1,0:T(8,128)(2,1)}, bf16[256,1536]{1,0:T(8,128)(2,1)}, u32[]{:S(2)}, u32[]{:S(2)}) collective-permute-start(bf16[256,1536]{1,0:T(8,128)(2,1)} %get-tuple-element.207), channel_id=1, source_target_pairs={{16,0},{17,1},{18,2},{19,3},{20,4},{21,5},{22,6},{23,7},{24,8},{25... | collective-permute-start | bytes 2359304 | tf_op jit(solution)/shard_map/ppermute | solution.py:1133
  630.5 7.9 copy-start.13
  630.5 7.9 copy-start.21
  630.5 7.9 copy-start.34
  630.5 7.9 copy-start.60
  640.5 18.3 %collective-permute-start.9 = (bf16[256,1536]{1,0:T(8,128)(2,1)S(1)}, bf16[256,1536]{1,0:T(8,128)(2,1)S(1)}, u32[]{:S(2)}, u32[]{:S(2)}) collective-permute-start(bf16[256,1536]{1,0:T(8,128)(2,1)S(1)} %convert_element_type.222), channel_id=1, source_target_pairs={{16,0},{17,1},{18,2},{19,3},{20,4},{21,5},{22,6},{23,7},{24,8},{25... | collective-permute-start | bytes 2359304 | tf_op jit(solution)/shard_map/ppermute | solution.py:1133
  642.1 159.1 %collective-permute-start.8 = (f32[256,1536]{1,0:T(8,128)}, f32[256,1536]{1,0:T(8,128)}, u32[]{:S(2)}, u32[]{:S(2)}) collective-permute-start(f32[256,1536]{1,0:T(8,128)} %get-tuple-element.205), channel_id=1, source_target_pairs={{4,7},{5,6},{6,5},{7,4},{12,15},{13,14},{14,13},{15,12},{20,23},{2... | collective-permute-start | bytes 4718600 | tf_op jit(solution)/shard_map/ppermute | solution.py:1149
  645.9 152.5 %collective-permute-start.6 = (bf16[2,256,1536]{2,1,0:T(8,128)(2,1)}, bf16[2,256,1536]{2,1,0:T(8,128)(2,1)}, u32[]{:S(2)}, u32[]{:S(2)}) collective-permute-start(bf16[2,256,1536]{2,1,0:T(8,128)(2,1)} %pad_maximum_fusion), channel_id=1, source_target_pairs={{4,7},{5,6},{6,5},{7,4},{12,15},{13,14},{14,13},{15,12},{20,23},{2... | collective-permute-start | bytes 4718600 | tf_op jit(solution)/shard_map/ppermute | solution.py:1149
  651.3 7.5 copy-start.38
  651.3 7.5 copy-start.39
  743.1 59.6 %collective-permute-start.10 = (f32[256,1536]{1,0:T(8,128)}, f32[256,1536]{1,0:T(8,128)}, u32[]{:S(2)}, u32[]{:S(2)}) collective-permute-start(f32[256,1536]{1,0:T(8,128)} %add_select_fusion), channel_id=1, source_target_pairs={{4,7},{5,6},{6,5},{7,4},{12,15},{13,14},{14,13},{15,12},{20,23},{2... | collective-permute-start | bytes 4718600 | tf_op jit(solution)/shard_map/ppermute | solution.py:1149
  747.7 7.7 copy-start.43
  747.7 7.7 copy-start.44
  747.7 7.6 copy-start.50
  747.7 7.6 copy-start.51
  755.8 9.9 copy-start.52
  758.1 7.6 copy-start.94
  765.7 9.7 copy-start.48
  765.7 9.7 copy-start.70
  765.7 9.7 copy-start.75
  765.7 9.7 copy-start.92
  775.4 9.8 copy-start.85
  775.4 9.8 copy-start.86
  775.4 9.8 copy-start.87
  775.4 9.9 copy-start.15
  775.4 9.9 copy-start.17
  (70 other events, 237.7 us)

commit v7 on v6

--- a/solution.py
+++ b/solution.py
@@ -52,7 +52,7 @@
     pl.semaphore_wait(barrier, 2 + (place > 0).astype(jnp.int32) + (place < shards - 1).astype(jnp.int32))
 
 
-def gather_kernel(shards, chunks, count, *refs):
+def gather_kernel(shards, chunks, count, turns, matrix, *refs):
     pieces, wholes = refs[:count], refs[count : 2 * count]
     held = refs[2 * count : 3 * count]
     (local_sem, own_send, pass_send, line_recv, x_send, x_recv, core_send, core_recv) = refs[
@@ -86,7 +86,7 @@
     def own(j):
         index, first, length = chunks[j]
         width = pieces[index].shape[1] // PARTS
-        source = pieces[index].at[
+        source = (held if turns[index] else pieces)[index].at[
             pl.ds(first, length), pl.ds(pl.multiple_of(part * width, width), width)
         ]
         for slot, way in enumerate((1, -1)):
@@ -132,13 +132,33 @@
                     theirs, theirs, core_send.at[j, block, 1], core_recv.at[j, block, 1], {"replica": member ^ 1}
                 )
 
+    def prepare(index):
+        loads(index).wait()
+        block = held[index]
+        if turns[index] == "columns":
+            span = matrix.shape[0]
+            for at in range(0, block.shape[1], span):
+                part_value = dot(block[:, at : at + span], matrix[...], NN)
+                block[:, at : at + span] = part_value.astype(block.dtype)
+        elif turns[index] == "rows":
+            span = matrix.shape[0]
+            for at in range(0, block.shape[0], span):
+                part_value = dot(matrix[...], block[at : at + span, :], TN)
+                block[at : at + span, :] = part_value.astype(block.dtype)
+        stores(index).start()
+
     total = len(chunks)
-    for step in range(total + shards + 1):
+    waiting = list(range(count))
+    for step in range(max(total + shards + 1, count + 1)):
         if step < total:
+            index = chunks[step][0]
+            if turns[index] and index in waiting:
+                waiting.remove(index)
+                prepare(index)
             own(step)
-        if 1 <= step <= count:
-            loads(step - 1).wait()
-            stores(step - 1).start()
+        if 1 <= step <= count and step - 1 in waiting:
+            waiting.remove(step - 1)
+            prepare(step - 1)
         for k in range(1, shards):
             if 0 <= step - k < total:
                 hop(step - k, k)
@@ -172,7 +192,7 @@
         stores(index).wait()
 
 
-def gather_weights(pieces, shards, pace=192 * 1024):
+def gather_weights(pieces, turns, shards, pace=192 * 1024):
     chunks = []
     for index, piece in enumerate(pieces):
         rows, width = piece.shape
@@ -184,9 +204,9 @@
     count, total = len(pieces), len(chunks)
     dma = pltpu.SemaphoreType.DMA
     return pl.pallas_call(
-        functools.partial(gather_kernel, shards, tuple(chunks), count),
+        functools.partial(gather_kernel, shards, tuple(chunks), count, tuple(turns)),
         out_shape=[jax.ShapeDtypeStruct((shards * p.shape[0], p.shape[1]), p.dtype) for p in pieces],
-        in_specs=[pl.BlockSpec(memory_space=pl.ANY)] * count,
+        in_specs=[pl.BlockSpec(memory_space=pltpu.VMEM)] + [pl.BlockSpec(memory_space=pl.ANY)] * count,
         out_specs=[pl.BlockSpec(memory_space=pl.ANY)] * count,
         scratch_shapes=[pltpu.VMEM(p.shape, p.dtype) for p in pieces]
         + [
@@ -201,7 +221,7 @@
         ],
         compiler_params=pltpu.CompilerParams(collective_id=0, has_side_effects=True, vmem_limit_bytes=24 * 1024 * 1024),
         name="gather_weights",
-    )(*pieces)
+    )(jnp.asarray(tile_matrix(), jnp.bfloat16), *pieces)
 
 
 def add_rows(target, left, right, rows):
@@ -516,18 +536,6 @@
 def tile_matrix():
     order = tile_order()
     return (np.arange(4 * HD)[:, None] == order[None, :]).astype(np.float32)
-
-
-def to_tiles(x):
-    matrix = jnp.asarray(tile_matrix(), jnp.bfloat16)
-    span = 4 * HD
-    return jnp.concatenate(
-        [
-            jnp.dot(x[:, i : i + span], matrix, preferred_element_type=jnp.float32).astype(x.dtype)
-            for i in range(0, x.shape[1], span)
-        ],
-        axis=1,
-    )
 
 
 def from_tiles(x):
@@ -1160,14 +1168,19 @@
     shards = lax.axis_size("shard")
     gains = jnp.concatenate([norm_attn, norm_ffn])
     gains = jnp.pad(gains[None], ((0, 15), (0, gain_width(rows) - 2 * rows)))
-    w_qkv = to_tiles(jnp.concatenate([w_query, w_key, w_value], axis=1))
-    w_qkv, w_out, w_gate, w_up, w_down, gains = gather_weights(
-        [w_qkv, w_out, w_gate, w_up, w_down, gains], shards
+    w_qkv = jnp.concatenate([w_query, w_key, w_value], axis=1)
+    inside_rows = rows % (4 * HD) == 0
+    w_gate, w_up, w_down, gains, w_out, w_qkv = gather_weights(
+        [w_gate, w_up, w_down, gains, w_out, w_qkv],
+        [None, None, None, None, "rows" if inside_rows else None, "columns"],
+        shards,
     )
+    if not inside_rows:
+        w_out = rows_to_tiles(w_out)
     gains = gains.reshape(shards, 16, -1)[:, 0].astype(jnp.float32)
     norm_attn = gains[:, :rows].reshape(-1)
     norm_ffn = gains[:, rows : 2 * rows].reshape(-1)
-    return norm_attn, w_qkv, rows_to_tiles(w_out), norm_ffn, w_gate, w_up, w_down
+    return norm_attn, w_qkv, w_out, norm_ffn, w_gate, w_up, w_down
 
 
 def sequence_tables(segment, rows, hops):

time: 1150 us -> 1140 us (level)
    unnamed x216 -> x198, local copies, waits for them, and re-layouts: 26.5 us -> 20.5 us
where the time goes in v7:
time: 1140 us
  Pallas kernels  891 us (78%)
  matrix products  88.4 us (8%)
  other arithmetic  72.2 us (6%)
  local copies, waits for them, and re-layouts  33.4 us (3%)
  starting transfers between devices  32.4 us (3%)
  waiting for transfers between devices  15.7 us (1%)
    pallas_call x1, Pallas kernels, reduce_terms(): pl.pallas_call(functools.partial(reduce_kernel, shards, (tuple(leads), tu...  315 us
    pallas_call x1, Pallas kernels, gather_weights(): pl.pallas_call(functools.partial(gather_kernel, shards, tuple(chunks), co...  230 us
    pallas_call x3, Pallas kernels, attend_back(): pl.pallas_call(functools.partial(attend_back_kernel, shards, hops, rows),...  107 us
    pallas_call x3, Pallas kernels, attend(): pl.pallas_call(functools.partial(attend_kernel, shards, hops, rows), out_...  91.8 us
    pallas_call x3, Pallas kernels, feed_back(): pl.pallas_call(feed_back_kernel, grid=(units // block,), out_shape=[jax.S...  76.1 us
    pallas_call x3, Pallas kernels, feed_forward(): pl.pallas_call(feed_kernel, grid=(units // block,), out_shape=[jax.ShapeD...  71.2 us
    dot_general x6, matrix products, row_product(): jnp.einsum('td,tq->dq', left, right, preferred_element_type=jnp.float32)  44.5 us
    select_n x18, other arithmetic, choose(): jnp.where(first_section, a, b)  26.9 us
  transfers between devices with their start and end apart: 11, of which 2 were waited for; matrix products, arithmetic and copies ran while one was open for 11% of the time, Pallas kernels for 40%

profile of v7, /device:TPU:13, one launch (start us, length us, event | category | flops | bytes accessed | tf_op | source)
XLA Modules:
  0.0 1135.0 jit_solution(2095104709140486439)
XLA Ops:
  0.7 2.8 fusion.87
  3.4 3.2 collective-permute-start
  11.6 230.2 %gather_weights.1 = (bf16[1536,4096]{1,0:T(8,128)(2,1)}, bf16[1536,4096]{1,0:T(8,128)(2,1)}, bf16[4096,1536]{1,0:T(8,128)(2,1)}, bf16[64,1024]{1,0:T(8,128)(2,1)...) custom-call(bf16[384,384]{1,0:T(8,128)(2,1)S(1)} %copy-done.5, bf16[384,4096]{1,0:T(8,128)(2,1)S(1)} %bitcast.117, ...), custom_call_target="tpu_custom_call" | custom-call | tf_op jit(solution)/shard_map/gather_weights/pallas_call | solution.py:206
  241.8 2.2 copy-done
  244.0 3.6 copy-done.6
  247.7 5.1 collective-permute-start.1
  256.2 4.2 fusion.61
  260.4 2.4 slice_bitcast_fusion.3
  265.7 4.4 fusion.63.raw
  270.1 27.6 %attend.3 = (bf16[256,1536]{1,0:T(8,128)(2,1)}, bf16[768,1536]{1,0:T(8,128)(2,1)}, bf16[256,1536]{1,0:T(8,128)(2,1)}, f32[256,128]{1,0:T(8,128)}) custom-call(f32[256,3072]{1,0:T(8,128)} %fusion.63.raw, f32[256,384]{1,0:T(8,128)} %get-tuple-element.241.cosine, f32[256,384]{1,0:T(8,128)} %get-tuple-element.231.sine, s32[256,1]{1,0:T(8,128)} %copy.56.own_segment, ...), custom_call_target="tpu_custom_call" | custom-call | tf_op jit(solution)/shard_map/attend/pallas_call | solution.py:785
  297.7 2.1 collective-permute-start.3
  299.8 23.7 %feed_forward.3 = (f32[256,1536]{1,0:T(8,128)}, bf16[256,1536]{1,0:T(8,128)(2,1)}, bf16[256,4096]{1,0:T(8,128)(2,1)}, bf16[256,4096]{1,0:T(8,128)(2,1)}, bf16[25...) custom-call(f32[256,1536]{1,0:T(8,128)} %select_bitcast_fusion.2.inputs, bf16[256,1536]{1,0:T(8,128)(2,1)} %get-tuple-element.85.attended, ...), custom_call_target="tpu_custom_call" | custom-call | flops 10871635968 | bytes 54263808 | tf_op jit(solution)/shard_map/feed_forward/pallas_call | solution.py:1001
  327.8 10.9 collective-permute-done.2
  341.5 8.2 fusion.90.raw
  349.7 34.9 %attend.4 = (bf16[256,1536]{1,0:T(8,128)(2,1)}, bf16[768,1536]{1,0:T(8,128)(2,1)}, bf16[256,1536]{1,0:T(8,128)(2,1)}, f32[256,128]{1,0:T(8,128)}) custom-call(f32[256,3072]{1,0:T(8,128)} %fusion.90.raw, f32[256,384]{1,0:T(8,128)} %get-tuple-element.234.cosine, f32[256,384]{1,0:T(8,128)} %get-tuple-element.230.sine, s32[256,1]{1,0:T(8,128)} %get-tuple-element.220.own_segment, ...), custom_call_target="tpu_custom_call" | custom-call | tf_op jit(solution)/shard_map/attend/pallas_call | solution.py:785
  384.7 23.7 %feed_forward.4 = (f32[256,1536]{1,0:T(8,128)}, bf16[256,1536]{1,0:T(8,128)(2,1)}, bf16[256,4096]{1,0:T(8,128)(2,1)}, bf16[256,4096]{1,0:T(8,128)(2,1)}, bf16[25...) custom-call(f32[256,1536]{1,0:T(8,128)} %copy-done.9, bf16[256,1536]{1,0:T(8,128)(2,1)} %get-tuple-element.94.attended, ...), custom_call_target="tpu_custom_call" | custom-call | flops 10871635968 | bytes 54263808 | tf_op jit(solution)/shard_map/feed_forward/pallas_call | solution.py:1001
  413.0 25.4 %feed_back.3 = (bf16[256,4096]{1,0:T(8,128)(2,1)}, bf16[256,4096]{1,0:T(8,128)(2,1)}, f32[256,1536]{1,0:T(8,128)}, bf16[256,1536]{1,0:T(8,128)(2,1)}, bf16[256,1536]{1,0:T(8,128)(2,1)}, /*index=5*/f32[1,1536]{1,0:T(1,128)}) custom-call(f32[256,1536]{1,0:T(8,128)} %select_select_fusion.grads, f32[256,1536]{1,0:T(8,128)} %get-tuple-element.101.middle, ...), custom_call_target="tpu_custom_call" | custom-call | flops 10871635968 | bytes 57147392 | tf_op jit(solution)/shard_map/feed_back/pallas_call | solution.py:1097
  438.3 33.5 %attend_back.3 = bf16[256,3072]{1,0:T(8,128)(2,1)} custom-call(bf16[256,1536]{1,0:T(8,128)(2,1)} %get-tuple-element.105.queries, bf16[768,1536]{1,0:T(8,128)(2,1)} %get-tuple-element.106.window, f32[256,128]{1,0:T(8,128)} %get-tuple-element.107.log_total, bf16[256,1536]{1,0:T(8,128)(2,1)} %get-tuple-element.108.grads, f32[256,384]{1,0:T(8,128)} %get-tuple-element.234.cosine, ...), custom_call_target="tpu_custom_call" | custom-call | tf_op jit(solution)/shard_map/attend_back/pallas_call | solution.py:927
  471.8 6.1 multiply_reduce_fusion.3
  480.0 5.9 collective-permute-start.7
  489.9 4.4 fusion.84.raw
  494.3 29.2 %attend.5 = (bf16[256,1536]{1,0:T(8,128)(2,1)}, bf16[768,1536]{1,0:T(8,128)(2,1)}, bf16[256,1536]{1,0:T(8,128)(2,1)}, f32[256,128]{1,0:T(8,128)}) custom-call(f32[256,3072]{1,0:T(8,128)} %fusion.84.raw, f32[256,384]{1,0:T(8,128)} %get-tuple-element.242.cosine, f32[256,384]{1,0:T(8,128)} %get-tuple-element.232.sine, s32[256,1]{1,0:T(8,128)} %copy-done.61, ...), custom_call_target="tpu_custom_call" | custom-call | tf_op jit(solution)/shard_map/attend/pallas_call | solution.py:785
  523.6 23.8 %feed_forward.5 = (f32[256,1536]{1,0:T(8,128)}, bf16[256,1536]{1,0:T(8,128)(2,1)}, bf16[256,4096]{1,0:T(8,128)(2,1)}, bf16[256,4096]{1,0:T(8,128)(2,1)}, bf16[25...) custom-call(f32[256,1536]{1,0:T(8,128)} %copy-done.12, bf16[256,1536]{1,0:T(8,128)(2,1)} %get-tuple-element.98.attended, ...), custom_call_target="tpu_custom_call" | custom-call | flops 10871635968 | bytes 54263808 | tf_op jit(solution)/shard_map/feed_forward/pallas_call | solution.py:1001
  547.4 2.3 broadcast_select_fusion.17.queries
  549.7 3.3 broadcast_select_fusion.4.up
  560.3 2.9 fusion.85
  563.1 25.3 %feed_back.4 = (bf16[256,4096]{1,0:T(8,128)(2,1)}, bf16[256,4096]{1,0:T(8,128)(2,1)}, f32[256,1536]{1,0:T(8,128)}, bf16[256,1536]{1,0:T(8,128)(2,1)}, bf16[256,1536]{1,0:T(8,128)(2,1)}, /*index=5*/f32[1,1536]{1,0:T(1,128)}) custom-call(f32[256,1536]{1,0:T(8,128)} %get-tuple-element.204.grads, f32[256,1536]{1,0:T(8,128)} %broadcast_select_fusion.18.middle, ...), custom_call_target="tpu_custom_call" | custom-call | flops 10871635968 | bytes 57147392 | tf_op jit(solution)/shard_map/feed_back/pallas_call | solution.py:1097
  588.5 33.6 %attend_back.4 = bf16[256,3072]{1,0:T(8,128)(2,1)} custom-call(bf16[256,1536]{1,0:T(8,128)(2,1)} %broadcast_select_fusion.17.queries, bf16[768,1536]{1,0:T(8,128)(2,1)} %broadcast_select_fusion.window, f32[256,128]{1,0:T(8,128)} %broadcast_select_fusion.19.log_total, bf16[256,1536]{1,0:T(8,128)(2,1)} %get-tuple-element.123.grads, ...), custom_call_target="tpu_custom_call" | custom-call | tf_op jit(solution)/shard_map/attend_back/pallas_call | solution.py:927
  622.1 7.8 multiply_reduce_fusion.2
  637.6 3.4 collective-permute-start.6
  644.6 4.7 collective-permute-done.9
  655.8 25.4 %feed_back.5 = (bf16[256,4096]{1,0:T(8,128)(2,1)}, bf16[256,4096]{1,0:T(8,128)(2,1)}, f32[256,1536]{1,0:T(8,128)}, bf16[256,1536]{1,0:T(8,128)(2,1)}, bf16[256,1536]{1,0:T(8,128)(2,1)}, /*index=5*/f32[1,1536]{1,0:T(1,128)}) custom-call(f32[256,1536]{1,0:T(8,128)} %fusion.9.grads, f32[256,1536]{1,0:T(8,128)} %get-tuple-element.101.middle, ...), custom_call_target="tpu_custom_call" | custom-call | flops 10871635968 | bytes 57147392 | tf_op jit(solution)/shard_map/feed_back/pallas_call | solution.py:1097
  681.2 39.8 %attend_back.5 = bf16[256,3072]{1,0:T(8,128)(2,1)} custom-call(bf16[256,1536]{1,0:T(8,128)(2,1)} %get-tuple-element.105.queries, bf16[768,1536]{1,0:T(8,128)(2,1)} %get-tuple-element.106.window, f32[256,128]{1,0:T(8,128)} %get-tuple-element.107.log_total, bf16[256,1536]{1,0:T(8,128)(2,1)} %get-tuple-element.124.grads, f32[256,384]{1,0:T(8,128)} %get-tuple-element.234.cosine, ...), custom_call_target="tpu_custom_call" | custom-call | tf_op jit(solution)/shard_map/attend_back/pallas_call | solution.py:927
  722.9 5.6 multiply_reduce_fusion
  735.1 4.5 collective-permute-start.10
  739.6 7.6 convolution_convert_fusion.2.refs_6_
  750.0 7.6 convolution_convert_fusion.3.refs_2_
  757.6 9.7 convolution_convert_fusion.refs_1_
  767.4 9.8 convolution_convert_fusion.1.refs_0_
  778.8 5.1 convolution_convert_fusion.5.refs_4_
  785.5 4.8 convolution_convert_fusion.4.refs_5_
  790.3 2.8 select_bitcast_fusion.1
  794.7 2.8 broadcast_select_fusion.7
  798.1 314.7 %reduce_terms.1 = (bf16[1024,1536]{1,0:T(8,128)(2,1)}, bf16[384,4096]{1,0:T(8,128)(2,1)}, bf16[384,3072]{1,0:T(8,128)(2,1)}, bf16[16,1024]{1,0:T(8,128)(2,1)}, b...) custom-call(bf16[4096,1536]{1,0:T(8,128)(2,1)} %convolution_convert_, ...), custom_call_target="tpu_custom_call" | custom-call | tf_op jit(solution)/shard_map/reduce_terms/pallas_call | solution.py:508
  1112.8 2.2 convert_element_type.207
  1119.3 3.6 bitcast_convert_fusion
  1122.9 3.5 bitcast_convert_fusion.1
  1129.5 3.5 fusion.8
  (297 shorter events, 79.3 us)
Async XLA Ops:
  0.7 8.2 copy-start.2
  3.4 259.3 %collective-permute-start = (bf16[1,1,256,1536]{3,2,1,0:T(8,128)(2,1)}, bf16[1,1,256,1536]{3,2,1,0:T(8,128)(2,1)}, u32[]{:S(2)}, u32[]{:S(2)}) collective-permute-start(bf16[1,1,256,1536]{3,2,1,0:T(8,128)(2,1)} %get-tuple-element.216), channel_id=1, source_target_pairs={{4,7},{5,6},{6,5},{7,4},{12,15},{13,14},{14,13},{15,12},{20,23},{2... | collective-permute-start | bytes 2359304 | tf_op jit(solution)/shard_map/ppermute | solution.py:1157
  11.6 241.2 %copy-start.82 = (s32[2,1,1024]{2,1,0:T(1,128)S(1)}, s32[2,1,1024]{2,1,0:T(1,128)}, u32[]{:S(2)}) copy-start(s32[2,1,1024]{2,1,0:T(1,128)} %param.20) | copy-start | bytes 24580
  11.6 244.6 %copy-start.86 = (f32[384]{0:T(512)S(1)}, f32[384]{0:T(512)}, u32[]{:S(2)}) copy-start(f32[384]{0:T(512)} %constant.121) | copy-start | bytes 4612
  11.6 244.6 %copy-start.87 = (f32[384]{0:T(512)S(1)}, f32[384]{0:T(512)}, u32[]{:S(2)}) copy-start(f32[384]{0:T(512)} %constant.96.clone) | copy-start | bytes 4612
  247.7 80.1 %collective-permute-start.1 = (bf16[1,1,256,1536]{3,2,1,0:T(8,128)(2,1)}, bf16[1,1,256,1536]{3,2,1,0:T(8,128)(2,1)}, u32[]{:S(2)}, u32[]{:S(2)}) collective-permute-start(bf16[1,1,256,1536]{3,2,1,0:T(8,128)(2,1)} %get-tuple-element.91), channel_id=1, source_target_pairs={{4,7},{5,6},{6,5},{7,4},{12,15},{13,14},{14,13},{15,12},{20,23},{2... | collective-permute-start | bytes 2359304 | tf_op jit(solution)/shard_map/ppermute | solution.py:1157
  252.9 9.9 copy-start.35
  256.2 9.5 copy-start.7
  297.7 28.9 %collective-permute-start.3 = (bf16[256,1536]{1,0:T(8,128)(2,1)S(1)}, bf16[256,1536]{1,0:T(8,128)(2,1)}, u32[]{:S(2)}, u32[]{:S(2)}) collective-permute-start(bf16[256,1536]{1,0:T(8,128)(2,1)S(1)} %get-tuple-element.92), channel_id=1, source_target_pairs={{4,7},{5,6},{6,5},{7,4},{12,15},{13,14},{14,13},{15,12},{20,23},{2... | collective-permute-start | bytes 2359304 | tf_op jit(solution)/shard_map/ppermute | solution.py:1157
  299.8 26.0 %copy-start.62 = (s32[256,1]{1,0:T(8,128)S(1)}, s32[256,1]{1,0:T(8,128)}, u32[]{:S(2)}) copy-start(s32[256,1]{1,0:T(8,128)} %copy.56.own_segment) | copy-start | bytes 3076
  323.5 15.2 %copy-start.28 = (bf16[1,1,256,1536]{3,2,1,0:T(8,128)(2,1)S(1)}, bf16[1,1,256,1536]{3,2,1,0:T(8,128)(2,1)}, u32[]{:S(2)}) copy-start(bf16[1,1,256,1536]{3,2,1,0:T(8,128)(2,1)} %get-tuple-element.91) | copy-start | bytes 2359300
  323.5 15.1 %collective-permute-start.2 = (bf16[256,1536]{1,0:T(8,128)(2,1)}, bf16[256,1536]{1,0:T(8,128)(2,1)}, u32[]{:S(2)}, u32[]{:S(2)}) collective-permute-start(bf16[256,1536]{1,0:T(8,128)(2,1)} %get-tuple-element.90), channel_id=1, source_target_pairs={{0,16},{1,17},{2,18},{3,19},{4,20},{5,21},{6,22},{7,23},{8,24},{9,... | collective-permute-start | bytes 2359304 | tf_op jit(solution)/shard_map/ppermute | solution.py:1141
  325.1 15.2 %copy-start.61 = (s32[256,1]{1,0:T(8,128)}, s32[256,1]{1,0:T(8,128)S(1)}, u32[]{:S(2)}) copy-start(s32[256,1]{1,0:T(8,128)S(1)} %copy.57.own_segment) | copy-start | bytes 3076
  327.8 83.8 %copy-start.30 = (bf16[256,1536]{1,0:T(8,128)(2,1)}, bf16[256,1536]{1,0:T(8,128)(2,1)S(1)}, u32[]{:S(2)}) copy-start(bf16[256,1536]{1,0:T(8,128)(2,1)S(1)} %broadcast_select_fusion.9) | copy-start | bytes 2359300
  341.5 8.2 copy-start.66
  408.4 77.5 %collective-permute-start.5 = (bf16[256,1536]{1,0:T(8,128)(2,1)}, bf16[256,1536]{1,0:T(8,128)(2,1)}, u32[]{:S(2)}, u32[]{:S(2)}) collective-permute-start(bf16[256,1536]{1,0:T(8,128)(2,1)} %get-tuple-element.96), channel_id=1, source_target_pairs={{4,7},{5,6},{6,5},{7,4},{12,15},{13,14},{14,13},{15,12},{20,23},{2... | collective-permute-start | bytes 2359304 | tf_op jit(solution)/shard_map/ppermute | solution.py:1157
  410.3 77.7 %collective-permute-start.4 = (bf16[256,1536]{1,0:T(8,128)(2,1)}, bf16[256,1536]{1,0:T(8,128)(2,1)}, u32[]{:S(2)}, u32[]{:S(2)}) collective-permute-start(bf16[256,1536]{1,0:T(8,128)(2,1)} %get-tuple-element.95), channel_id=1, source_target_pairs={{0,16},{1,17},{2,18},{3,19},{4,20},{5,21},{6,22},{7,23},{8,24},{9,... | collective-permute-start | bytes 2359304 | tf_op jit(solution)/shard_map/ppermute | solution.py:1141
  438.3 33.5 %copy-start.10 = (f32[256,1536]{1,0:T(8,128)S(1)}, f32[256,1536]{1,0:T(8,128)}, u32[]{:S(2)}) copy-start(f32[256,1536]{1,0:T(8,128)} %copy-done.9) | copy-start | bytes 4718596
  471.8 18.0 %slice-start = ((s8[9437184]{0:T(1024)(128)(4,1)}), s8[4194304]{0:T(1024)(128)(4,1)S(1)}, s32[]{:S(2)}) async-start(s8[9437184]{0:T(1024)(128)(4,1)} %bitcast.122), calls=%async_computation | async-start | bytes 8388608
  471.8 18.0 %slice-start.1 = ((s8[9437184]{0:T(1024)(128)(4,1)}), s8[1048576]{0:T(1024)(128)(4,1)S(1)}, s32[]{:S(2)}) async-start(s8[9437184]{0:T(1024)(128)(4,1)} %bitcast.122), calls=%async_computation.1 | async-start | bytes 2097152
  478.0 11.9 %slice-start.2 = ((s8[9437184]{0:T(1024)(128)(4,1)}), s8[4194304]{0:T(1024)(128)(4,1)S(1)}, s32[]{:S(2)}) async-start(s8[9437184]{0:T(1024)(128)(4,1)} %bitcast.122), calls=%async_computation.2 | async-start | bytes 8388608
  480.0 8.0 copy-start.29
  480.0 80.3 %collective-permute-start.7 = (bf16[256,1536]{1,0:T(8,128)(2,1)}, bf16[256,1536]{1,0:T(8,128)(2,1)}, u32[]{:S(2)}, u32[]{:S(2)}) collective-permute-start(bf16[256,1536]{1,0:T(8,128)(2,1)} %get-tuple-element.207), channel_id=1, source_target_pairs={{16,0},{17,1},{18,2},{19,3},{20,4},{21,5},{22,6},{23,7},{24,8},{25... | collective-permute-start | bytes 2359304 | tf_op jit(solution)/shard_map/ppermute | solution.py:1141
  622.1 7.9 copy-start.13
  622.1 7.9 copy-start.21
  622.1 7.9 copy-start.34
  622.1 7.9 copy-start.59
  632.1 17.3 %collective-permute-start.9 = (bf16[256,1536]{1,0:T(8,128)(2,1)S(1)}, bf16[256,1536]{1,0:T(8,128)(2,1)S(1)}, u32[]{:S(2)}, u32[]{:S(2)}) collective-permute-start(bf16[256,1536]{1,0:T(8,128)(2,1)S(1)} %convert_element_type.182), channel_id=1, source_target_pairs={{16,0},{17,1},{18,2},{19,3},{20,4},{21,5},{22,6},{23,7},{24,8},{25... | collective-permute-start | bytes 2359304 | tf_op jit(solution)/shard_map/ppermute | solution.py:1141
  633.7 159.4 %collective-permute-start.8 = (f32[256,1536]{1,0:T(8,128)}, f32[256,1536]{1,0:T(8,128)}, u32[]{:S(2)}, u32[]{:S(2)}) collective-permute-start(f32[256,1536]{1,0:T(8,128)} %get-tuple-element.205), channel_id=1, source_target_pairs={{4,7},{5,6},{6,5},{7,4},{12,15},{13,14},{14,13},{15,12},{20,23},{2... | collective-permute-start | bytes 4718600 | tf_op jit(solution)/shard_map/ppermute | solution.py:1157
  637.6 152.7 %collective-permute-start.6 = (bf16[2,256,1536]{2,1,0:T(8,128)(2,1)}, bf16[2,256,1536]{2,1,0:T(8,128)(2,1)}, u32[]{:S(2)}, u32[]{:S(2)}) collective-permute-start(bf16[2,256,1536]{2,1,0:T(8,128)(2,1)} %pad_maximum_fusion.1), channel_id=1, source_target_pairs={{4,7},{5,6},{6,5},{7,4},{12,15},{13,14},{14,13},{15,12},{20,23},{2... | collective-permute-start | bytes 4718600 | tf_op jit(solution)/shard_map/ppermute | solution.py:1157
  642.9 6.5 copy-start.38
  642.9 6.5 copy-start.39
  735.1 59.6 %collective-permute-start.10 = (f32[256,1536]{1,0:T(8,128)}, f32[256,1536]{1,0:T(8,128)}, u32[]{:S(2)}, u32[]{:S(2)}) collective-permute-start(f32[256,1536]{1,0:T(8,128)} %add_select_fusion), channel_id=1, source_target_pairs={{4,7},{5,6},{6,5},{7,4},{12,15},{13,14},{14,13},{15,12},{20,23},{2... | collective-permute-start | bytes 4718600 | tf_op jit(solution)/shard_map/ppermute | solution.py:1157
  739.6 7.6 copy-start.43
  739.6 7.6 copy-start.44
  739.6 7.6 copy-start.50
  739.6 7.6 copy-start.51
  747.7 9.9 copy-start.52
  750.0 7.6 copy-start.92
  757.6 9.7 copy-start.48
  757.6 9.7 copy-start.69
  757.6 9.7 copy-start.74
  757.6 9.7 copy-start.90
  767.3 9.8 copy-start.83
  767.3 9.8 copy-start.84
  767.3 9.8 copy-start.85
  767.3 9.9 copy-start.15
  767.3 9.9 copy-start.17
  (61 other events, 209.4 us)
